TPU v7x, 32 devices: a whole 2x2x4 slice. The times are simulated.
32 devices in a mesh: dp: 4 (over z), ctx: 8 (over y, x, core).
Axes of the slice: x: 2, y: 2, z: 4, core: 2. Of those that a mesh axis runs over, the one named last changes fastest.
Arguments:
- tokens: bfloat16 [2, 32, 1024, 512], P(None, 'dp', 'ctx'), may hold values from -8 to 8
- prefix: int32 [2, 32], P(None, 'dp'), may hold values from 102 to 512
- w_qkv: bfloat16 [512, 1536], P('dp', 'ctx'), may hold values from -0.25 to 0.25
- w_out: bfloat16 [512, 512], P('dp', 'ctx'), may hold values from -0.75 to 0.75
- w_up: bfloat16 [512, 2048], P('dp', 'ctx'), may hold values from -0.25 to 0.25
- w_down: bfloat16 [2048, 512], P('dp', 'ctx'), may hold values from -0.125 to 0.125
- gain_one: bfloat16 [512], P('ctx'), may hold values from 0.25 to 1.75
- gain_two: bfloat16 [512], P('ctx'), may hold values from 0.25 to 1.75
- cotangent: bfloat16 [2, 32, 1024, 512], P(None, 'dp', 'ctx'), may hold values from -6 to 6
Outputs:
- output: bfloat16 [2, 32, 1024, 512], P(None, 'dp', 'ctx')
- input_grad: bfloat16 [2, 32, 1024, 512], P(None, 'dp', 'ctx')
- grad_qkv: float32 [512, 1536], P('dp', 'ctx')
- grad_out: float32 [512, 512], P('dp', 'ctx')
- grad_up: float32 [512, 2048], P('dp', 'ctx')
- grad_down: float32 [2048, 512], P('dp', 'ctx')
- grad_gain_one: float32 [512], P('ctx')
- grad_gain_two: float32 [512], P('ctx')
Inputs may be any that keep to these rules, and one draw needn't show every extreme that they name: `prefix`: each sequence's number of leading positions that attend both ways.
All inputs are finite; a program needn't handle non-finite values.
Results may differ from a plain program's by a relative error of at most 0.017.
Values may be sent and summed in bfloat16 or wider, within the bound.
A program may use at most 192 MiB of HBM per device.

v0:
```python
import math

import jax
import jax.numpy as jnp
from jax import lax
from jax.sharding import PartitionSpec as P

HEADS = 8


EPSILON = 1e-05


def from_behind(shard, axis, by):
    peers = lax.axis_size(axis)
    pairs = [(i, i + by) for i in range(peers) if 0 <= i + by < peers]
    return lax.ppermute(shard, axis, pairs)


def standardize(values):
    row_mean = jnp.mean(values, axis=-1, keepdims=True)
    centred = values - row_mean
    variance = jnp.mean(centred * centred, axis=-1, keepdims=True)
    inv_std = lax.rsqrt(variance + EPSILON)
    return (centred * inv_std, inv_std)


def norm_back(grad_in, unit_rows, inv_std, gain):
    scaled = grad_in * gain
    row_mean = jnp.mean(scaled, axis=-1, keepdims=True)
    cross_mean = jnp.mean(scaled * unit_rows, axis=-1, keepdims=True)
    return (
        inv_std * (scaled - row_mean - unit_rows * cross_mean),
        jnp.sum(grad_in * unit_rows, axis=0),
    )


def gelu_exact(values):
    return 0.5 * values * (1.0 + lax.erf(values * 0.7071067811865476))


def gelu_slope(values):
    return (
        0.5 * (1.0 + lax.erf(values * 0.7071067811865476))
        + values * jnp.exp(-0.5 * values * values) * 0.3989422804014327
    )


def visible_units(block_ids, prefix_len, span_length, block_count):
    query_pos = jnp.arange(span_length)[:, None]
    unit_positions = jnp.arange(2 * span_length + block_count)[None, :]
    start_pos = block_ids * span_length
    query_abs = start_pos + query_pos
    prev_ok = (unit_positions < span_length) & (block_ids >= 1)
    own_pos = unit_positions - span_length
    own_ok = (
        (unit_positions >= span_length)
        & (unit_positions < 2 * span_length)
        & ((own_pos <= query_pos) | (start_pos + own_pos < prefix_len))
    )
    summary_id = unit_positions - 2 * span_length
    far_ok = (summary_id <= block_ids - 1) | (query_abs < prefix_len) & (
        summary_id >= block_ids + 1
    ) & ((summary_id + 1) * span_length <= prefix_len)
    summary_ok = (unit_positions >= 2 * span_length) & far_ok
    return prev_ok | own_ok | summary_ok


def unit_scores(query_rows, key_units, permitted_mask, span_length):
    head_features = query_rows.shape[-1]
    unscaled_scores = jnp.einsum(
        "sqhd,skhd->shqk", query_rows, key_units, preferred_element_type=jnp.float32
    )
    unit_positions = jnp.arange(key_units.shape[1])
    summary_extra_bias = jnp.where(
        unit_positions >= 2 * span_length, math.log(span_length), 0.0
    ).astype(jnp.float32)
    return jnp.where(
        permitted_mask, unscaled_scores * head_features ** (-0.5) + summary_extra_bias, -1e30
    )


def fetch_weights(w_qkv, w_out, w_up, w_down, gain_one, gain_two):
    columns = (
        lax.all_gather(w_qkv, "ctx", axis=1, tiled=True),
        lax.all_gather(w_out, "ctx", axis=1, tiled=True),
        lax.all_gather(w_up, "ctx", axis=1, tiled=True),
        lax.all_gather(w_down, "ctx", axis=1, tiled=True),
        lax.all_gather(gain_one, "ctx", axis=0, tiled=True),
        lax.all_gather(gain_two, "ctx", axis=0, tiled=True),
    )
    full_rows = (
        lax.all_gather(columns[0], "dp", axis=0, tiled=True),
        lax.all_gather(columns[1], "dp", axis=0, tiled=True),
        lax.all_gather(columns[2], "dp", axis=0, tiled=True),
        lax.all_gather(columns[3], "dp", axis=0, tiled=True),
    )
    return (
        full_rows[0],
        full_rows[1],
        full_rows[2],
        full_rows[3],
        columns[4].astype(jnp.float32),
        columns[5].astype(jnp.float32),
    )


def forward_pass(block_tokens, prefix_len, weights):
    w_qkv, w_out, w_up, w_down, gain_one, gain_two = weights
    seq_count, span_length, model_width = block_tokens.shape
    head_features = model_width // HEADS
    stretch_index = lax.axis_index("ctx")
    block_count = lax.axis_size("ctx")
    tok_rows = block_tokens.reshape(-1, model_width).astype(jnp.float32)
    unit_one, inv_one = standardize(tok_rows)
    normed_one = (unit_one * gain_one).astype(jnp.bfloat16)
    projected = jnp.dot(normed_one, w_qkv, preferred_element_type=jnp.float32).astype(jnp.bfloat16)
    query_rows = projected[:, :model_width].reshape(seq_count, span_length, HEADS, head_features)
    key_rows = projected[:, model_width : 2 * model_width].reshape(
        seq_count, span_length, model_width
    )
    value_rows = projected[:, 2 * model_width :].reshape(seq_count, span_length, model_width)
    key_mean = jnp.mean(key_rows, axis=1, keepdims=True, dtype=jnp.float32).astype(jnp.bfloat16)
    value_mean = jnp.mean(value_rows, axis=1, keepdims=True, dtype=jnp.float32).astype(jnp.bfloat16)
    summaries = (
        lax.all_gather(key_mean, "ctx", axis=1, tiled=True),
        lax.all_gather(value_mean, "ctx", axis=1, tiled=True),
    )
    previous = from_behind((key_rows, value_rows), "ctx", 1)
    key_units = jnp.concatenate([previous[0], key_rows, summaries[0]], axis=1).reshape(
        seq_count, -1, HEADS, head_features
    )
    value_units = jnp.concatenate([previous[1], value_rows, summaries[1]], axis=1).reshape(
        seq_count, -1, HEADS, head_features
    )
    permitted_mask = visible_units(
        stretch_index, prefix_len[:, None, None], span_length, block_count
    )[:, None]
    score_matrix = unit_scores(query_rows, key_units, permitted_mask, span_length)
    highest = jnp.max(score_matrix, axis=-1, keepdims=True)
    log_total = highest + jnp.log(jnp.sum(jnp.exp(score_matrix - highest), axis=-1, keepdims=True))
    prob_low = jnp.exp(score_matrix - log_total).astype(jnp.bfloat16)
    attended = jnp.einsum(
        "shqk,skhd->sqhd", prob_low, value_units, preferred_element_type=jnp.float32
    )
    mixed = attended.astype(jnp.bfloat16).reshape(-1, model_width)
    resid = tok_rows + jnp.dot(mixed, w_out, preferred_element_type=jnp.float32)
    unit_two, inv_two = standardize(resid)
    normed_two = (unit_two * gain_two).astype(jnp.bfloat16)
    upper = jnp.dot(normed_two, w_up, preferred_element_type=jnp.float32)
    hidden = gelu_exact(upper).astype(jnp.bfloat16)
    result = resid + jnp.dot(hidden, w_down, preferred_element_type=jnp.float32)
    saved = (
        unit_one,
        inv_one,
        normed_one,
        query_rows,
        key_units,
        value_units,
        permitted_mask,
        log_total,
        mixed,
        unit_two,
        inv_two,
        normed_two,
        upper,
        hidden,
    )
    return (result.astype(jnp.bfloat16).reshape(block_tokens.shape), saved)


def backward_pass(grad_block, weights, saved, running):
    w_qkv, w_out, w_up, w_down, gain_one, gain_two = weights
    (
        unit_one,
        inv_one,
        normed_one,
        query_rows,
        key_units,
        value_units,
        permitted_mask,
        log_total,
        mixed,
        unit_two,
        inv_two,
        normed_two,
        upper,
        hidden,
    ) = saved
    seq_count, span_length, model_width = grad_block.shape
    score_scale = query_rows.shape[-1] ** (-0.5)
    grad_rows = grad_block.reshape(-1, model_width)
    grad_down = jnp.dot(hidden.T, grad_rows, preferred_element_type=jnp.float32)
    grad_hidden = jnp.dot(grad_rows, w_down.T, preferred_element_type=jnp.float32)
    grad_upper = (grad_hidden * gelu_slope(upper)).astype(jnp.bfloat16)
    grad_up = jnp.dot(normed_two.T, grad_upper, preferred_element_type=jnp.float32)
    grad_norm_two = jnp.dot(grad_upper, w_up.T, preferred_element_type=jnp.float32)
    resid_part, grad_gain_two = norm_back(grad_norm_two, unit_two, inv_two, gain_two)
    grad_resid = grad_rows.astype(jnp.float32) + resid_part
    grad_branch = grad_resid.astype(jnp.bfloat16)
    grad_out = jnp.dot(mixed.T, grad_branch, preferred_element_type=jnp.float32)
    grad_mixed = (
        jnp.dot(grad_branch, w_out.T, preferred_element_type=jnp.float32)
        .astype(jnp.bfloat16)
        .reshape(query_rows.shape)
    )
    score_matrix = unit_scores(query_rows, key_units, permitted_mask, span_length)
    prob_full = jnp.exp(score_matrix - log_total)
    grad_prob = jnp.einsum(
        "sqhd,skhd->shqk", grad_mixed, value_units, preferred_element_type=jnp.float32
    )
    grad_score = (
        prob_full * (grad_prob - jnp.sum(prob_full * grad_prob, axis=-1, keepdims=True))
    ).astype(jnp.bfloat16)
    grad_query = (
        jnp.einsum("shqk,skhd->sqhd", grad_score, key_units, preferred_element_type=jnp.float32)
        * score_scale
    )
    grad_key_units = (
        jnp.einsum("shqk,sqhd->skhd", grad_score, query_rows, preferred_element_type=jnp.float32)
        * score_scale
    ).reshape(seq_count, -1, model_width)
    grad_value_units = jnp.einsum(
        "shqk,sqhd->skhd",
        prob_full.astype(jnp.bfloat16),
        grad_mixed,
        preferred_element_type=jnp.float32,
    ).reshape(seq_count, -1, model_width)
    returned = (
        from_behind(grad_key_units[:, :span_length].astype(jnp.bfloat16), "ctx", -1).astype(
            jnp.float32
        ),
        from_behind(grad_value_units[:, :span_length].astype(jnp.bfloat16), "ctx", -1).astype(
            jnp.float32
        ),
    )
    owned = (
        lax.psum_scatter(
            grad_key_units[:, 2 * span_length :].astype(jnp.bfloat16),
            "ctx",
            scatter_dimension=1,
            tiled=True,
        ).astype(jnp.float32),
        lax.psum_scatter(
            grad_value_units[:, 2 * span_length :].astype(jnp.bfloat16),
            "ctx",
            scatter_dimension=1,
            tiled=True,
        ).astype(jnp.float32),
    )
    grad_keys = (
        grad_key_units[:, span_length : 2 * span_length] + returned[0] + owned[0] / span_length
    )
    grad_values = (
        grad_value_units[:, span_length : 2 * span_length] + returned[1] + owned[1] / span_length
    )
    grad_proj = jnp.concatenate(
        [
            grad_query.reshape(-1, model_width),
            grad_keys.reshape(-1, model_width),
            grad_values.reshape(-1, model_width),
        ],
        axis=1,
    ).astype(jnp.bfloat16)
    grad_qkv = jnp.dot(normed_one.T, grad_proj, preferred_element_type=jnp.float32)
    grad_norm_one = jnp.dot(grad_proj, w_qkv.T, preferred_element_type=jnp.float32)
    input_part, grad_gain_one = norm_back(grad_norm_one, unit_one, inv_one, gain_one)
    input_grad = (grad_resid + input_part).astype(jnp.bfloat16).reshape(grad_block.shape)
    updated = (
        running[0] + grad_qkv,
        running[1] + grad_out,
        running[2] + grad_up,
        running[3] + grad_down,
        running[4] + grad_gain_one,
        running[5] + grad_gain_two,
    )
    return (input_grad, updated)


def shards(tokens, prefix, w_qkv, w_out, w_up, w_down, gain_one, gain_two, cotangent):
    batch_count = tokens.shape[0]
    row_factor = lax.axis_size("dp")
    col_factor = lax.axis_size("ctx")
    running = (
        jnp.zeros((w_qkv.shape[0] * row_factor, w_qkv.shape[1] * col_factor), jnp.float32),
        jnp.zeros((w_out.shape[0] * row_factor, w_out.shape[1] * col_factor), jnp.float32),
        jnp.zeros((w_up.shape[0] * row_factor, w_up.shape[1] * col_factor), jnp.float32),
        jnp.zeros((w_down.shape[0] * row_factor, w_down.shape[1] * col_factor), jnp.float32),
        jnp.zeros((gain_one.shape[0] * col_factor,), jnp.float32),
        jnp.zeros((gain_two.shape[0] * col_factor,), jnp.float32),
    )
    outputs = []
    input_grads = []
    for batch_index in range(batch_count):
        forward_weights = fetch_weights(w_qkv, w_out, w_up, w_down, gain_one, gain_two)
        result, saved = forward_pass(tokens[batch_index], prefix[batch_index], forward_weights)
        backward_weights = fetch_weights(w_qkv, w_out, w_up, w_down, gain_one, gain_two)
        input_grad, running = backward_pass(
            cotangent[batch_index], backward_weights, saved, running
        )
        outputs.append(result)
        input_grads.append(input_grad)
    column_sums = (
        lax.psum_scatter(
            running[0].astype(jnp.bfloat16), "ctx", scatter_dimension=1, tiled=True
        ).astype(jnp.float32),
        lax.psum_scatter(
            running[1].astype(jnp.bfloat16), "ctx", scatter_dimension=1, tiled=True
        ).astype(jnp.float32),
        lax.psum_scatter(
            running[2].astype(jnp.bfloat16), "ctx", scatter_dimension=1, tiled=True
        ).astype(jnp.float32),
        lax.psum_scatter(
            running[3].astype(jnp.bfloat16), "ctx", scatter_dimension=1, tiled=True
        ).astype(jnp.float32),
        lax.psum_scatter(
            running[4].astype(jnp.bfloat16), "ctx", scatter_dimension=0, tiled=True
        ).astype(jnp.float32),
        lax.psum_scatter(
            running[5].astype(jnp.bfloat16), "ctx", scatter_dimension=0, tiled=True
        ).astype(jnp.float32),
    )
    row_sums = (
        lax.psum_scatter(
            column_sums[0].astype(jnp.bfloat16), "dp", scatter_dimension=0, tiled=True
        ).astype(jnp.float32),
        lax.psum_scatter(
            column_sums[1].astype(jnp.bfloat16), "dp", scatter_dimension=0, tiled=True
        ).astype(jnp.float32),
        lax.psum_scatter(
            column_sums[2].astype(jnp.bfloat16), "dp", scatter_dimension=0, tiled=True
        ).astype(jnp.float32),
        lax.psum_scatter(
            column_sums[3].astype(jnp.bfloat16), "dp", scatter_dimension=0, tiled=True
        ).astype(jnp.float32),
    )
    gain_sums = lax.psum((column_sums[4], column_sums[5]), "dp")
    return (
        jnp.stack(outputs),
        jnp.stack(input_grads),
        row_sums[0],
        row_sums[1],
        row_sums[2],
        row_sums[3],
        gain_sums[0],
        gain_sums[1],
    )


def solution(mesh):
    placed = (
        P(None, "dp", "ctx", None),
        P(None, "dp"),
        P("dp", "ctx"),
        P("dp", "ctx"),
        P("dp", "ctx"),
        P("dp", "ctx"),
        P("ctx"),
        P("ctx"),
        P(None, "dp", "ctx", None),
    )
    return jax.shard_map(
        shards,
        mesh=mesh,
        in_specs=placed,
        out_specs=(
            P(None, "dp", "ctx", None),
            P(None, "dp", "ctx", None),
            P("dp", "ctx"),
            P("dp", "ctx"),
            P("dp", "ctx"),
            P("dp", "ctx"),
            P("ctx"),
            P("ctx"),
        ),
        check_vma=False,
    )
```

profile of v0, /device:TPU:0, one launch (start us, length us, event | category | flops | bytes accessed | tf_op | source)
XLA Modules:
  0.0 764.9 jit_solution(8124542610371507982)
XLA Ops:
  7.2 13.0 %all_gather.29 = bf16[128,1536]{0,1:T(8,128)(2,1)} all-gather(bf16[128,192]{0,1:T(8,128)(2,1)} %param.11), channel_id=1, replica_groups=mesh['dp'=4,'ctx'=8] {'ctx'}, dimensions={1}, use_global_device_ids=true | all-gather | bytes 442368 | tf_op jit(solution)/shard_map/all_gather | solution.py:85
  20.3 12.7 %all_gather.36 = bf16[128,2048]{1,0:T(8,128)(2,1)} all-gather(bf16[128,256]{1,0:T(8,128)(2,1)} %param.13), channel_id=1, replica_groups=mesh['dp'=4,'ctx'=8] {'ctx'}, dimensions={1}, use_global_device_ids=true | all-gather | bytes 589824 | tf_op jit(solution)/shard_map/all_gather | solution.py:87
  33.1 10.8 %all_gather.38 = bf16[512,512]{0,1:T(8,128)(2,1)} all-gather(bf16[512,64]{0,1:T(8,128)(2,1)} %param.14), channel_id=1, replica_groups=mesh['dp'=4,'ctx'=8] {'ctx'}, dimensions={1}, use_global_device_ids=true | all-gather | bytes 589824 | tf_op jit(solution)/shard_map/all_gather | solution.py:88
  47.8 13.7 %all-reduce.6 = (bf16[512]{0:T(512)(128)(2,1)S(1)}, bf16[512]{0:T(512)(128)(2,1)S(1)}) all-reduce(bf16[512]{0:T(512)(128)(2,1)S(1)} %dynamic-update-slice, bf16[512]{0:T(512)(128)(2,1)S(1)} %dynamic-update-slice.1), channel_id=1, replica_groups=mesh['dp'=4,'ctx'=8] {'ctx'}, use_global_device_ids=true, to_apply=%add | all-reduce | flops 1024 | bytes 4096
  62.6 8.3 %all_gather.33 = bf16[128,512]{0,1:T(8,128)(2,1)S(1)} all-gather(bf16[128,64]{0,1:T(8,128)(2,1)S(1)} %copy-done.64), channel_id=1, replica_groups=mesh['dp'=4,'ctx'=8] {'ctx'}, dimensions={1}, use_global_device_ids=true | all-gather | bytes 147456 | tf_op jit(solution)/shard_map/all_gather | solution.py:86
  70.9 28.1 %all_gather.34 = bf16[512,512]{0,1:T(8,128)(2,1)S(1)} all-gather(bf16[128,512]{0,1:T(8,128)(2,1)S(1)} %all_gather.33), channel_id=1, replica_groups=mesh['dp'=4,'ctx'=8] {'dp'}, dimensions={0}, use_global_device_ids=true | all-gather | bytes 655360 | tf_op jit(solution)/shard_map/all_gather | solution.py:94
  119.4 15.0 %all-gather.1 = bf16[8,4096]{1,0:T(8,128)(2,1)S(1)} all-gather(bf16[8,512]{1,0:T(8,128)(2,1)S(1)} %multiply_convert_fusion.10), channel_id=3, replica_groups=mesh['dp'=4,'ctx'=8] {'ctx'}, dimensions={1}, use_global_device_ids=true | all-gather | bytes 73728 | tf_op jit(solution)/shard_map/all_gather | solution.py:126
  134.5 9.4 %all-gather = bf16[8,4096]{1,0:T(8,128)(2,1)S(1)} all-gather(bf16[8,512]{1,0:T(8,128)(2,1)S(1)} %multiply_convert_fusion.11), channel_id=2, replica_groups=mesh['dp'=4,'ctx'=8] {'ctx'}, dimensions={1}, use_global_device_ids=true | all-gather | bytes 73728 | tf_op jit(solution)/shard_map/all_gather | solution.py:127
  178.7 12.9 %all-gather.3 = bf16[8,4096]{1,0:T(8,128)(2,1)S(1)} all-gather(bf16[8,512]{1,0:T(8,128)(2,1)S(1)} %multiply_convert_fusion.8), channel_id=5, replica_groups=mesh['dp'=4,'ctx'=8] {'ctx'}, dimensions={1}, use_global_device_ids=true | all-gather | bytes 73728 | tf_op jit(solution)/shard_map/all_gather | solution.py:126
  191.7 9.2 %all-gather.2 = bf16[8,4096]{1,0:T(8,128)(2,1)S(1)} all-gather(bf16[8,512]{1,0:T(8,128)(2,1)S(1)} %multiply_convert_fusion.9), channel_id=4, replica_groups=mesh['dp'=4,'ctx'=8] {'ctx'}, dimensions={1}, use_global_device_ids=true | all-gather | bytes 73728 | tf_op jit(solution)/shard_map/all_gather | solution.py:127
  265.5 8.2 %multiply_convert_fusion.3 = (bf16[1024,2048]{1,0:T(8,128)(2,1)}, f32[1024,2048]{1,0:T(8,128)}) fusion(bf16[512,2048]{1,0:T(8,128)(2,1)} %all-gather.10.cloned.1.call-done, f32[1024,512]{1,0:T(8,128)} %copy-done.5, f32[512]{0:T(512)S(1)} %convert_element_type.279, f32[1024]{0:T(1024)S(1)} %add_rsqrt_fusion.1, f32[1024]{0:T(1024)S(1)} %broadcast_multiply_fusion.11), kind=kOutput, calls=%fused_computation.26 | convolution fusion | flops 2160066560 | bytes 16787456 | tf_op jit(solution)/shard_map/dot_general | solution.py:150
  273.7 7.3 fusion.5
  310.3 10.9 %multiply_reduce_fusion = (f32[8,8,128]{2,1,0:T(8,128)S(1)}, f32[8,8,128,264]{2,3,1,0:T(8,128)}) fusion(f32[8,8,128,264]{2,3,1,0:T(8,128)} %copy-done.1, f32[8,8,128]{2,1,0:T(8,128)S(1)} %log_add_fusion, bf16[8,128,8,64]{1,3,2,0:T(8,128)(2,1)} %copy.117, bf16[8,8,8,64]{1,3,2,0:T(8,128)(2,1)} %copy.95, bf16[8,128,8,64]{1,3,2,0:T(8,128)(2,1)} %copy-done.31, ...), kind=kOutput, calls=%fused_computation.3 | convolution fusion | flops 289792000 | bytes 20578304 | tf_op jit(solution)/shard_map/sqhd,skhd->shqk/dot_general | solution.py:209
  321.1 9.9 %multiply_convert_fusion = bf16[8,8,128,264]{2,3,1,0:T(8,128)(2,1)} fusion(f32[8,8,128,264]{2,3,1,0:T(8,128)} %get-tuple-element.86, f32[8,8,128,264]{2,3,1,0:T(8,128)} %copy-done.1, f32[8,8,128]{2,1,0:T(8,128)S(1)} %get-tuple-element.85, f32[8,8,128]{2,1,0:T(8,128)S(1)} %log_add_fusion), kind=kLoop, calls=%fused_computation.2 | loop fusion | flops 8650752 | bytes 21692416 | tf_op jit(solution)/shard_map/convert_element_type | solution.py:214
  331.1 7.5 broadcast_multiply_fusion
  357.3 10.3 %multiply_reduce_fusion.1 = (f32[8,8,128]{2,1,0:T(8,128)S(1)}, f32[8,8,128,264]{2,3,1,0:T(8,128)}) fusion(f32[8,8,128,264]{2,3,1,0:T(8,128)} %copy-done, f32[8,8,128]{2,1,0:T(8,128)S(1)} %log_add_fusion.1, bf16[8,128,8,64]{1,3,2,0:T(8,128)(2,1)S(1)} %copy.104, bf16[8,8,8,64]{1,3,2,0:T(8,128)(2,1)} %copy.84, bf16[8,128,8,64]{1,3,2,0:T(8,128)(2,1)} %copy.83, ...), kind=kOutput, calls=%fused_computation.5 | convolution fusion | flops 289792000 | bytes 20578304 | tf_op jit(solution)/shard_map/sqhd,skhd->shqk/dot_general | solution.py:209
  367.7 8.6 %fusion.61 = f32[8,8,64,264]{3,2,1,0:T(8,128)} fusion(bf16[8,128,8,64]{1,3,2,0:T(8,128)(2,1)} %copy.117, f32[8,8,128,264]{2,3,1,0:T(8,128)} %copy-done.1, f32[8,8,128]{2,1,0:T(8,128)S(1)} %log_add_fusion), kind=kOutput, calls=%fused_computation.133 | convolution fusion | flops 281149440 | bytes 14057472 | tf_op jit(solution)/shard_map/shqk,sqhd->skhd/dot_general | solution.py:223
  387.0 10.4 %multiply_convert_fusion.1 = bf16[8,8,128,264]{2,3,1,0:T(8,128)(2,1)} fusion(f32[8,8,128,264]{2,3,1,0:T(8,128)} %get-tuple-element.84, f32[8,8,128,264]{2,3,1,0:T(8,128)} %copy-done, f32[8,8,128]{2,1,0:T(8,128)S(1)} %get-tuple-element.83, f32[8,8,128]{2,1,0:T(8,128)S(1)} %log_add_fusion.1), kind=kLoop, calls=%fused_computation.4 | loop fusion | flops 8650752 | bytes 21692416 | tf_op jit(solution)/shard_map/convert_element_type | solution.py:214
  397.4 7.4 broadcast_multiply_fusion.1
  415.6 8.3 %fusion.64 = f32[8,8,64,264]{3,2,1,0:T(8,128)} fusion(bf16[8,128,8,64]{1,3,2,0:T(8,128)(2,1)S(1)} %copy.104, f32[8,8,128,264]{2,3,1,0:T(8,128)} %copy-done, f32[8,8,128]{2,1,0:T(8,128)S(1)} %log_add_fusion.1), kind=kOutput, calls=%fused_computation.134 | convolution fusion | flops 281149440 | bytes 14057472 | tf_op jit(solution)/shard_map/shqk,sqhd->skhd/dot_general | solution.py:223
  435.1 7.0 fusion.110
  443.8 7.2 add_convert_fusion
  474.1 6.9 add_convert_fusion.3
  493.7 12.5 %reduce-scatter.17.cloned.1.call-done = bf16[8,1,512]{2,0,1:T(8,128)(2,1)} async-done(((bf16[8,8,512]{2,0,1:T(8,128)(2,1)}), bf16[8,1,512]{2,0,1:T(8,128)(2,1)}) %reduce-scatter.17.cloned.1.call-update) | async-done | bytes 8208 | tf_op jit(solution)/shard_map/reduce_scatter | solution.py:238
  506.9 35.8 %reduce-scatter.19.cloned.1.call-done = bf16[8,1,512]{2,0,1:T(8,128)(2,1)} async-done(((bf16[8,8,512]{2,0,1:T(8,128)(2,1)}), bf16[8,1,512]{2,0,1:T(8,128)(2,1)}) %reduce-scatter.19.cloned.1.call-update) | async-done | bytes 8208 | tf_op jit(solution)/shard_map/reduce_scatter | solution.py:244
  585.7 21.7 %reduce-scatter.33.cloned.1.call-done = bf16[2048,64]{0,1:T(8,128)(2,1)} async-done(((bf16[2048,512]{0,1:T(8,128)(2,1)}), bf16[2048,64]{0,1:T(8,128)(2,1)}) %reduce-scatter.33.cloned.1.call-update) | async-done | bytes 262160 | tf_op jit(solution)/shard_map/reduce_scatter | solution.py:313
  607.6 44.3 %reduce-scatter.29.cloned.1.call-done = bf16[512,256]{1,0:T(8,128)(2,1)} async-done(((bf16[512,2048]{1,0:T(8,128)(2,1)}), bf16[512,256]{1,0:T(8,128)(2,1)}) %reduce-scatter.29.cloned.1.call-update) | async-done | bytes 262160 | tf_op jit(solution)/shard_map/reduce_scatter | solution.py:310
  657.0 36.5 %reduce-scatter.25.cloned.1.call-done = bf16[512,192]{0,1:T(8,128)(2,1)} async-done(((bf16[512,1536]{0,1:T(8,128)(2,1)}), bf16[512,192]{0,1:T(8,128)(2,1)}) %reduce-scatter.25.cloned.1.call-update) | async-done | bytes 196624 | tf_op jit(solution)/shard_map/reduce_scatter | solution.py:304
  695.3 12.5 %all-reduce.5 = (bf16[512]{0:T(512)(128)(2,1)S(1)}, bf16[512]{0:T(512)(128)(2,1)S(1)}) all-reduce(bf16[512]{0:T(512)(128)(2,1)S(1)} %add_convert_fusion.5, bf16[512]{0:T(512)(128)(2,1)S(1)} %add_convert_fusion.4), channel_id=18, replica_groups=mesh['dp'=4,'ctx'=8] {'ctx'}, use_global_device_ids=true, to_apply=%region_40.41.clone | all-reduce | flops 1024 | bytes 4096
  708.0 12.2 %all-reduce.4 = (f32[64]{0:T(128)}, f32[64]{0:T(128)}) all-reduce(f32[64]{0:T(128)S(1)} %dynamic-slice_convert_fusion.1, f32[64]{0:T(128)S(1)} %dynamic-slice_convert_fusion), channel_id=1, replica_groups=mesh['dp'=4,'ctx'=8] {'dp'}, use_global_device_ids=true, to_apply=%region_41.42 | all-reduce | flops 128 | bytes 1024 | tf_op jit(solution)/shard_map/psum | solution.py:337
  724.4 11.8 %reduce-scatter.31.cloned.1.call-done = bf16[128,256]{1,0:T(8,128)(2,1)} async-done(((bf16[512,256]{1,0:T(8,128)(2,1)}), bf16[128,256]{1,0:T(8,128)(2,1)}) %reduce-scatter.31.cloned.1.call-update) | async-done | bytes 65552 | tf_op jit(solution)/shard_map/reduce_scatter | solution.py:330
  737.6 18.9 %reduce-scatter.37.cloned.1.call-done = bf16[128,192]{1,0:T(8,128)(2,1)} async-done(((bf16[512,192]{1,0:T(8,128)(2,1)}), bf16[128,192]{1,0:T(8,128)(2,1)}) %reduce-scatter.37.cloned.1.call-update) | async-done | bytes 49168
  (362 shorter events, 298.7 us)
Async XLA Ops:
  7.2 36.9 %copy-start.2 = (bf16[2,8,128,512]{3,2,1,0:T(8,128)(2,1)S(1)}, bf16[2,8,128,512]{3,2,1,0:T(8,128)(2,1)}, u32[]{:S(2)}) copy-start(bf16[2,8,128,512]{3,2,1,0:T(8,128)(2,1)} %param.9) | copy-start | bytes 6291460
  7.2 97.1 %all-gather.8.cloned.1.call-start = ((), (), s32[]{:S(2)}) async-start(), calls=%async_computation.12 | async-start | bytes 1966080 | tf_op jit(solution)/shard_map/all_gather | solution.py:93
  20.3 245.2 %all-gather.10.cloned.1.call-start = ((), (), s32[]{:S(2)}) async-start(), calls=%async_computation.13 | async-start | bytes 2621440 | tf_op jit(solution)/shard_map/all_gather | solution.py:95
  33.1 240.6 %all-gather.12.cloned.1.call-start = ((), (), s32[]{:S(2)}) async-start(), calls=%async_computation.14 | async-start | bytes 2621440 | tf_op jit(solution)/shard_map/all_gather | solution.py:96
  43.9 398.2 %reduce-scatter.27.cloned.1.call-start = ((), (), s32[]{:S(2)}) async-start(), calls=%async_computation.20 | async-start | bytes 589824 | tf_op jit(solution)/shard_map/reduce_scatter | solution.py:307
  44.1 17.3 %copy-start.67 = (s32[2,8]{1,0:T(2,128)S(1)}, s32[2,8]{1,0:T(2,128)}, u32[]{:S(2)}) copy-start(s32[2,8]{1,0:T(2,128)} %param.10) | copy-start | bytes 196
  44.5 18.2 %copy-start.64 = (bf16[128,64]{0,1:T(8,128)(2,1)S(1)}, bf16[128,64]{0,1:T(8,128)(2,1)}, u32[]{:S(2)}) copy-start(bf16[128,64]{0,1:T(8,128)(2,1)} %param.12) | copy-start | bytes 49156
  61.4 37.6 %copy-start.34 = (bf16[2,8,128,512]{3,2,1,0:T(8,128)(2,1)S(1)}, bf16[2,8,128,512]{3,2,1,0:T(8,128)(2,1)}, u32[]{:S(2)}) copy-start(bf16[2,8,128,512]{3,2,1,0:T(8,128)(2,1)} %param.17) | copy-start | bytes 6291460
  61.5 39.3 %copy-start.62 = (f32[512]{0:T(512)}, f32[512]{0:T(512)S(1)}, u32[]{:S(2)}) copy-start(f32[512]{0:T(512)S(1)} %convert_element_type.267) | copy-start | bytes 6148
  61.5 39.3 %copy-start.58 = (f32[1024]{0:T(1024)}, f32[1024]{0:T(1024)S(1)}, u32[]{:S(2)}) copy-start(f32[1024]{0:T(1024)S(1)} %get-tuple-element.52) | copy-start | bytes 12292
  61.5 39.3 %copy-start.60 = (f32[1024]{0:T(1024)}, f32[1024]{0:T(1024)S(1)}, u32[]{:S(2)}) copy-start(f32[1024]{0:T(1024)S(1)} %get-tuple-element.89) | copy-start | bytes 12292
  62.5 40.2 %copy-start.54 = (f32[1024]{0:T(1024)}, f32[1024]{0:T(1024)S(1)}, u32[]{:S(2)}) copy-start(f32[1024]{0:T(1024)S(1)} %rsqrt_bitcast_fusion.1) | copy-start | bytes 12292
  62.5 40.1 %copy-start.56 = (f32[1024]{0:T(1024)}, f32[1024]{0:T(1024)S(1)}, u32[]{:S(2)}) copy-start(f32[1024]{0:T(1024)S(1)} %rsqrt_bitcast_fusion) | copy-start | bytes 12292
  114.1 108.4 %collective-permute-start.3 = (bf16[8,128,512]{2,1,0:T(8,128)(2,1)}, bf16[8,128,512]{2,1,0:T(8,128)(2,1)}, u32[]{:S(2)}, u32[]{:S(2)}) collective-permute-start(bf16[8,128,512]{2,1,0:T(8,128)(2,1)} %bitcast.17), channel_id=1, source_target_pairs={{0,1},{1,2},{2,3},{3,4},{4,5},{5,6},{6,7},{8,9},{9,10},{10,11},{11... | collective-permute-start | bytes 3145736 | tf_op jit(solution)/shard_map/ppermute | solution.py:17
  161.3 91.1 %collective-permute-start = (bf16[8,128,512]{2,1,0:T(8,128)(2,1)}, bf16[8,128,512]{2,1,0:T(8,128)(2,1)}, u32[]{:S(2)}, u32[]{:S(2)}) collective-permute-start(bf16[8,128,512]{2,1,0:T(8,128)(2,1)} %bitcast.210), channel_id=1, source_target_pairs={{0,1},{1,2},{2,3},{3,4},{4,5},{5,6},{6,7},{8,9},{9,10},{10,11},{11... | collective-permute-start | bytes 3145736 | tf_op jit(solution)/shard_map/ppermute | solution.py:17
  168.4 73.9 %collective-permute-start.1 = (bf16[8,128,512]{2,1,0:T(8,128)(2,1)}, bf16[8,128,512]{2,1,0:T(8,128)(2,1)}, u32[]{:S(2)}, u32[]{:S(2)}) collective-permute-start(bf16[8,128,512]{2,1,0:T(8,128)(2,1)} %bitcast.212), channel_id=1, source_target_pairs={{0,1},{1,2},{2,3},{3,4},{4,5},{5,6},{6,7},{8,9},{9,10},{10,11},{11... | collective-permute-start | bytes 3145736 | tf_op jit(solution)/shard_map/ppermute | solution.py:17
  214.6 18.2 %collective-permute-start.2 = (bf16[8,128,512]{2,1,0:T(8,128)(2,1)}, bf16[8,128,512]{2,1,0:T(8,128)(2,1)}, u32[]{:S(2)}, u32[]{:S(2)}) collective-permute-start(bf16[8,128,512]{2,1,0:T(8,128)(2,1)} %bitcast.211), channel_id=1, source_target_pairs={{0,1},{1,2},{2,3},{3,4},{4,5},{5,6},{6,7},{8,9},{9,10},{10,11},{11... | collective-permute-start | bytes 3145736 | tf_op jit(solution)/shard_map/ppermute | solution.py:17
  303.3 188.9 %reduce-scatter.21.cloned.1.call-start = ((), (), s32[]{:S(2)}) async-start(), calls=%async_computation.17 | async-start | bytes 73728 | tf_op jit(solution)/shard_map/reduce_scatter | solution.py:238
  367.7 125.3 %reduce-scatter.23.cloned.1.call-start = ((), (), s32[]{:S(2)}) async-start(), calls=%async_computation.18 | async-start | bytes 73728 | tf_op jit(solution)/shard_map/reduce_scatter | solution.py:244
  387.0 119.2 %reduce-scatter.17.cloned.1.call-start = ((), (), s32[]{:S(2)}) async-start(), calls=%async_computation.15 | async-start | bytes 73728 | tf_op jit(solution)/shard_map/reduce_scatter | solution.py:238
  415.5 127.2 %reduce-scatter.19.cloned.1.call-start = ((), (), s32[]{:S(2)}) async-start(), calls=%async_computation.16 | async-start | bytes 73728 | tf_op jit(solution)/shard_map/reduce_scatter | solution.py:244
  435.0 140.8 %reduce-scatter.39.cloned.1.call-start = ((), (), s32[]{:S(2)}) async-start(), calls=%async_computation.26 | async-start | bytes 163840
  443.7 163.7 %reduce-scatter.33.cloned.1.call-start = ((), (), s32[]{:S(2)}) async-start(), calls=%async_computation.23 | async-start | bytes 2359296 | tf_op jit(solution)/shard_map/reduce_scatter | solution.py:313
  451.1 200.8 %reduce-scatter.29.cloned.1.call-start = ((), (), s32[]{:S(2)}) async-start(), calls=%async_computation.21 | async-start | bytes 2359296 | tf_op jit(solution)/shard_map/reduce_scatter | solution.py:310
  458.7 84.7 %collective-permute-start.6 = (bf16[8,128,512]{2,0,1:T(8,128)(2,1)}, bf16[8,128,512]{2,0,1:T(8,128)(2,1)}, u32[]{:S(2)}, u32[]{:S(2)}) collective-permute-start(bf16[8,128,512]{2,0,1:T(8,128)(2,1)} %slice.117), channel_id=1, source_target_pairs={{1,0},{2,1},{3,2},{4,3},{5,4},{6,5},{7,6},{9,8},{10,9},{11,10},{12... | collective-permute-start | bytes 3145736 | tf_op jit(solution)/shard_map/ppermute | solution.py:17
  460.3 87.0 %collective-permute-start.7 = (bf16[8,128,512]{2,0,1:T(8,128)(2,1)}, bf16[8,128,512]{2,0,1:T(8,128)(2,1)}, u32[]{:S(2)}, u32[]{:S(2)}) collective-permute-start(bf16[8,128,512]{2,0,1:T(8,128)(2,1)} %slice.120), channel_id=1, source_target_pairs={{1,0},{2,1},{3,2},{4,3},{5,4},{6,5},{7,6},{9,8},{10,9},{11,10},{12... | collective-permute-start | bytes 3145736 | tf_op jit(solution)/shard_map/ppermute | solution.py:17
  461.7 89.4 %collective-permute-start.4 = (bf16[8,128,512]{2,0,1:T(8,128)(2,1)}, bf16[8,128,512]{2,0,1:T(8,128)(2,1)}, u32[]{:S(2)}, u32[]{:S(2)}) collective-permute-start(bf16[8,128,512]{2,0,1:T(8,128)(2,1)} %slice.111), channel_id=1, source_target_pairs={{1,0},{2,1},{3,2},{4,3},{5,4},{6,5},{7,6},{9,8},{10,9},{11,10},{12... | collective-permute-start | bytes 3145736 | tf_op jit(solution)/shard_map/ppermute | solution.py:17
  473.9 219.6 %reduce-scatter.25.cloned.1.call-start = ((), (), s32[]{:S(2)}) async-start(), calls=%async_computation.19 | async-start | bytes 1769472 | tf_op jit(solution)/shard_map/reduce_scatter | solution.py:304
  490.9 64.1 %collective-permute-start.5 = (bf16[8,128,512]{2,0,1:T(8,128)(2,1)}, bf16[8,128,512]{2,0,1:T(8,128)(2,1)}, u32[]{:S(2)}, u32[]{:S(2)}) collective-permute-start(bf16[8,128,512]{2,0,1:T(8,128)(2,1)} %slice.114), channel_id=1, source_target_pairs={{1,0},{2,1},{3,2},{4,3},{5,4},{6,5},{7,6},{9,8},{10,9},{11,10},{12... | collective-permute-start | bytes 3145736 | tf_op jit(solution)/shard_map/ppermute | solution.py:17
  568.7 154.2 %reduce-scatter.35.cloned.1.call-start = ((), (), s32[]{:S(2)}) async-start(), calls=%async_computation.24 | async-start | bytes 327680 | tf_op jit(solution)/shard_map/reduce_scatter | solution.py:333
  607.5 128.7 %reduce-scatter.31.cloned.1.call-start = ((), (), s32[]{:S(2)}) async-start(), calls=%async_computation.22 | async-start | bytes 327680 | tf_op jit(solution)/shard_map/reduce_scatter | solution.py:330
  651.9 104.6 %reduce-scatter.37.cloned.1.call-start = ((), (), s32[]{:S(2)}) async-start(), calls=%async_computation.25 | async-start | bytes 327680
  (65 other events, 308.5 us)
Sparse Core Ops, SparseCore 0:
  20.4 37.9 all-gather.7
  60.0 52.2 all-gather.9
  113.9 44.4 all-gather.11
  303.5 35.3 reduce-scatter.26
  367.8 34.8 reduce-scatter.20
  406.1 33.5 reduce-scatter.22
  442.7 63.4 reduce-scatter.16
  509.2 33.5 reduce-scatter.18
  545.5 19.4 reduce-scatter.38
  568.2 39.2 reduce-scatter.32
  610.7 41.1 reduce-scatter.28
  655.1 38.3 reduce-scatter.24
  695.7 19.9 reduce-scatter.34
  717.9 18.2 reduce-scatter.30
  738.2 18.2 reduce-scatter.36
where the time goes:
time: 776 us; the launch traced here: 765 us
  waiting for transfers between devices  182 us (23%)
  matrix products  176 us (23%)
  blocking collectives  158 us (20%)
  local copies, waits for them, and re-layouts  145 us (19%)
  other arithmetic  69.3 us (9%)
  starting transfers between devices  18.1 us (2%)
  between operations  16.9 us (2%)
    reduce_scatter x1, waiting for transfers between devices, shards(): lax.psum_scatter(running[2].astype(jnp.bfloat16), 'ctx', scatter_dimensio...  44.3 us
    reduce_scatter x1, waiting for transfers between devices, shards(): lax.psum_scatter(running[0].astype(jnp.bfloat16), 'ctx', scatter_dimensio...  36.5 us
    reduce_scatter x2, waiting for transfers between devices, backward_pass(): lax.psum_scatter(grad_value_units[:, 2 * span_length:].astype(jnp.bfloat1...  35.8 us
    all_gather x1, blocking collectives, fetch_weights(): lax.all_gather(columns[1], 'dp', axis=0, tiled=True)  28.1 us
    all_gather x2, blocking collectives, forward_pass(): lax.all_gather(key_mean, 'ctx', axis=1, tiled=True)  27.8 us
    unnamed x2, blocking collectives  26.2 us
    reduce_scatter x1, waiting for transfers between devices, shards(): lax.psum_scatter(running[3].astype(jnp.bfloat16), 'ctx', scatter_dimensio...  21.7 us
    unnamed x159, local copies, waits for them, and re-layouts  21.3 us
  transfers between devices with their start and end apart: 23, of which 7 were waited for; matrix products, arithmetic and copies ran while one was open for 45% of the time, Pallas kernels for 0%

commit v1 on v0

v1 whole, which is shorter than its diff:
```python
import functools
import math

import jax
import jax.numpy as jnp
from jax import lax
from jax.experimental import pallas as pl
from jax.experimental.pallas import tpu as pltpu
from jax.sharding import PartitionSpec as P

HEADS = 8
EPSILON = 1e-05
MASKED = -1e30
F32 = jnp.float32
BF16 = jnp.bfloat16
TILE_SEQS = 2
FF_CHUNK = 512
VMEM_MOST = 60 * 1024 * 1024


def dot(a, b):
    return jnp.dot(a, b, preferred_element_type=F32)


def dot_t(a, b):
    return lax.dot_general(a, b, (((1,), (1,)), ((), ())), preferred_element_type=F32)


def standardize(values):
    row_mean = jnp.mean(values, axis=-1, keepdims=True)
    centred = values - row_mean
    variance = jnp.mean(centred * centred, axis=-1, keepdims=True)
    inv_std = lax.rsqrt(variance + EPSILON)
    return (centred * inv_std, inv_std)


def norm_back(grad_in, unit_rows, inv_std, gain):
    scaled = grad_in * gain
    row_mean = jnp.mean(scaled, axis=-1, keepdims=True)
    cross_mean = jnp.mean(scaled * unit_rows, axis=-1, keepdims=True)
    return inv_std * (scaled - row_mean - unit_rows * cross_mean)


def fold_rows(values):
    return jnp.sum(values.reshape(-1, 8, values.shape[-1]), axis=0)


def gelu_parts(upper):
    cdf = 0.5 * (1.0 + lax.erf(upper * 0.7071067811865476))
    slope = cdf + upper * jnp.exp(-0.5 * upper * upper) * 0.3989422804014327
    return (upper * cdf, slope)


def pair_halves(rows):
    lanes = lax.broadcasted_iota(jnp.int32, rows.shape, 1)
    half = rows.shape[1] // 2
    zero = jnp.zeros_like(rows)
    return jnp.concatenate(
        [jnp.where(lanes < half, rows, zero), jnp.where(lanes >= half, rows, zero)], axis=0
    )


def head_select(count, width):
    head_of_row = lax.broadcasted_iota(jnp.int32, (HEADS * count, width), 0) // count
    head_of_lane = lax.broadcasted_iota(jnp.int32, (HEADS * count, width), 1) // (width // HEADS)
    return head_of_row == head_of_lane


def per_head(rows, select):
    tiled = jnp.concatenate([rows.astype(F32)] * HEADS, axis=0)
    return jnp.where(select, tiled, 0.0).astype(BF16)


def project_kernel(x_ref, xp_ref, w_ref, gain_ref, q_ref, k_ref, v_ref, kp_ref, vp_ref, n_ref, np_ref, sum_ref):
    width = x_ref.shape[1]
    gain = gain_ref[...]
    normed = (standardize(x_ref[...].astype(F32))[0] * gain).astype(BF16)
    n_ref[...] = normed
    scale = (width // HEADS) ** -0.5
    q_ref[...] = (dot(normed, w_ref[:, :width]).astype(BF16).astype(F32) * scale).astype(BF16)
    for part, out in ((1, k_ref), (2, v_ref)):
        rows = dot(normed, w_ref[:, part * width : (part + 1) * width]).astype(BF16)
        out[...] = rows
        means = jnp.mean(rows.astype(F32).reshape(TILE_SEQS, -1, width), axis=1)
        sum_ref[0, :, (part - 1) * width : part * width] = means.astype(BF16)
    normed_prev = (standardize(xp_ref[...].astype(F32))[0] * gain).astype(BF16)
    np_ref[...] = normed_prev
    kp_ref[...] = dot(normed_prev, w_ref[:, width : 2 * width]).astype(BF16)
    vp_ref[...] = dot(normed_prev, w_ref[:, 2 * width :]).astype(BF16)


def row_spec(rows, width):
    return pl.BlockSpec((rows, width), lambda i: (i, 0))


def whole_spec(shape):
    return pl.BlockSpec(shape, lambda i: (0,) * len(shape))


def params():
    return pltpu.CompilerParams(vmem_limit_bytes=VMEM_MOST)


def project(x, x_prev, w_qkv, gain, span):
    rows, width = x.shape
    tile = TILE_SEQS * span
    low = jax.ShapeDtypeStruct((rows, width), BF16)
    return pl.pallas_call(
        project_kernel,
        grid=(rows // tile,),
        in_specs=[row_spec(tile, width)] * 2 + [whole_spec(w_qkv.shape), whole_spec(gain.shape)],
        out_specs=[row_spec(tile, width)] * 7
        + [pl.BlockSpec((1, TILE_SEQS, 2 * width), lambda i: (i, 0, 0))],
        out_shape=[low] * 7 + [jax.ShapeDtypeStruct((rows // tile, TILE_SEQS, 2 * width), BF16)],
        compiler_params=params(),
        name="project",
    )(x, x_prev, w_qkv, gain)


def attend_kernel(
    span, prefix_ref, block_ref, q_ref, k_ref, v_ref, kp_ref, vp_ref, sums_ref, mixed_ref, prob_ref, psum_ref
):
    width = q_ref.shape[1]
    pair = 2 * width // HEADS
    half = pair // 2
    count = sums_ref.shape[1]
    tile = pl.program_id(0)
    block = block_ref[0]
    select = head_select(count, width)
    unit_pos = lax.broadcasted_iota(jnp.int32, (span, span), 0)
    query_pos = lax.broadcasted_iota(jnp.int32, (span, span), 1)
    sum_id = lax.broadcasted_iota(jnp.int32, (count, span), 0)
    sum_query = lax.broadcasted_iota(jnp.int32, (count, span), 1)
    bias_prev = jnp.where(block >= 1, 0.0, MASKED).astype(F32)
    for s in range(TILE_SEQS):
        prefix = prefix_ref[tile * TILE_SEQS + s]
        start = block * span
        rows = slice(s * span, (s + 1) * span)
        own_ok = (unit_pos <= query_pos) | (start + unit_pos < prefix)
        bias_own = jnp.where(own_ok, 0.0, MASKED)
        sum_ok = (sum_id <= block - 1) | (
            (start + sum_query < prefix) & (sum_id >= block + 1) & ((sum_id + 1) * span <= prefix)
        )
        bias_sum = jnp.where(sum_ok, math.log(span), MASKED)
        queries = q_ref[rows, :]
        keys = jnp.concatenate([kp_ref[rows, :], k_ref[rows, :]], axis=0)
        values_t = jnp.concatenate([vp_ref[rows, :], v_ref[rows, :]], axis=0).T
        sum_keys = per_head(sums_ref[s, :, :width], select)
        sum_values_t = per_head(sums_ref[s, :, width:], select).T
        sum_scores = dot_t(sum_keys, queries)
        mixed_parts = []
        sum_probs = []
        for p in range(HEADS // 2):
            lanes = slice(p * pair, (p + 1) * pair)
            scores = dot_t(keys[:, lanes], pair_halves(queries[:, lanes]))
            probs = []
            for e in range(2):
                h = 2 * p + e
                cols = slice(e * span, (e + 1) * span)
                s_prev = scores[:span, cols]
                s_own = scores[span:, cols] + bias_own
                s_sum = sum_scores[h * count : (h + 1) * count] + bias_sum
                most = jnp.maximum(
                    jnp.maximum(
                        jnp.max(s_prev, axis=0, keepdims=True) + bias_prev,
                        jnp.max(s_own, axis=0, keepdims=True),
                    ),
                    jnp.max(s_sum, axis=0, keepdims=True),
                )
                e_prev = jnp.exp(s_prev + (bias_prev - most))
                e_own = jnp.exp(s_own - most)
                e_sum = jnp.exp(s_sum - most)
                total = (
                    jnp.sum(e_prev, axis=0, keepdims=True)
                    + jnp.sum(e_own, axis=0, keepdims=True)
                    + jnp.sum(e_sum, axis=0, keepdims=True)
                )
                inverse = 1.0 / total
                probs.append(
                    jnp.concatenate([e_prev * inverse, e_own * inverse], axis=0).astype(BF16)
                )
                sum_probs.append(e_sum * inverse)
            both = jnp.concatenate(probs, axis=1)
            prob_ref[s, p] = both
            crossed = dot(values_t[lanes, :], both)
            mixed_parts.append(crossed[:half, :span])
            mixed_parts.append(crossed[half:, span:])
        all_sums = jnp.concatenate(sum_probs, axis=0).astype(BF16)
        psum_ref[s] = all_sums
        mixed_t = jnp.concatenate(mixed_parts, axis=0) + dot(sum_values_t, all_sums)
        mixed_ref[rows, :] = mixed_t.T.astype(BF16)


def attend(prefix, block, q, k, v, kp, vp, sums, span):
    rows, width = q.shape
    tile = TILE_SEQS * span
    seqs, count = sums.shape[0], sums.shape[1]
    pairs = HEADS // 2
    return pl.pallas_call(
        functools.partial(attend_kernel, span),
        grid=(rows // tile,),
        in_specs=[pl.BlockSpec(memory_space=pltpu.SMEM)] * 2
        + [row_spec(tile, width)] * 5
        + [pl.BlockSpec((TILE_SEQS, count, 2 * width), lambda i: (i, 0, 0))],
        out_specs=[
            row_spec(tile, width),
            pl.BlockSpec((TILE_SEQS, pairs, 2 * span, 2 * span), lambda i: (i, 0, 0, 0)),
            pl.BlockSpec((TILE_SEQS, HEADS * count, span), lambda i: (i, 0, 0)),
        ],
        out_shape=[
            jax.ShapeDtypeStruct((rows, width), BF16),
            jax.ShapeDtypeStruct((seqs, pairs, 2 * span, 2 * span), BF16),
            jax.ShapeDtypeStruct((seqs, HEADS * count, span), BF16),
        ],
        compiler_params=params(),
        name="attend",
    )(prefix, block, q, k, v, kp, vp, sums)


def feed_kernel(
    x_ref, mixed_ref, g_ref, wo_ref, wu_ref, wd_ref, gain_ref,
    out_ref, gm_ref, gr_ref, gout_ref, gup_ref, gdown_ref, ggain_ref,
    acc_out, acc_up, acc_down, acc_gain,
):
    step = pl.program_id(0)

    @pl.when(step == 0)
    def _():
        acc_out[...] = jnp.zeros_like(acc_out)
        acc_up[...] = jnp.zeros_like(acc_up)
        acc_down[...] = jnp.zeros_like(acc_down)
        acc_gain[...] = jnp.zeros_like(acc_gain)

    gain = gain_ref[...]
    mixed = mixed_ref[...]
    resid = x_ref[...].astype(F32) + dot(mixed, wo_ref[...])
    unit, inv = standardize(resid)
    normed = (unit * gain).astype(BF16)
    normed_t = normed.T
    grad = g_ref[...]
    grad_t = grad.T
    hidden_width = wu_ref.shape[1]
    result = resid
    grad_norm = None
    for c in range(hidden_width // FF_CHUNK):
        cols = slice(c * FF_CHUNK, (c + 1) * FF_CHUNK)
        upper = dot(normed, wu_ref[:, cols])
        grad_hidden = dot_t(grad, wd_ref[cols, :])
        activated, slope = gelu_parts(upper)
        hidden = activated.astype(BF16)
        grad_upper = (grad_hidden * slope).astype(BF16)
        result = result + dot(hidden, wd_ref[cols, :])
        back = dot_t(grad_upper, wu_ref[:, cols])
        grad_norm = back if grad_norm is None else grad_norm + back
        acc_down[:, cols] += dot(grad_t, hidden)
        acc_up[:, cols] += dot(normed_t, grad_upper)
    out_ref[...] = result.astype(BF16)
    acc_gain[...] += fold_rows(grad_norm * unit)
    grad_resid = grad.astype(F32) + norm_back(grad_norm, unit, inv, gain)
    gr_ref[...] = grad_resid
    grad_branch = grad_resid.astype(BF16)
    acc_out[...] += dot(mixed.T, grad_branch)
    gm_ref[...] = dot_t(grad_branch, wo_ref[...]).astype(BF16)

    @pl.when(step == pl.num_programs(0) - 1)
    def _():
        gout_ref[...] = acc_out[...].astype(BF16)
        gup_ref[...] = acc_up[...].astype(BF16)
        gdown_ref[...] = acc_down[...].astype(BF16)
        ggain_ref[...] = acc_gain[...]


def feed(x, mixed, grad, w_out, w_up, w_down, gain, tile):
    rows, width = x.shape
    hidden = w_up.shape[1]
    wide = (width, hidden)
    square = (width, width)
    return pl.pallas_call(
        feed_kernel,
        grid=(rows // tile,),
        in_specs=[row_spec(tile, width)] * 3
        + [whole_spec(w_out.shape), whole_spec(w_up.shape), whole_spec(w_down.shape), whole_spec(gain.shape)],
        out_specs=[row_spec(tile, width)] * 3
        + [whole_spec(square), whole_spec(wide), whole_spec(wide), whole_spec((8, width))],
        out_shape=[
            jax.ShapeDtypeStruct((rows, width), BF16),
            jax.ShapeDtypeStruct((rows, width), BF16),
            jax.ShapeDtypeStruct((rows, width), F32),
            jax.ShapeDtypeStruct(square, BF16),
            jax.ShapeDtypeStruct(wide, BF16),
            jax.ShapeDtypeStruct(wide, BF16),
            jax.ShapeDtypeStruct((8, width), F32),
        ],
        scratch_shapes=[
            pltpu.VMEM(square, F32),
            pltpu.VMEM(wide, F32),
            pltpu.VMEM(wide, F32),
            pltpu.VMEM((8, width), F32),
        ],
        compiler_params=params(),
        name="feed",
    )(x, mixed, grad, w_out, w_up, w_down, gain)


def return_kernel(
    span, q_ref, k_ref, v_ref, kp_ref, vp_ref, sums_ref, gm_ref, prob_ref, psum_ref, n_ref, np_ref, nsum_ref, w_ref,
    gn_ref, gp_ref, gs_ref, gqkv_ref, acc,
):
    width = q_ref.shape[1]
    pair = 2 * width // HEADS
    half = pair // 2
    count = sums_ref.shape[1]
    scale = half ** -0.5
    step = pl.program_id(0)
    select = head_select(count, width)

    @pl.when(step == 0)
    def _():
        acc[...] = jnp.zeros_like(acc)

    own = []
    before = []
    shared = []
    for s in range(TILE_SEQS):
        rows = slice(s * span, (s + 1) * span)
        queries = q_ref[rows, :]
        grad_mixed = gm_ref[rows, :]
        keys_t = jnp.concatenate([kp_ref[rows, :], k_ref[rows, :]], axis=0).T
        values = jnp.concatenate([vp_ref[rows, :], v_ref[rows, :]], axis=0)
        sum_keys_t = per_head(sums_ref[s, :, :width], select).T
        sum_values = per_head(sums_ref[s, :, width:], select)
        sum_low = psum_ref[s]
        sum_prob = sum_low.astype(F32)
        sum_moved = sum_prob * dot_t(sum_values, grad_mixed)
        grad_q_parts = []
        grad_k_parts = []
        grad_v_parts = []
        sum_grads = []
        for p in range(HEADS // 2):
            lanes = slice(p * pair, (p + 1) * pair)
            grads2 = pair_halves(grad_mixed[:, lanes])
            grad_prob = dot_t(values[:, lanes], grads2)
            low = prob_ref[s, p]
            prob = low.astype(F32)
            moved = prob * grad_prob
            deltas = jnp.sum(moved, axis=0, keepdims=True)
            sums = []
            for e in range(2):
                h = 2 * p + e
                part = slice(h * count, (h + 1) * count)
                delta = deltas[:, e * span : (e + 1) * span] + jnp.sum(
                    sum_moved[part], axis=0, keepdims=True
                )
                sums.append(delta)
                sum_grads.append(sum_moved[part] - sum_prob[part] * delta)
            grad_scores = (moved - prob * jnp.concatenate(sums, axis=1)).astype(BF16)
            grad_k_parts.append(dot(grad_scores, pair_halves(queries[:, lanes])))
            grad_v_parts.append(dot(low, grads2))
            crossed = dot(keys_t[lanes, :], grad_scores)
            grad_q_parts.append(crossed[:half, :span])
            grad_q_parts.append(crossed[half:, span:])
        sum_scores_grad = jnp.concatenate(sum_grads, axis=0).astype(BF16)
        grad_q = jnp.concatenate(grad_q_parts, axis=0) + dot(sum_keys_t, sum_scores_grad)
        grad_q = (grad_q.T * scale).astype(BF16)
        grad_k = jnp.concatenate(grad_k_parts, axis=1).astype(BF16)
        grad_v = jnp.concatenate(grad_v_parts, axis=1).astype(BF16)
        own.append(jnp.concatenate([grad_q, grad_k[span:], grad_v[span:]], axis=1))
        before.append(jnp.concatenate([grad_k[:span], grad_v[:span]], axis=1))
        wide_k = jnp.where(select, dot(sum_scores_grad, queries), 0.0)
        wide_v = jnp.where(select, dot(sum_low, grad_mixed), 0.0)
        folded_k = jnp.sum(wide_k.reshape(HEADS, count, width), axis=0)
        folded_v = jnp.sum(wide_v.reshape(HEADS, count, width), axis=0)
        shared.append(jnp.concatenate([folded_k, folded_v], axis=1) * (1.0 / span))
    grad_own = jnp.concatenate(own, axis=0)
    grad_before = jnp.concatenate(before, axis=0)
    grad_shared = jnp.concatenate(shared, axis=0).astype(BF16)
    gn_ref[...] = dot_t(grad_own, w_ref[...])
    gp_ref[...] = dot_t(grad_before, w_ref[:, width:]).astype(BF16)
    gs_ref[...] = dot_t(grad_shared, w_ref[:, width:]).reshape(gs_ref.shape).astype(BF16)
    normed_t = n_ref[...].T
    normed_prev_t = np_ref[...].T
    normed_sum_t = nsum_ref[...].reshape(-1, width).T
    acc[:, :width] += dot(normed_t, grad_own[:, :width])
    acc[:, width:] += (
        dot(normed_t, grad_own[:, width:]) + dot(normed_prev_t, grad_before) + dot(normed_sum_t, grad_shared)
    )

    @pl.when(step == pl.num_programs(0) - 1)
    def _():
        gqkv_ref[...] = acc[...].astype(BF16)


def give_back(q, k, v, kp, vp, sums, gm, prob, psum, n, n_prev, n_sum, w_qkv, span):
    rows, width = q.shape
    tile = TILE_SEQS * span
    seqs, count = sums.shape[0], sums.shape[1]
    pairs = HEADS // 2
    return pl.pallas_call(
        functools.partial(return_kernel, span),
        grid=(rows // tile,),
        in_specs=[row_spec(tile, width)] * 5
        + [
            pl.BlockSpec((TILE_SEQS, count, 2 * width), lambda i: (i, 0, 0)),
            row_spec(tile, width),
            pl.BlockSpec((TILE_SEQS, pairs, 2 * span, 2 * span), lambda i: (i, 0, 0, 0)),
            pl.BlockSpec((TILE_SEQS, HEADS * count, span), lambda i: (i, 0, 0)),
            row_spec(tile, width),
            row_spec(tile, width),
            pl.BlockSpec((TILE_SEQS, count, width), lambda i: (i, 0, 0)),
            whole_spec(w_qkv.shape),
        ],
        out_specs=[
            row_spec(tile, width),
            row_spec(tile, width),
            pl.BlockSpec((TILE_SEQS, count, width), lambda i: (i, 0, 0)),
            whole_spec(w_qkv.shape),
        ],
        out_shape=[
            jax.ShapeDtypeStruct((rows, width), F32),
            jax.ShapeDtypeStruct((rows, width), BF16),
            jax.ShapeDtypeStruct((seqs, count, width), BF16),
            jax.ShapeDtypeStruct(w_qkv.shape, BF16),
        ],
        scratch_shapes=[pltpu.VMEM(w_qkv.shape, F32)],
        compiler_params=params(),
        name="give_back",
    )(q, k, v, kp, vp, sums, gm, prob, psum, n, n_prev, n_sum, w_qkv)


def close_kernel(span, x_ref, gn_ref, gb_ref, gs_ref, gr_ref, gain_ref, out_ref, ggain_ref, acc):
    step = pl.program_id(0)
    width = x_ref.shape[1]

    @pl.when(step == 0)
    def _():
        acc[...] = jnp.zeros_like(acc)

    unit, inv = standardize(x_ref[...].astype(F32))
    grad_norm = gn_ref[...] + gb_ref[...].astype(F32)
    lifted = [
        grad_norm[s * span : (s + 1) * span] + gs_ref[s].astype(F32) for s in range(TILE_SEQS)
    ]
    grad_norm = jnp.concatenate(lifted, axis=0)
    acc[...] += fold_rows(grad_norm * unit)
    part = norm_back(grad_norm, unit, inv, gain_ref[...])
    out_ref[...] = (gr_ref[...] + part).astype(BF16)

    @pl.when(step == pl.num_programs(0) - 1)
    def _():
        ggain_ref[...] = acc[...]


def close(x, gn, gb, gs, gr, gain, span):
    rows, width = x.shape
    tile = TILE_SEQS * span
    return pl.pallas_call(
        functools.partial(close_kernel, span),
        grid=(rows // tile,),
        in_specs=[row_spec(tile, width)] * 3
        + [pl.BlockSpec((TILE_SEQS, 1, width), lambda i: (i, 0, 0)), row_spec(tile, width), whole_spec(gain.shape)],
        out_specs=[row_spec(tile, width), whole_spec((8, width))],
        out_shape=[jax.ShapeDtypeStruct((rows, width), BF16), jax.ShapeDtypeStruct((8, width), F32)],
        scratch_shapes=[pltpu.VMEM((8, width), F32)],
        compiler_params=params(),
        name="close",
    )(x, gn, gb, gs, gr, gain)


def fetch(shard):
    return lax.all_gather(lax.all_gather(shard, "ctx", axis=1, tiled=True), "dp", axis=0, tiled=True)


def reduce_weight(partial, row_axis):
    columns = lax.psum_scatter(partial, "ctx", scatter_dimension=1 - row_axis, tiled=True)
    return lax.psum_scatter(columns, "dp", scatter_dimension=row_axis, tiled=True).astype(F32)


def shards(tokens, prefix, w_qkv, w_out, w_up, w_down, gain_one, gain_two, cotangent):
    span, width = tokens.shape[2], tokens.shape[3]
    count = lax.axis_size("ctx")
    x = tokens.reshape(-1, width)
    grad = cotangent.reshape(-1, width)
    tile = TILE_SEQS * span
    block = lax.axis_index("ctx").reshape(1).astype(jnp.int32)
    x_prev = lax.ppermute(x, "ctx", [(i, i + 1) for i in range(count - 1)])
    gain1 = lax.all_gather(gain_one, "ctx", axis=0, tiled=True).astype(F32).reshape(1, width)
    gain2 = lax.all_gather(gain_two, "ctx", axis=0, tiled=True).astype(F32).reshape(1, width)
    wq, wo, wu, wd = (fetch(w) for w in (w_qkv, w_out, w_up, w_down))
    q, k, v, kp, vp, n, n_prev, own_sums = project(x, x_prev, wq, gain1, span)
    own_sums = own_sums.reshape(-1, 2 * width)
    n_sum = jnp.sum(n.reshape(-1, span, width).astype(F32), axis=1).astype(BF16)
    everything = lax.all_gather(jnp.concatenate([own_sums, n_sum], axis=1), "ctx", axis=0, tiled=False)
    everything = jnp.transpose(everything, (1, 0, 2))
    sums, n_sums = everything[:, :, : 2 * width], everything[:, :, 2 * width :]
    mixed, prob, psum = attend(prefix.reshape(-1), block, q, k, v, kp, vp, sums, span)
    out, gm, gr, gout, gup, gdown, ggain2 = feed(x, mixed, grad, wo, wu, wd, gain2, tile)
    gn, gp, gs, gqkv = give_back(q, k, v, kp, vp, sums, gm, prob, psum, n, n_prev, n_sums, wq, span)
    gb = lax.ppermute(gp, "ctx", [(i, i - 1) for i in range(1, count)])
    gs_own = lax.psum_scatter(gs, "ctx", scatter_dimension=1, tiled=True)
    input_grad, ggain1 = close(x, gn, gb, gs_own, gr, gain1, span)
    gains = jnp.concatenate([jnp.sum(ggain1, axis=0), jnp.sum(ggain2, axis=0)]).reshape(2, width)
    gains = lax.psum(gains, "dp")
    gains = lax.psum_scatter(gains, "ctx", scatter_dimension=1, tiled=True)
    return (
        out.reshape(tokens.shape),
        input_grad.reshape(tokens.shape),
        reduce_weight(gqkv, 0),
        reduce_weight(gout, 0),
        reduce_weight(gup, 0),
        reduce_weight(gdown, 1).T,
        gains[0],
        gains[1],
    )


def solution(mesh):
    rows = P(None, "dp", "ctx", None)
    both = P("dp", "ctx")
    return jax.shard_map(
        shards,
        mesh=mesh,
        in_specs=(rows, P(None, "dp"), both, both, both, both, P("ctx"), P("ctx"), rows),
        out_specs=(rows, rows, both, both, both, both, P("ctx"), P("ctx")),
        check_vma=False,
    )
```

time: 776 us -> 555 us (0.72); the launches traced: 765 us -> 553 us
  matrix products: 176 us -> 0 us
  Pallas kernels: 0 us -> 133 us
  local copies, waits for them, and re-layouts: 145 us -> 23.7 us
  waiting for transfers between devices: 182 us -> 255 us
  other arithmetic: 69.3 us -> 6.87 us
  blocking collectives: 158 us -> 115 us
  starting transfers between devices: 18.1 us -> 5.64 us
    dot_general x36 -> x0, matrix products: 176 us -> none  [the longest x2 21.2 us: backward_pass(): jnp.einsum('sqhd,skhd->shqk', grad_mixed, value_units, preferred_element_...]
    pallas_call x0 -> x5, Pallas kernels: none -> 133 us  [the longest x1 43.1 us: feed(): pl.pallas_call(feed_kernel, grid=(rows // tile,), in_specs=[row_spec(tile...]
    reshape x16 -> x3, local copies, waits for them, and re-layouts: 57.4 us -> 1.38 us  [the longest x1 0.78 us: shards(): own_sums = own_sums.reshape(-1, 2 * width)]
    unnamed x17 -> x16, waiting for transfers between devices: 19.1 us -> 62.8 us
    all_gather x9 -> x6, blocking collectives: 119 us -> 77.1 us  [the longest x4 45.1 us: fetch(): lax.all_gather(shard, 'ctx', axis=1, tiled=True)]
    concatenate x16 -> x0, local copies, waits for them, and re-layouts: 31 us -> none  [the longest x8 16.3 us: forward_pass(): jnp.concatenate([previous[1], value_rows, summaries[1]], axis=1)]
    convert_element_type x18 -> x1, other arithmetic: 31.7 us -> 1.5 us  [reduce_weight(): lax.psum_scatter(columns, 'dp', scatter_dimension=row_axis, tiled=True)]
    reduce_scatter x10 -> x7, waiting for transfers between devices: 163 us -> 192 us  [the longest x2 86.9 us: reduce_weight(): lax.psum_scatter(partial, 'ctx', scatter_dimension=1 - row_axis, tiled=True)]
  transfers between devices with their start and end apart: 23 -> 15, of which waited for: 7 -> 9; matrix products, arithmetic and copies ran while one was open for 45% -> 4% of each run, Pallas kernels for 0% -> 16%
where the time goes in v1:
time: 555 us; the launch traced here: 553 us
  waiting for transfers between devices  255 us (46%)
  Pallas kernels  133 us (24%)
  blocking collectives  115 us (21%)
  local copies, waits for them, and re-layouts  23.7 us (4%)
  between operations  14.7 us (3%)
  other arithmetic  6.87 us (1%)
  starting transfers between devices  5.64 us (1%)
    reduce_scatter x2, waiting for transfers between devices, reduce_weight(): lax.psum_scatter(partial, 'ctx', scatter_dimension=1 - row_axis, tiled=True)  86.9 us
    reduce_scatter x4, waiting for transfers between devices, reduce_weight(): lax.psum_scatter(columns, 'dp', scatter_dimension=row_axis, tiled=True)  69.4 us
    unnamed x16, waiting for transfers between devices  62.8 us
    all_gather x4, blocking collectives, fetch(): lax.all_gather(shard, 'ctx', axis=1, tiled=True)  45.1 us
    pallas_call x1, Pallas kernels, feed(): pl.pallas_call(feed_kernel, grid=(rows // tile,), in_specs=[row_spec(tile...  43.1 us
    pallas_call x1, Pallas kernels, give_back(): pl.pallas_call(functools.partial(return_kernel, span), grid=(rows // tile...  41.4 us
    reduce_scatter x1, waiting for transfers between devices, shards(): gs_own = lax.psum_scatter(gs, 'ctx', scatter_dimension=1, tiled=True)  35.9 us
    pallas_call x1, Pallas kernels, attend(): pl.pallas_call(functools.partial(attend_kernel, span), grid=(rows // tile...  26.6 us
  transfers between devices with their start and end apart: 15, of which 9 were waited for; matrix products, arithmetic and copies ran while one was open for 4% of the time, Pallas kernels for 16%

profile of v1, /device:TPU:0, one launch (start us, length us, event | category | flops | bytes accessed | tf_op | source)
XLA Modules:
  0.0 553.2 jit_solution(10079045991467041556)
XLA Ops:
  7.2 11.3 %all_gather.36 = bf16[128,1536]{0,1:T(8,128)(2,1)S(1)} all-gather(bf16[128,192]{0,1:T(8,128)(2,1)} %param.11), channel_id=1, replica_groups=mesh['dp'=4,'ctx'=8] {'ctx'}, dimensions={1}, use_global_device_ids=true | all-gather | bytes 442368 | tf_op jit(solution)/shard_map/all_gather | solution.py:470
  19.6 12.7 %all_gather.43 = bf16[128,2048]{1,0:T(8,128)(2,1)} all-gather(bf16[128,256]{1,0:T(8,128)(2,1)} %param.13), channel_id=1, replica_groups=mesh['dp'=4,'ctx'=8] {'ctx'}, dimensions={1}, use_global_device_ids=true | all-gather | bytes 589824 | tf_op jit(solution)/shard_map/all_gather | solution.py:470
  32.3 9.6 %all_gather.45 = bf16[512,512]{0,1:T(8,128)(2,1)S(1)} all-gather(bf16[512,64]{0,1:T(8,128)(2,1)S(1)} %copy-done.2), channel_id=1, replica_groups=mesh['dp'=4,'ctx'=8] {'ctx'}, dimensions={1}, use_global_device_ids=true | all-gather | bytes 589824 | tf_op jit(solution)/shard_map/all_gather | solution.py:470
  43.0 3.6 collective-permute-start
  49.0 26.0 %all-reduce.2 = (bf16[512]{0:T(512)(128)(2,1)S(1)}, bf16[512]{0:T(512)(128)(2,1)S(1)}) all-reduce(bf16[512]{0:T(512)(128)(2,1)S(1)} %dynamic-update-slice, bf16[512]{0:T(512)(128)(2,1)S(1)} %dynamic-update-slice.1), channel_id=1, replica_groups=mesh['dp'=4,'ctx'=8] {'ctx'}, use_global_device_ids=true, to_apply=%add | all-reduce | flops 1024 | bytes 4096
  76.1 11.5 %all_gather.41 = bf16[128,512]{0,1:T(8,128)(2,1)S(1)} all-gather(bf16[128,64]{0,1:T(8,128)(2,1)S(1)} %copy-done.3), channel_id=1, replica_groups=mesh['dp'=4,'ctx'=8] {'ctx'}, dimensions={1}, use_global_device_ids=true | all-gather | bytes 147456 | tf_op jit(solution)/shard_map/all_gather | solution.py:470
  87.7 23.4 %all_gather.42.wo_ref = bf16[512,512]{1,0:T(8,128)(2,1)} all-gather(bf16[128,512]{1,0:T(8,128)(2,1)S(1)} %copy.30), channel_id=1, replica_groups=mesh['dp'=4,'ctx'=8] {'dp'}, dimensions={0}, use_global_device_ids=true | all-gather | bytes 655360 | tf_op jit(solution)/shard_map/all_gather | solution.py:470
  111.2 12.2 %project.1 = (bf16[2048,512]{1,0:T(8,128)(2,1)}, bf16[2048,512]{1,0:T(8,128)(2,1)}, bf16[2048,512]{1,0:T(8,128)(2,1)}, bf16[2048,512]{1,0:T(8,128)(2,1)}, bf16[2...) custom-call(bf16[2048,512]{1,0:T(8,128)(2,1)} %bitcast.26, ...), custom_call_target="tpu_custom_call" | custom-call | tf_op jit(solution)/shard_map/project/pallas_call | solution.py:108
  124.2 1.9 bitcast_reduce_fusion
  126.1 8.5 %all-gather = bf16[128,1536]{1,0:T(8,128)(2,1)S(1)} all-gather(bf16[16,1536]{1,0:T(8,128)(2,1)S(1)} %pad_maximum_fusion), channel_id=2, replica_groups=mesh['dp'=4,'ctx'=8] {'ctx'}, dimensions={0}, use_global_device_ids=true | all-gather | bytes 442368 | tf_op jit(solution)/shard_map/all_gather | solution.py:492
  135.6 26.6 %attend.1 = (bf16[2048,512]{1,0:T(8,128)(2,1)}, bf16[16,4,256,256]{3,2,1,0:T(8,128)(2,1)}, bf16[16,64,128]{2,1,0:T(8,128)(2,1)}) custom-call(s32[16]{0:T(128)} %reshape.54.prefix_ref, s32[1]{0:T(128)} %bitcast.7.block_ref, bf16[2048,512]{1,0:T(8,128)(2,1)} %get-tuple-element.32.q_ref, bf16[2048,512]{1,0:T(8,128)(2,1)} %get-tuple-element.33.k_ref, ...), custom_call_target="tpu_custom_call" | custom-call | tf_op jit(solution)/shard_map/attend/pallas_call | solution.py:199
  162.3 43.1 %feed.1 = (bf16[2048,512]{1,0:T(8,128)(2,1)}, bf16[2048,512]{1,0:T(8,128)(2,1)}, f32[2048,512]{1,0:T(8,128)}, bf16[512,512]{1,0:T(8,128)(2,1)}, bf16[512,2048]{1...) custom-call(bf16[2048,512]{1,0:T(8,128)(2,1)} %bitcast.27, bf16[2048,512]{1,0:T(8,128)(2,1)} %get-tuple-element.39.mixed_ref, ...), custom_call_target="tpu_custom_call" | custom-call | tf_op jit(solution)/shard_map/feed/pallas_call | solution.py:278
  205.4 2.1 copy.38
  208.4 41.4 %give_back.1 = (f32[2048,512]{1,0:T(8,128)}, bf16[2048,512]{1,0:T(8,128)(2,1)}, bf16[16,8,512]{2,1,0:T(8,128)(2,1)}, bf16[512,1536]{1,0:T(8,128)(2,1)}) custom-call(bf16[2048,512]{1,0:T(8,128)(2,1)} %get-tuple-element.32.q_ref, bf16[2048,512]{1,0:T(8,128)(2,1)} %get-tuple-element.33.k_ref, bf16[2048,512]{1,0:T(8,128)(2,1)} %get-tuple-element.34.v_ref, ...), custom_call_target="tpu_custom_call" | custom-call | tf_op jit(solution)/shard_map/give_back/pallas_call | solution.py:398
  249.8 1.6 copy.32
  251.5 2.6 copy.36
  257.0 1.6 copy.39
  258.7 35.9 %reduce-scatter.17.cloned.1.call-done = bf16[16,1,512]{2,0,1:T(8,128)(2,1)} async-done(((bf16[16,8,512]{2,0,1:T(8,128)(2,1)}), bf16[16,1,512]{2,0,1:T(8,128)(2,1)}) %reduce-scatter.17.cloned.1.call-update) | async-done | bytes 16400 | tf_op jit(solution)/shard_map/reduce_scatter | solution.py:499
  297.3 9.2 %close.1 = (bf16[2048,512]{1,0:T(8,128)(2,1)}, f32[8,512]{1,0:T(8,128)}) custom-call(bf16[2048,512]{1,0:T(8,128)(2,1)} %bitcast.28, f32[2048,512]{1,0:T(8,128)} %get-tuple-element.45.gn_ref, bf16[2048,512]{1,0:T(8,128)(2,1)} %copy-done.1, bf16[16,1,512]{2,1,0:T(2,128)(2,1)} %copy.33.gs_ref, f32[2048,512]{1,0:T(8,128)} %get-tuple-element.48.gr_ref, ...), custom_call_target="tpu_custom_call" | custom-call | tf_op jit(solution)/shard_map/close/pallas_call | solution.py:456
  308.2 27.9 %reduce-scatter.31.cloned.1.call-done = bf16[192,512]{1,0:T(8,128)(2,1)} async-done(((bf16[1536,512]{1,0:T(8,128)(2,1)}), bf16[192,512]{1,0:T(8,128)(2,1)}) %reduce-scatter.31.cloned.1.call-update) | async-done | bytes 196624
  336.1 1.8 copy.37
  338.0 42.6 %reduce-scatter.27.cloned.1.call-done = bf16[64,2048]{1,0:T(8,128)(2,1)} async-done(((bf16[512,2048]{1,0:T(8,128)(2,1)}), bf16[64,2048]{1,0:T(8,128)(2,1)}) %reduce-scatter.27.cloned.1.call-update) | async-done | bytes 262160 | tf_op jit(solution)/shard_map/reduce_scatter | solution.py:474
  380.6 44.4 %reduce-scatter.23.cloned.1.call-done = bf16[512,256]{1,0:T(8,128)(2,1)} async-done(((bf16[512,2048]{1,0:T(8,128)(2,1)}), bf16[512,256]{1,0:T(8,128)(2,1)}) %reduce-scatter.23.cloned.1.call-update) | async-done | bytes 262160 | tf_op jit(solution)/shard_map/reduce_scatter | solution.py:474
  425.0 22.3 %reduce-scatter.21.cloned.1.call-done = bf16[128,64]{1,0:T(8,128)(2,1)} async-done(((bf16[512,64]{1,0:T(8,128)(2,1)}), bf16[128,64]{1,0:T(8,128)(2,1)}) %reduce-scatter.21.cloned.1.call-update) | async-done | bytes 16400 | tf_op jit(solution)/shard_map/reduce_scatter | solution.py:475
  448.7 33.3 %reduce-scatter.35.cloned.1.call-done = f32[64,2]{1,0:T(8,128)} async-done(((f32[512,2]{1,0:T(8,128)}), f32[64,2]{1,0:T(8,128)}) %reduce-scatter.35.cloned.1.call-update) | async-done | bytes 528
  482.9 11.7 %psum.8 = f32[2,64]{1,0:T(2,128)S(1)} all-reduce(f32[2,64]{1,0:T(2,128)S(1)} %copy.41), channel_id=1, replica_groups=mesh['dp'=4,'ctx'=8] {'dp'}, use_global_device_ids=true, to_apply=%region_12.0 | all-reduce | flops 128 | bytes 1024 | tf_op jit(solution)/shard_map/psum | solution.py:502
  495.1 9.4 %reduce-scatter.19.cloned.1.call-done = bf16[128,192]{1,0:T(8,128)(2,1)} async-done(((bf16[512,192]{1,0:T(8,128)(2,1)}), bf16[128,192]{1,0:T(8,128)(2,1)}) %reduce-scatter.19.cloned.1.call-update) | async-done | bytes 49168 | tf_op jit(solution)/shard_map/reduce_scatter | solution.py:475
  504.4 1.6 copy.34
  506.0 18.7 %reduce-scatter.29.cloned.1.call-done = bf16[64,512]{1,0:T(8,128)(2,1)} async-done(((bf16[64,2048]{1,0:T(8,128)(2,1)}), bf16[64,512]{1,0:T(8,128)(2,1)}) %reduce-scatter.29.cloned.1.call-update) | async-done | bytes 65552 | tf_op jit(solution)/shard_map/reduce_scatter | solution.py:475
  524.7 1.5 convert_bitcast_fusion
  526.2 19.0 %reduce-scatter.25.cloned.1.call-done = bf16[128,256]{1,0:T(8,128)(2,1)} async-done(((bf16[512,256]{1,0:T(8,128)(2,1)}), bf16[128,256]{1,0:T(8,128)(2,1)}) %reduce-scatter.25.cloned.1.call-update) | async-done | bytes 65552 | tf_op jit(solution)/shard_map/reduce_scatter | solution.py:475
  545.2 1.5 convert_element_type.16
  (76 shorter events, 18.1 us)
Async XLA Ops:
  7.2 25.2 %copy-start.2 = (bf16[512,64]{0,1:T(8,128)(2,1)S(1)}, bf16[512,64]{0,1:T(8,128)(2,1)}, u32[]{:S(2)}) copy-start(bf16[512,64]{0,1:T(8,128)(2,1)} %param.14) | copy-start | bytes 196612
  7.2 104.0 %all-gather.5.cloned.1.call-start = ((), (), s32[]{:S(2)}) async-start(), calls=%async_computation.10 | async-start | bytes 1966080 | tf_op jit(solution)/shard_map/all_gather | solution.py:470
  18.5 24.5 %copy-start = (bf16[2,8,128,512]{3,2,1,0:T(8,128)(2,1)S(1)}, bf16[2,8,128,512]{3,2,1,0:T(8,128)(2,1)}, u32[]{:S(2)}) copy-start(bf16[2,8,128,512]{3,2,1,0:T(8,128)(2,1)} %param.9) | copy-start | bytes 6291460
  18.5 28.1 %copy-start.5 = (s32[2,8]{1,0:T(2,128)S(1)}, s32[2,8]{1,0:T(2,128)}, u32[]{:S(2)}) copy-start(s32[2,8]{1,0:T(2,128)} %param.10) | copy-start | bytes 196
  18.5 28.7 %copy-start.8 = (u32[32]{0:T(128)S(1)}, u32[32]{0:T(128)}, u32[]{:S(2)}) copy-start(u32[32]{0:T(128)} %constant.10) | copy-start | bytes 388
  18.5 29.9 %copy-start.6 = (bf16[64]{0:T(256)(128)(2,1)S(1)}, bf16[64]{0:T(256)(128)(2,1)}, u32[]{:S(2)}) copy-start(bf16[64]{0:T(256)(128)(2,1)} %param.15) | copy-start | bytes 388
  18.5 30.2 %copy-start.7 = (bf16[64]{0:T(256)(128)(2,1)S(1)}, bf16[64]{0:T(256)(128)(2,1)}, u32[]{:S(2)}) copy-start(bf16[64]{0:T(256)(128)(2,1)} %param.16) | copy-start | bytes 388
  18.6 57.5 %copy-start.3 = (bf16[128,64]{0,1:T(8,128)(2,1)S(1)}, bf16[128,64]{0,1:T(8,128)(2,1)}, u32[]{:S(2)}) copy-start(bf16[128,64]{0,1:T(8,128)(2,1)} %param.12) | copy-start | bytes 49156
  19.5 142.7 %all-gather.7.cloned.1.call-start = ((), (), s32[]{:S(2)}) async-start(), calls=%async_computation.11 | async-start | bytes 2621440 | tf_op jit(solution)/shard_map/all_gather | solution.py:470
  32.3 130.0 %all-gather.9.cloned.1.call-start = ((), (), s32[]{:S(2)}) async-start(), calls=%async_computation.12 | async-start | bytes 2621440 | tf_op jit(solution)/shard_map/all_gather | solution.py:470
  43.0 214.0 %reduce-scatter.33.cloned.1.call-start = ((), (), s32[]{:S(2)}) async-start(), calls=%async_computation.21 | async-start | bytes 589824
  43.0 68.1 %collective-permute-start = (bf16[2048,512]{1,0:T(8,128)(2,1)S(1)}, bf16[2048,512]{1,0:T(8,128)(2,1)}, u32[]{:S(2)}, u32[]{:S(2)}) collective-permute-start(bf16[2048,512]{1,0:T(8,128)(2,1)S(1)} %bitcast.29), channel_id=1, source_target_pairs={{0,1},{1,2},{2,3},{3,4},{4,5},{5,6},{6,7},{8,9},{9,10},{10,11},{11... | collective-permute-start | bytes 6291464 | tf_op jit(solution)/shard_map/ppermute | solution.py:485
  207.5 87.2 %reduce-scatter.17.cloned.1.call-start = ((), (), s32[]{:S(2)}) async-start(), calls=%async_computation.13 | async-start | bytes 147456 | tf_op jit(solution)/shard_map/reduce_scatter | solution.py:499
  251.4 84.7 %reduce-scatter.31.cloned.1.call-start = ((), (), s32[]{:S(2)}) async-start(), calls=%async_computation.20 | async-start | bytes 1769472
  254.1 126.4 %reduce-scatter.27.cloned.1.call-start = ((), (), s32[]{:S(2)}) async-start(), calls=%async_computation.18 | async-start | bytes 2359296 | tf_op jit(solution)/shard_map/reduce_scatter | solution.py:474
  254.2 4.5 copy-start.4
  254.9 170.1 %reduce-scatter.23.cloned.1.call-start = ((), (), s32[]{:S(2)}) async-start(), calls=%async_computation.16 | async-start | bytes 2359296 | tf_op jit(solution)/shard_map/reduce_scatter | solution.py:474
  255.6 191.7 %reduce-scatter.21.cloned.1.call-start = ((), (), s32[]{:S(2)}) async-start(), calls=%async_computation.15 | async-start | bytes 163840 | tf_op jit(solution)/shard_map/reduce_scatter | solution.py:475
  255.7 40.3 %collective-permute-start.1 = (bf16[2048,512]{1,0:T(8,128)(2,1)}, bf16[2048,512]{1,0:T(8,128)(2,1)S(1)}, u32[]{:S(2)}, u32[]{:S(2)}) collective-permute-start(bf16[2048,512]{1,0:T(8,128)(2,1)} %get-tuple-element.46), channel_id=1, source_target_pairs={{1,0},{2,1},{3,2},{4,3},{5,4},{6,5},{7,6},{9,8},{10,9},{11,10},{12... | collective-permute-start | bytes 6291464 | tf_op jit(solution)/shard_map/ppermute | solution.py:498
  258.6 223.4 %reduce-scatter.35.cloned.1.call-start = ((), (), s32[]{:S(2)}) async-start(), calls=%async_computation.22 | async-start | bytes 294912
  296.0 1.3 copy-start.1
  308.2 196.3 %reduce-scatter.19.cloned.1.call-start = ((), (), s32[]{:S(2)}) async-start(), calls=%async_computation.14 | async-start | bytes 327680 | tf_op jit(solution)/shard_map/reduce_scatter | solution.py:475
  337.9 186.8 %reduce-scatter.29.cloned.1.call-start = ((), (), s32[]{:S(2)}) async-start(), calls=%async_computation.19 | async-start | bytes 327680 | tf_op jit(solution)/shard_map/reduce_scatter | solution.py:475
  380.6 164.7 %reduce-scatter.25.cloned.1.call-start = ((), (), s32[]{:S(2)}) async-start(), calls=%async_computation.17 | async-start | bytes 327680 | tf_op jit(solution)/shard_map/reduce_scatter | solution.py:475
Sparse Core Ops, SparseCore 0:
  19.6 37.2 all-gather.4
  58.5 52.9 all-gather.6
  113.7 44.4 all-gather.8
  207.6 33.1 reduce-scatter.32
  251.6 43.0 reduce-scatter.16
  297.8 38.3 reduce-scatter.30
  339.4 41.0 reduce-scatter.26
  383.8 41.1 reduce-scatter.22
  427.8 19.4 reduce-scatter.20
  450.1 31.8 reduce-scatter.34
  484.3 20.0 reduce-scatter.18
  506.5 18.1 reduce-scatter.28
  527.0 18.2 reduce-scatter.24

commit v2 on v1

--- a/solution.py
+++ b/solution.py
@@ -17,6 +17,272 @@
 FF_CHUNK = 512
 VMEM_MOST = 60 * 1024 * 1024
 
+MESH = pl.DeviceIdType.MESH
+FLIPS = 8
+
+
+def place():
+    depth, spot = lax.axis_index("dp"), lax.axis_index("ctx")
+    return depth, spot, (spot % 2, (spot // 2) % 2, spot // 4)
+
+
+def flipped(bits, flip):
+    out = 0
+    for i, bit in enumerate(bits):
+        out = out + ((1 - bit) if (flip >> i) & 1 else bit) * (1 << i)
+    return out
+
+
+def spot_of(depths, turn, flip):
+    depth, _, bits = place()
+    return lax.rem(depth + turn, depths), flipped(bits, flip)
+
+
+def greet(depths):
+    barrier = pltpu.get_barrier_semaphore()
+    peers = [(turn, 0) for turn in range(1, depths)] + [(0, 1), (0, 2), (0, 4)]
+    for turn, flip in peers:
+        pl.semaphore_signal(barrier, inc=1, device_id=spot_of(depths, turn, flip), device_id_type=MESH)
+    pl.semaphore_wait(barrier, len(peers))
+
+
+class Gather:
+    def __init__(self, depths, own, full, send, recv):
+        self.depths, self.own, self.full, self.send, self.recv = depths, own, full, send, recv
+        self.sent = []
+
+    def block(self, turn, flip):
+        return self.full.at[spot_of(self.depths, turn, flip)]
+
+    def push(self, turn, flip, to_turn, to_flip):
+        there = ((turn - to_turn) % self.depths) * FLIPS + (flip ^ to_flip)
+        source = self.own if (turn, flip) == (0, 0) else self.block(turn, flip)
+        copy = pltpu.make_async_remote_copy(
+            src_ref=source,
+            dst_ref=self.block(turn, flip),
+            send_sem=self.send.at[len(self.sent)],
+            recv_sem=self.recv.at[there],
+            device_id=spot_of(self.depths, to_turn, to_flip),
+            device_id_type=MESH,
+        )
+        copy.start()
+        self.sent.append(copy)
+
+    def arrive(self, turn, flip):
+        pltpu.make_async_remote_copy(
+            src_ref=self.block(turn, flip),
+            dst_ref=self.block(turn, flip),
+            send_sem=self.send.at[0],
+            recv_sem=self.recv.at[turn * FLIPS + flip],
+            device_id=spot_of(self.depths, 0, 1),
+            device_id_type=MESH,
+        ).wait_recv()
+
+    def begin(self, keep):
+        self.keep = pltpu.make_async_copy(self.own, self.block(0, 0), keep)
+        self.keep.start()
+        for turn in range(1, self.depths):
+            self.push(0, 0, turn, 0)
+        for flip in (2, 4, 1):
+            self.push(0, 0, 0, flip)
+
+    def spread(self):
+        for turn in range(1, self.depths):
+            self.arrive(turn, 0)
+            for flip in (2, 4, 1):
+                self.push(turn, 0, 0, flip)
+
+    def cross(self):
+        for turn in range(self.depths):
+            self.arrive(turn, 2)
+            if turn < self.depths // 2:
+                self.push(turn, 2, 0, 4)
+            self.push(turn, 2, 0, 1)
+            self.arrive(turn, 4)
+            if turn >= self.depths // 2:
+                self.push(turn, 4, 0, 2)
+            self.push(turn, 4, 0, 1)
+
+    def hand_over(self):
+        for turn in range(self.depths):
+            self.arrive(turn, 6)
+            self.push(turn, 6, 0, 1)
+
+    def complete(self):
+        for turn in range(self.depths):
+            for flip in (1, 3, 5, 7):
+                self.arrive(turn, flip)
+        for copy in self.sent:
+            copy.wait_send()
+        self.keep.wait()
+
+
+def gather_kernel(depths, *refs):
+    count = len(refs) // 2 - 1
+    owns, fulls = refs[:count], refs[count : 2 * count]
+    send, recv, keep = refs[2 * count :]
+    greet(depths)
+    moves = [Gather(depths, owns[a], fulls[a], send.at[a], recv.at[a]) for a in range(count)]
+    for a, move in enumerate(moves):
+        move.begin(keep.at[a])
+    for move in moves:
+        move.spread()
+    for move in moves:
+        move.cross()
+    for move in moves:
+        move.hand_over()
+    for move in moves:
+        move.complete()
+
+
+def gather_blocks(blocks, depths):
+    total = depths * FLIPS
+    return pl.pallas_call(
+        functools.partial(gather_kernel, depths),
+        in_specs=[pl.BlockSpec(memory_space=pltpu.VMEM)] * len(blocks),
+        out_specs=[pl.BlockSpec(memory_space=pl.ANY)] * len(blocks),
+        out_shape=[jax.ShapeDtypeStruct((depths, FLIPS) + b.shape, b.dtype) for b in blocks],
+        scratch_shapes=[
+            pltpu.SemaphoreType.DMA((len(blocks), total)),
+            pltpu.SemaphoreType.DMA((len(blocks), total)),
+            pltpu.SemaphoreType.DMA((len(blocks),)),
+        ],
+        compiler_params=pltpu.CompilerParams(collective_id=0, has_side_effects=True, vmem_limit_bytes=VMEM_MOST),
+        name="gather",
+    )(*blocks)
+
+
+class Scatter:
+    def __init__(self, depths, part, mate, total, near, far, send, recv):
+        self.depths, self.part, self.mate, self.total = depths, part, mate, total
+        self.near, self.far, self.send, self.recv = near, far, send, recv
+        self.sent = []
+
+    def block(self, turn, flip):
+        return self.part.at[spot_of(self.depths, turn, flip)]
+
+    def push(self, source, target, slot, to_turn, to_flip):
+        copy = pltpu.make_async_remote_copy(
+            src_ref=source,
+            dst_ref=target,
+            send_sem=self.send.at[len(self.sent)],
+            recv_sem=self.recv.at[slot],
+            device_id=spot_of(self.depths, to_turn, to_flip),
+            device_id_type=MESH,
+        )
+        copy.start()
+        self.sent.append(copy)
+
+    def arrive(self, target, slot):
+        pltpu.make_async_remote_copy(
+            src_ref=target,
+            dst_ref=target,
+            send_sem=self.send.at[0],
+            recv_sem=self.recv.at[slot],
+            device_id=spot_of(self.depths, 0, 1),
+            device_id_type=MESH,
+        ).wait_recv()
+
+    def begin(self):
+        for flip in (6, 2, 4, 0):
+            for turn in range(self.depths):
+                at = (flip // 2, turn)
+                self.push(self.block(turn, flip ^ 1), self.mate.at[at], flip // 2 * self.depths + turn, 0, 1)
+
+    def fold(self, turn, flip):
+        self.arrive(self.mate.at[flip // 2, turn], flip // 2 * self.depths + turn)
+        mine = self.block(turn, flip)[...].astype(F32)
+        self.total[flip // 2, turn] = (mine + self.mate[flip // 2, turn].astype(F32)).astype(BF16)
+
+    def cross(self):
+        base = 4 * self.depths
+        for turn in range(self.depths):
+            self.fold(turn, 6)
+            by = 2 if turn < self.depths // 2 else 4
+            self.push(self.total.at[3, turn], self.near.at[turn], base + turn, 0, by)
+
+    def spread(self):
+        base = 4 * self.depths
+        late = 5 * self.depths
+        for turn in range(self.depths):
+            self.fold(turn, 2)
+            self.fold(turn, 4)
+            via = 2 if turn < self.depths // 2 else 1
+            self.arrive(self.near.at[turn], base + turn)
+            self.total[via, turn] = (self.total[via, turn].astype(F32) + self.near[turn].astype(F32)).astype(BF16)
+            self.push(self.total.at[1, turn], self.far.at[0, turn], late + turn, 0, 2)
+            self.push(self.total.at[2, turn], self.far.at[1, turn], late + self.depths + turn, 0, 4)
+
+    def climb(self):
+        late = 5 * self.depths
+        last = 7 * self.depths
+        for turn in [*range(1, self.depths), 0]:
+            self.fold(turn, 0)
+            self.arrive(self.far.at[0, turn], late + turn)
+            self.arrive(self.far.at[1, turn], late + self.depths + turn)
+            self.total[0, turn] = (
+                self.total[0, turn].astype(F32) + self.far[0, turn].astype(F32) + self.far[1, turn].astype(F32)
+            ).astype(BF16)
+            if turn:
+                back = self.depths - turn
+                self.push(self.total.at[0, turn], self.far.at[2, back], last + back, turn, 0)
+
+    def finish(self):
+        last = 7 * self.depths
+        out = self.total[0, 0].astype(F32)
+        for turn in range(1, self.depths):
+            self.arrive(self.far.at[2, turn], last + turn)
+            out = out + self.far[2, turn].astype(F32)
+        for copy in self.sent:
+            copy.wait_send()
+        return out
+
+
+def scatter_scratch(block, depths):
+    return [
+        pltpu.VMEM((4, depths) + block, BF16),
+        pltpu.VMEM((4, depths) + block, BF16),
+        pltpu.VMEM((depths,) + block, BF16),
+        pltpu.VMEM((3, depths) + block, BF16),
+    ]
+
+
+def scatter_kernel(depths, count, *refs):
+    parts, outs = refs[:count], refs[count : 2 * count]
+    send, recv = refs[-2:]
+    greet(depths)
+    moves = []
+    for a in range(count):
+        mate, total, near, far = refs[2 * count + 4 * a : 2 * count + 4 * a + 4]
+        moves.append(Scatter(depths, parts[a], mate, total, near, far, send.at[a], recv.at[a]))
+    for move in moves:
+        move.begin()
+    for move in moves:
+        move.cross()
+    for move in moves:
+        move.spread()
+    for move in moves:
+        move.climb()
+    for a, move in enumerate(moves):
+        outs[a][...] = move.finish()
+
+
+def scatter_blocks(parts, depths):
+    count = len(parts)
+    scratch = []
+    for part in parts:
+        scratch += scatter_scratch(part.shape[2:], depths)
+    return pl.pallas_call(
+        functools.partial(scatter_kernel, depths, count),
+        in_specs=[pl.BlockSpec(memory_space=pltpu.VMEM)] * count,
+        out_specs=[pl.BlockSpec(memory_space=pltpu.VMEM)] * count,
+        out_shape=[jax.ShapeDtypeStruct(p.shape[2:], F32) for p in parts],
+        scratch_shapes=scratch
+        + [pltpu.SemaphoreType.DMA((count, 8 * depths)), pltpu.SemaphoreType.DMA((count, 8 * depths))],
+        compiler_params=pltpu.CompilerParams(collective_id=1, has_side_effects=True, vmem_limit_bytes=VMEM_MOST),
+        name="scatter",
+    )(*parts)
+
 
 def dot(a, b):
     return jnp.dot(a, b, preferred_element_type=F32)
@@ -71,22 +337,47 @@
     return jnp.where(select, tiled, 0.0).astype(BF16)
 
 
+def rows_of(ref):
+    depths, lanes = ref.shape[0], ref.shape[3]
+    return jnp.concatenate([ref[d].reshape(-1, lanes) for d in range(depths)], axis=1)
+
+
+def lanes_of(ref, chunk, along):
+    lanes = ref.shape[3]
+    take = (lambda i: ref[i]) if along == 0 else (lambda i: ref[:, i])
+    if lanes >= FF_CHUNK:
+        per = lanes // FF_CHUNK
+        cut = slice(chunk % per * FF_CHUNK, (chunk % per + 1) * FF_CHUNK)
+        return take(chunk // per).reshape(-1, lanes)[:, cut]
+    per = FF_CHUNK // lanes
+    return jnp.concatenate([take(i).reshape(-1, lanes) for i in range(chunk * per, (chunk + 1) * per)], axis=1)
+
+
+def put_blocks(ref, values, rows_along):
+    depths, spots, rows, lanes = ref.shape
+    for d in range(depths):
+        for c in range(spots):
+            r, l = (c, d) if rows_along == 1 else (d, c)
+            ref[d, c] = values[r * rows : (r + 1) * rows, l * lanes : (l + 1) * lanes].astype(ref.dtype)
+
+
 def project_kernel(x_ref, xp_ref, w_ref, gain_ref, q_ref, k_ref, v_ref, kp_ref, vp_ref, n_ref, np_ref, sum_ref):
     width = x_ref.shape[1]
     gain = gain_ref[...]
+    weight = rows_of(w_ref)
     normed = (standardize(x_ref[...].astype(F32))[0] * gain).astype(BF16)
     n_ref[...] = normed
     scale = (width // HEADS) ** -0.5
-    q_ref[...] = (dot(normed, w_ref[:, :width]).astype(BF16).astype(F32) * scale).astype(BF16)
+    q_ref[...] = (dot_t(normed, weight[:width]).astype(BF16).astype(F32) * scale).astype(BF16)
     for part, out in ((1, k_ref), (2, v_ref)):
-        rows = dot(normed, w_ref[:, part * width : (part + 1) * width]).astype(BF16)
+        rows = dot_t(normed, weight[part * width : (part + 1) * width]).astype(BF16)
         out[...] = rows
         means = jnp.mean(rows.astype(F32).reshape(TILE_SEQS, -1, width), axis=1)
         sum_ref[0, :, (part - 1) * width : part * width] = means.astype(BF16)
     normed_prev = (standardize(xp_ref[...].astype(F32))[0] * gain).astype(BF16)
     np_ref[...] = normed_prev
-    kp_ref[...] = dot(normed_prev, w_ref[:, width : 2 * width]).astype(BF16)
-    vp_ref[...] = dot(normed_prev, w_ref[:, 2 * width :]).astype(BF16)
+    kp_ref[...] = dot_t(normed_prev, weight[width : 2 * width]).astype(BF16)
+    vp_ref[...] = dot_t(normed_prev, weight[2 * width :]).astype(BF16)
 
 
 def row_spec(rows, width):
@@ -233,24 +524,27 @@
 
     gain = gain_ref[...]
     mixed = mixed_ref[...]
-    resid = x_ref[...].astype(F32) + dot(mixed, wo_ref[...])
+    w_out = rows_of(wo_ref)
+    resid = x_ref[...].astype(F32) + dot_t(mixed, w_out)
     unit, inv = standardize(resid)
     normed = (unit * gain).astype(BF16)
     normed_t = normed.T
     grad = g_ref[...]
     grad_t = grad.T
-    hidden_width = wu_ref.shape[1]
+    hidden_width = acc_up.shape[1]
     result = resid
     grad_norm = None
     for c in range(hidden_width // FF_CHUNK):
         cols = slice(c * FF_CHUNK, (c + 1) * FF_CHUNK)
-        upper = dot(normed, wu_ref[:, cols])
-        grad_hidden = dot_t(grad, wd_ref[cols, :])
+        w_up = lanes_of(wu_ref, c, 1)
+        w_down = lanes_of(wd_ref, c, 0)
+        upper = dot(normed, w_up)
+        grad_hidden = dot(grad, w_down)
         activated, slope = gelu_parts(upper)
         hidden = activated.astype(BF16)
         grad_upper = (grad_hidden * slope).astype(BF16)
-        result = result + dot(hidden, wd_ref[cols, :])
-        back = dot_t(grad_upper, wu_ref[:, cols])
+        result = result + dot_t(hidden, w_down)
+        back = dot_t(grad_upper, w_up)
         grad_norm = back if grad_norm is None else grad_norm + back
         acc_down[:, cols] += dot(grad_t, hidden)
         acc_up[:, cols] += dot(normed_t, grad_upper)
@@ -259,20 +553,20 @@
     grad_resid = grad.astype(F32) + norm_back(grad_norm, unit, inv, gain)
     gr_ref[...] = grad_resid
     grad_branch = grad_resid.astype(BF16)
-    acc_out[...] += dot(mixed.T, grad_branch)
-    gm_ref[...] = dot_t(grad_branch, wo_ref[...]).astype(BF16)
+    acc_out[...] += dot(grad_branch.T, mixed)
+    gm_ref[...] = dot(grad_branch, w_out).astype(BF16)
 
     @pl.when(step == pl.num_programs(0) - 1)
     def _():
-        gout_ref[...] = acc_out[...].astype(BF16)
-        gup_ref[...] = acc_up[...].astype(BF16)
-        gdown_ref[...] = acc_down[...].astype(BF16)
+        put_blocks(gout_ref, acc_out, 1)
+        put_blocks(gup_ref, acc_up, 0)
+        put_blocks(gdown_ref, acc_down, 1)
         ggain_ref[...] = acc_gain[...]
 
 
 def feed(x, mixed, grad, w_out, w_up, w_down, gain, tile):
     rows, width = x.shape
-    hidden = w_up.shape[1]
+    hidden = w_up.shape[1] * w_up.shape[3]
     wide = (width, hidden)
     square = (width, width)
     return pl.pallas_call(
@@ -281,14 +575,14 @@
         in_specs=[row_spec(tile, width)] * 3
         + [whole_spec(w_out.shape), whole_spec(w_up.shape), whole_spec(w_down.shape), whole_spec(gain.shape)],
         out_specs=[row_spec(tile, width)] * 3
-        + [whole_spec(square), whole_spec(wide), whole_spec(wide), whole_spec((8, width))],
+        + [whole_spec(w_out.shape), whole_spec(w_up.shape), whole_spec(w_down.shape), whole_spec((8, width))],
         out_shape=[
             jax.ShapeDtypeStruct((rows, width), BF16),
             jax.ShapeDtypeStruct((rows, width), BF16),
             jax.ShapeDtypeStruct((rows, width), F32),
-            jax.ShapeDtypeStruct(square, BF16),
-            jax.ShapeDtypeStruct(wide, BF16),
-            jax.ShapeDtypeStruct(wide, BF16),
+            jax.ShapeDtypeStruct(w_out.shape, BF16),
+            jax.ShapeDtypeStruct(w_up.shape, BF16),
+            jax.ShapeDtypeStruct(w_down.shape, BF16),
             jax.ShapeDtypeStruct((8, width), F32),
         ],
         scratch_shapes=[
@@ -374,9 +668,10 @@
     grad_own = jnp.concatenate(own, axis=0)
     grad_before = jnp.concatenate(before, axis=0)
     grad_shared = jnp.concatenate(shared, axis=0).astype(BF16)
-    gn_ref[...] = dot_t(grad_own, w_ref[...])
-    gp_ref[...] = dot_t(grad_before, w_ref[:, width:]).astype(BF16)
-    gs_ref[...] = dot_t(grad_shared, w_ref[:, width:]).reshape(gs_ref.shape).astype(BF16)
+    weight = rows_of(w_ref)
+    gn_ref[...] = dot(grad_own, weight)
+    gp_ref[...] = dot(grad_before, weight[width:]).astype(BF16)
+    gs_ref[...] = dot(grad_shared, weight[width:]).reshape(gs_ref.shape).astype(BF16)
     normed_t = n_ref[...].T
     normed_prev_t = np_ref[...].T
     normed_sum_t = nsum_ref[...].reshape(-1, width).T
@@ -387,7 +682,7 @@
 
     @pl.when(step == pl.num_programs(0) - 1)
     def _():
-        gqkv_ref[...] = acc[...].astype(BF16)
+        put_blocks(gqkv_ref, acc[...].astype(BF16).T, 1)
 
 
 def give_back(q, k, v, kp, vp, sums, gm, prob, psum, n, n_prev, n_sum, w_qkv, span):
@@ -421,7 +716,7 @@
             jax.ShapeDtypeStruct((seqs, count, width), BF16),
             jax.ShapeDtypeStruct(w_qkv.shape, BF16),
         ],
-        scratch_shapes=[pltpu.VMEM(w_qkv.shape, F32)],
+        scratch_shapes=[pltpu.VMEM((width, 3 * width), F32)],
         compiler_params=params(),
         name="give_back",
     )(q, k, v, kp, vp, sums, gm, prob, psum, n, n_prev, n_sum, w_qkv)
@@ -466,13 +761,16 @@
     )(x, gn, gb, gs, gr, gain)
 
 
-def fetch(shard):
-    return lax.all_gather(lax.all_gather(shard, "ctx", axis=1, tiled=True), "dp", axis=0, tiled=True)
-
-
-def reduce_weight(partial, row_axis):
-    columns = lax.psum_scatter(partial, "ctx", scatter_dimension=1 - row_axis, tiled=True)
-    return lax.psum_scatter(columns, "dp", scatter_dimension=row_axis, tiled=True).astype(F32)
+def fetch(block, rows_along):
+    spot, depth = (0, 1) if rows_along == 1 else (1, 0)
+    whole = lax.all_gather(lax.all_gather(block, "ctx", axis=spot, tiled=True), "dp", axis=depth, tiled=True)
+    return whole[None, None]
+
+
+def reduce_weight(partial, rows_along):
+    spot, depth = (0, 1) if rows_along == 1 else (1, 0)
+    columns = lax.psum_scatter(partial[0, 0], "ctx", scatter_dimension=spot, tiled=True)
+    return lax.psum_scatter(columns, "dp", scatter_dimension=depth, tiled=True).astype(F32)
 
 
 def shards(tokens, prefix, w_qkv, w_out, w_up, w_down, gain_one, gain_two, cotangent):
@@ -485,7 +783,14 @@
     x_prev = lax.ppermute(x, "ctx", [(i, i + 1) for i in range(count - 1)])
     gain1 = lax.all_gather(gain_one, "ctx", axis=0, tiled=True).astype(F32).reshape(1, width)
     gain2 = lax.all_gather(gain_two, "ctx", axis=0, tiled=True).astype(F32).reshape(1, width)
-    wq, wo, wu, wd = (fetch(w) for w in (w_qkv, w_out, w_up, w_down))
+    depths = lax.axis_size("dp")
+    blocks = (w_qkv.T, w_out.T, w_up, w_down.T)
+    along = (1, 1, 0, 1)
+    direct = count == FLIPS and all(b.shape[0] % 16 == 0 and b.shape[1] % 128 == 0 for b in blocks)
+    if direct:
+        wq, wo, wu, wd = gather_blocks(blocks, depths)
+    else:
+        wq, wo, wu, wd = (fetch(b, r) for b, r in zip(blocks, along))
     q, k, v, kp, vp, n, n_prev, own_sums = project(x, x_prev, wq, gain1, span)
     own_sums = own_sums.reshape(-1, 2 * width)
     n_sum = jnp.sum(n.reshape(-1, span, width).astype(F32), axis=1).astype(BF16)
@@ -501,13 +806,18 @@
     gains = jnp.concatenate([jnp.sum(ggain1, axis=0), jnp.sum(ggain2, axis=0)]).reshape(2, width)
     gains = lax.psum(gains, "dp")
     gains = lax.psum_scatter(gains, "ctx", scatter_dimension=1, tiled=True)
+    partials = (gqkv, gout, gup, gdown)
+    if direct:
+        sums_w = scatter_blocks(partials, depths)
+    else:
+        sums_w = [reduce_weight(p, r) for p, r in zip(partials, along)]
     return (
         out.reshape(tokens.shape),
         input_grad.reshape(tokens.shape),
-        reduce_weight(gqkv, 0),
-        reduce_weight(gout, 0),
-        reduce_weight(gup, 0),
-        reduce_weight(gdown, 1).T,
+        sums_w[0].T,
+        sums_w[1].T,
+        sums_w[2],
+        sums_w[3].T,
         gains[0],
         gains[1],
     )

time: 555 us -> 345 us (0.62)
  waiting for transfers between devices: 255 us -> 37.1 us
  Pallas kernels: 133 us -> 218 us
  blocking collectives: 115 us -> 46 us
    reduce_scatter x6 -> x0, waiting for transfers between devices: 156 us -> none  [the longest x2 86.9 us: reduce_weight(): lax.psum_scatter(partial, 'ctx', scatter_dimension=1 - row_axis, tiled=True)]
    pallas_call x0 -> x2, Pallas kernels: none -> 85.4 us  [the longest x1 43.2 us: scatter_blocks(): pl.pallas_call(functools.partial(scatter_kernel, depths, count), in_specs...]
    all_gather x5 -> x0, blocking collectives: 68.5 us -> none  [the longest x4 45.1 us: fetch(): lax.all_gather(shard, 'ctx', axis=1, tiled=True)]
    unnamed x16 -> x3, waiting for transfers between devices: 62.8 us -> 0.05 us
    unnamed x31 -> x17, local copies, waits for them, and re-layouts: 15.2 us -> 13.3 us
  transfers between devices with their start and end apart: 15 -> 4, of which waited for: 9 -> 1; matrix products, arithmetic and copies ran while one was open for 4% -> 2% of each run, Pallas kernels for 16% -> 25%
where the time goes in v2:
time: 345 us; the launch traced here: 344 us
  Pallas kernels  218 us (63%)
  blocking collectives  46 us (13%)
  waiting for transfers between devices  37.1 us (11%)
  local copies, waits for them, and re-layouts  20.5 us (6%)
  between operations  14.8 us (4%)
  starting transfers between devices  3.9 us (1%)
  other arithmetic  3.87 us (1%)
    pallas_call x1, Pallas kernels, feed(): pl.pallas_call(feed_kernel, grid=(rows // tile,), in_specs=[row_spec(tile...  43.3 us
    pallas_call x1, Pallas kernels, scatter_blocks(): pl.pallas_call(functools.partial(scatter_kernel, depths, count), in_specs...  43.2 us
    pallas_call x1, Pallas kernels, gather_blocks(): pl.pallas_call(functools.partial(gather_kernel, depths), in_specs=[pl.Blo...  42.2 us
    pallas_call x1, Pallas kernels, give_back(): pl.pallas_call(functools.partial(return_kernel, span), grid=(rows // tile...  41 us
    reduce_scatter x1, waiting for transfers between devices, shards(): gs_own = lax.psum_scatter(gs, 'ctx', scatter_dimension=1, tiled=True)  37.1 us
    unnamed x1, blocking collectives  27.1 us
    pallas_call x1, Pallas kernels, attend(): pl.pallas_call(functools.partial(attend_kernel, span), grid=(rows // tile...  26.5 us
    unnamed x17, local copies, waits for them, and re-layouts  13.3 us
  transfers between devices with their start and end apart: 4, of which 1 were waited for; matrix products, arithmetic and copies ran while one was open for 2% of the time, Pallas kernels for 25%

profile of v2, /device:TPU:0, one launch (start us, length us, event | category | flops | bytes accessed | tf_op | source)
XLA Modules:
  0.0 344.0 jit_solution(12227833772956334844)
XLA Ops:
  7.2 2.5 collective-permute-start
  9.8 1.3 reshape.54.prefix_ref
  11.0 1.2 dynamic-slice
  12.9 0.9 dynamic-update-slice
  13.8 0.8 dynamic-update-slice.1
  14.6 27.1 %all-reduce.2 = (bf16[512]{0:T(512)(128)(2,1)S(1)}, bf16[512]{0:T(512)(128)(2,1)S(1)}) all-reduce(bf16[512]{0:T(512)(128)(2,1)S(1)} %dynamic-update-slice, bf16[512]{0:T(512)(128)(2,1)S(1)} %dynamic-update-slice.1), channel_id=1, replica_groups=mesh['dp'=4,'ctx'=8] {'ctx'}, use_global_device_ids=true, to_apply=%add | all-reduce | flops 1024 | bytes 4096
  42.9 42.2 %gather.1 = (bf16[4,8,192,128]{3,2,1,0:T(8,128)(2,1)}, bf16[4,8,64,128]{3,2,1,0:T(8,128)(2,1)}, bf16[4,8,128,256]{3,2,1,0:T(8,128)(2,1)}, bf16[4,8,64,512]{3,2,1,0:T(8,128)(2,1)}) custom-call(bf16[192,128]{1,0:T(8,128)(2,1)} %bitcast.38, bf16[64,128]{1,0:T(8,128)(2,1)} %bitcast.43, bf16[128,256]{1,0:T(8,128)(2,1)} %refs_2_.1, bf16[64,512]{1,0:T(8,128)(2,1)} %bitcast.37), custom_call_target="tpu_custom_call" | custom-call | tf_op jit(solution)/shard_map/gather/pallas_call | solution.py:140
  85.1 1.3 copy-done
  86.5 12.4 %project.1 = (bf16[2048,512]{1,0:T(8,128)(2,1)}, bf16[2048,512]{1,0:T(8,128)(2,1)}, bf16[2048,512]{1,0:T(8,128)(2,1)}, bf16[2048,512]{1,0:T(8,128)(2,1)}, bf16[2...) custom-call(bf16[2048,512]{1,0:T(8,128)(2,1)} %bitcast.27, ...), custom_call_target="tpu_custom_call" | custom-call | tf_op jit(solution)/shard_map/project/pallas_call | solution.py:399
  98.8 0.8 reshape.58
  99.6 1.9 bitcast_reduce_fusion
  101.5 8.5 %all-gather = bf16[128,1536]{1,0:T(8,128)(2,1)S(1)} all-gather(bf16[16,1536]{1,0:T(8,128)(2,1)S(1)} %pad_maximum_fusion), channel_id=2, replica_groups=mesh['dp'=4,'ctx'=8] {'ctx'}, dimensions={0}, use_global_device_ids=true | all-gather | bytes 442368 | tf_op jit(solution)/shard_map/all_gather | solution.py:797
  110.3 0.7 slice.17.nsum_ref
  110.9 0.7 slice.16.sums_ref
  111.7 26.5 %attend.1 = (bf16[2048,512]{1,0:T(8,128)(2,1)}, bf16[16,4,256,256]{3,2,1,0:T(8,128)(2,1)}, bf16[16,64,128]{2,1,0:T(8,128)(2,1)}) custom-call(s32[16]{0:T(128)} %reshape.54.prefix_ref, s32[1]{0:T(128)} %bitcast.3.block_ref, bf16[2048,512]{1,0:T(8,128)(2,1)} %get-tuple-element.41.q_ref, bf16[2048,512]{1,0:T(8,128)(2,1)} %get-tuple-element.42.k_ref, ...), custom_call_target="tpu_custom_call" | custom-call | tf_op jit(solution)/shard_map/attend/pallas_call | solution.py:490
  138.2 43.3 %feed.1 = (bf16[2048,512]{1,0:T(8,128)(2,1)}, bf16[2048,512]{1,0:T(8,128)(2,1)}, f32[2048,512]{1,0:T(8,128)}, bf16[4,8,64,128]{3,2,1,0:T(8,128)(2,1)}, bf16[4,8,...) custom-call(bf16[2048,512]{1,0:T(8,128)(2,1)} %bitcast.28, ...), custom_call_target="tpu_custom_call" | custom-call | tf_op jit(solution)/shard_map/feed/pallas_call | solution.py:572
  181.5 41.0 %give_back.1 = (f32[2048,512]{1,0:T(8,128)}, bf16[2048,512]{1,0:T(8,128)(2,1)}, bf16[16,8,512]{2,1,0:T(8,128)(2,1)}, bf16[4,8,192,128]{3,2,1,0:T(8,128)(2,1)}) custom-call(bf16[2048,512]{1,0:T(8,128)(2,1)} %get-tuple-element.41.q_ref, bf16[2048,512]{1,0:T(8,128)(2,1)} %get-tuple-element.42.k_ref, bf16[2048,512]{1,0:T(8,128)(2,1)} %get-tuple-element.43.v_ref, ...), custom_call_target="tpu_custom_call" | custom-call | tf_op jit(solution)/shard_map/give_back/pallas_call | solution.py:693
  222.5 1.3 collective-permute-start.1
  223.8 1.6 copy.19
  225.6 37.1 %reduce-scatter.5.cloned.1.call-done = bf16[16,1,512]{2,0,1:T(8,128)(2,1)} async-done(((bf16[16,8,512]{2,0,1:T(8,128)(2,1)}), bf16[16,1,512]{2,0,1:T(8,128)(2,1)}) %reduce-scatter.5.cloned.1.call-update) | async-done | bytes 16400 | tf_op jit(solution)/shard_map/reduce_scatter | solution.py:804
  262.6 1.4 copy.20.gs_ref
  264.0 1.4 copy-done.1
  265.3 9.1 %close.1 = (bf16[2048,512]{1,0:T(8,128)(2,1)}, f32[8,512]{1,0:T(8,128)}) custom-call(bf16[2048,512]{1,0:T(8,128)(2,1)} %bitcast.29, f32[2048,512]{1,0:T(8,128)} %get-tuple-element.57.gn_ref, bf16[2048,512]{1,0:T(8,128)(2,1)} %copy-done.1, bf16[16,1,512]{2,1,0:T(2,128)(2,1)} %copy.20.gs_ref, f32[2048,512]{1,0:T(8,128)} %get-tuple-element.60.gr_ref, ...), custom_call_target="tpu_custom_call" | custom-call | tf_op jit(solution)/shard_map/close/pallas_call | solution.py:751
  274.4 0.7 reduce_sum.31
  275.2 0.8 copy.21
  276.1 43.2 %scatter.1 = (f32[192,128]{1,0:T(8,128)}, f32[64,128]{1,0:T(8,128)}, f32[128,256]{1,0:T(8,128)}, f32[64,512]{1,0:T(8,128)}) custom-call(bf16[4,8,192,128]{3,2,1,0:T(8,128)(2,1)} %get-tuple-element.62.refs_0_, bf16[4,8,64,128]{3,2,1,0:T(8,128)(2,1)} %get-tuple-element.63.refs_1_, bf16[4,8,128,256]{3,2,1,0:T(8,128)(2,1)} %get-tuple-element.64.refs_2_, ...), custom_call_target="tpu_custom_call" | custom-call | tf_op jit(solution)/shard_map/scatter/pallas_call | solution.py:275
  319.3 0.8 copy.22
  320.1 10.4 %psum.8 = f32[2,64]{1,0:T(2,128)S(1)} all-reduce(f32[2,64]{1,0:T(2,128)S(1)} %copy.22), channel_id=1, replica_groups=mesh['dp'=4,'ctx'=8] {'dp'}, use_global_device_ids=true, to_apply=%region_4.0 | all-reduce | flops 128 | bytes 1024 | tf_op jit(solution)/shard_map/psum | solution.py:807
  331.1 1.5 copy.31
  332.6 1.4 copy.32
  334.0 1.6 copy.33
  335.6 1.6 copy.34
  (21 shorter events, 2.1 us)
Async XLA Ops:
  7.2 255.4 %reduce-scatter.5.cloned.1.call-start = ((), (), s32[]{:S(2)}) async-start(), calls=%async_computation.2 | async-start | bytes 147456 | tf_op jit(solution)/shard_map/reduce_scatter | solution.py:804
  7.2 77.9 %collective-permute-start = (bf16[2048,512]{1,0:T(8,128)(2,1)}, bf16[2048,512]{1,0:T(8,128)(2,1)S(1)}, u32[]{:S(2)}, u32[]{:S(2)}) collective-permute-start(bf16[2048,512]{1,0:T(8,128)(2,1)} %bitcast.26), channel_id=1, source_target_pairs={{0,1},{1,2},{2,3},{3,4},{4,5},{5,6},{6,7},{8,9},{9,10},{10,11},{11... | collective-permute-start | bytes 6291464 | tf_op jit(solution)/shard_map/ppermute | solution.py:783
  85.1 1.3 copy-start
  181.5 44.0 %copy-start.2 = (f32[8,512]{1,0:T(8,128)S(1)}, f32[8,512]{1,0:T(8,128)}, u32[]{:S(2)}) copy-start(f32[8,512]{1,0:T(8,128)} %get-tuple-element.71) | copy-start | bytes 49156
  222.5 41.4 %collective-permute-start.1 = (bf16[2048,512]{1,0:T(8,128)(2,1)}, bf16[2048,512]{1,0:T(8,128)(2,1)S(1)}, u32[]{:S(2)}, u32[]{:S(2)}) collective-permute-start(bf16[2048,512]{1,0:T(8,128)(2,1)} %get-tuple-element.58), channel_id=1, source_target_pairs={{1,0},{2,1},{3,2},{4,3},{5,4},{6,5},{7,6},{9,8},{10,9},{11,10},{12... | collective-permute-start | bytes 6291464 | tf_op jit(solution)/shard_map/ppermute | solution.py:803
  225.5 93.8 %reduce-scatter.7.cloned.1.call-start = ((), (), s32[]{:S(2)}) async-start(), calls=%async_computation.3 | async-start | bytes 294912
  264.0 1.4 copy-start.1
Sparse Core Ops, SparseCore 0:
  225.6 36.9 reduce-scatter.4
  276.2 33.8 reduce-scatter.6

commit v3 on v2

--- a/solution.py
+++ b/solution.py
@@ -40,16 +40,42 @@
 
 def greet(depths):
     barrier = pltpu.get_barrier_semaphore()
-    peers = [(turn, 0) for turn in range(1, depths)] + [(0, 1), (0, 2), (0, 4)]
+    peers = [(turn, 0) for turn in range(1, depths)] + [(0, flip) for flip in range(1, FLIPS)]
     for turn, flip in peers:
         pl.semaphore_signal(barrier, inc=1, device_id=spot_of(depths, turn, flip), device_id_type=MESH)
     pl.semaphore_wait(barrier, len(peers))
 
 
-class Gather:
-    def __init__(self, depths, own, full, send, recv):
-        self.depths, self.own, self.full, self.send, self.recv = depths, own, full, send, recv
-        self.sent = []
+class Moves:
+    def __init__(self, depths, send, recv):
+        self.depths, self.send, self.recv, self.sent = depths, send, recv, 0
+
+    def copy(self, source, target, number, slot, to_turn, to_flip):
+        return pltpu.make_async_remote_copy(
+            src_ref=source,
+            dst_ref=target,
+            send_sem=self.send.at[number],
+            recv_sem=self.recv.at[slot],
+            device_id=spot_of(self.depths, to_turn, to_flip),
+            device_id_type=MESH,
+        )
+
+    def start(self, source, target, slot, to_turn, to_flip):
+        self.copy(source, target, self.sent, slot, to_turn, to_flip).start()
+        self.sent += 1
+
+    def landed(self, target, slot):
+        self.copy(target, target, 0, slot, 0, 1).wait_recv()
+
+    def drain(self, like):
+        for number in range(self.sent):
+            self.copy(like, like, number, 0, 0, 1).wait_send()
+
+
+class Gather(Moves):
+    def __init__(self, depths, own, full, send, recv, keep):
+        super().__init__(depths, send, recv)
+        self.own, self.full, self.keep = own, full, keep
 
     def block(self, turn, flip):
         return self.full.at[spot_of(self.depths, turn, flip)]
@@ -57,34 +83,17 @@
     def push(self, turn, flip, to_turn, to_flip):
         there = ((turn - to_turn) % self.depths) * FLIPS + (flip ^ to_flip)
         source = self.own if (turn, flip) == (0, 0) else self.block(turn, flip)
-        copy = pltpu.make_async_remote_copy(
-            src_ref=source,
-            dst_ref=self.block(turn, flip),
-            send_sem=self.send.at[len(self.sent)],
-            recv_sem=self.recv.at[there],
-            device_id=spot_of(self.depths, to_turn, to_flip),
-            device_id_type=MESH,
-        )
-        copy.start()
-        self.sent.append(copy)
+        self.start(source, self.block(turn, flip), there, to_turn, to_flip)
 
     def arrive(self, turn, flip):
-        pltpu.make_async_remote_copy(
-            src_ref=self.block(turn, flip),
-            dst_ref=self.block(turn, flip),
-            send_sem=self.send.at[0],
-            recv_sem=self.recv.at[turn * FLIPS + flip],
-            device_id=spot_of(self.depths, 0, 1),
-            device_id_type=MESH,
-        ).wait_recv()
-
-    def begin(self, keep):
-        self.keep = pltpu.make_async_copy(self.own, self.block(0, 0), keep)
-        self.keep.start()
+        self.landed(self.block(turn, flip), turn * FLIPS + flip)
+
+    def begin(self):
         for turn in range(1, self.depths):
             self.push(0, 0, turn, 0)
         for flip in (2, 4, 1):
             self.push(0, 0, 0, flip)
+        pltpu.make_async_copy(self.own, self.block(0, 0), self.keep).start()
 
     def spread(self):
         for turn in range(1, self.depths):
@@ -112,76 +121,47 @@
         for turn in range(self.depths):
             for flip in (1, 3, 5, 7):
                 self.arrive(turn, flip)
-        for copy in self.sent:
-            copy.wait_send()
-        self.keep.wait()
-
-
-def gather_kernel(depths, *refs):
-    count = len(refs) // 2 - 1
-    owns, fulls = refs[:count], refs[count : 2 * count]
-    send, recv, keep = refs[2 * count :]
-    greet(depths)
-    moves = [Gather(depths, owns[a], fulls[a], send.at[a], recv.at[a]) for a in range(count)]
-    for a, move in enumerate(moves):
-        move.begin(keep.at[a])
-    for move in moves:
-        move.spread()
-    for move in moves:
-        move.cross()
-    for move in moves:
-        move.hand_over()
-    for move in moves:
-        move.complete()
-
-
-def gather_blocks(blocks, depths):
-    total = depths * FLIPS
-    return pl.pallas_call(
-        functools.partial(gather_kernel, depths),
-        in_specs=[pl.BlockSpec(memory_space=pltpu.VMEM)] * len(blocks),
-        out_specs=[pl.BlockSpec(memory_space=pl.ANY)] * len(blocks),
-        out_shape=[jax.ShapeDtypeStruct((depths, FLIPS) + b.shape, b.dtype) for b in blocks],
-        scratch_shapes=[
-            pltpu.SemaphoreType.DMA((len(blocks), total)),
-            pltpu.SemaphoreType.DMA((len(blocks), total)),
-            pltpu.SemaphoreType.DMA((len(blocks),)),
-        ],
-        compiler_params=pltpu.CompilerParams(collective_id=0, has_side_effects=True, vmem_limit_bytes=VMEM_MOST),
-        name="gather",
-    )(*blocks)
-
-
-class Scatter:
+        pltpu.make_async_copy(self.own, self.block(0, 0), self.keep).wait()
+
+    def close(self):
+        self.drain(self.own)
+
+
+class Share(Moves):
+    def __init__(self, depths, slots, send, recv):
+        super().__init__(depths, send, recv)
+        self.slots = slots
+
+    def block(self, flip):
+        return self.slots.at[spot_of(self.depths, 0, flip)[1]]
+
+    def begin(self):
+        for flip in (2, 4, 6, 1):
+            self.start(self.block(0), self.block(0), flip, 0, flip)
+
+    def forward(self):
+        for flip in (2, 4, 6):
+            self.landed(self.block(flip), flip)
+            self.start(self.block(flip), self.block(flip), flip ^ 1, 0, 1)
+
+    def complete(self):
+        for flip in (1, 3, 5, 7):
+            self.landed(self.block(flip), flip)
+
+    def close(self):
+        self.drain(self.block(0))
+
+
+class Scatter(Moves):
     def __init__(self, depths, part, mate, total, near, far, send, recv):
-        self.depths, self.part, self.mate, self.total = depths, part, mate, total
-        self.near, self.far, self.send, self.recv = near, far, send, recv
-        self.sent = []
+        super().__init__(depths, send, recv)
+        self.part, self.mate, self.total, self.near, self.far = part, mate, total, near, far
 
     def block(self, turn, flip):
         return self.part.at[spot_of(self.depths, turn, flip)]
 
-    def push(self, source, target, slot, to_turn, to_flip):
-        copy = pltpu.make_async_remote_copy(
-            src_ref=source,
-            dst_ref=target,
-            send_sem=self.send.at[len(self.sent)],
-            recv_sem=self.recv.at[slot],
-            device_id=spot_of(self.depths, to_turn, to_flip),
-            device_id_type=MESH,
-        )
-        copy.start()
-        self.sent.append(copy)
-
-    def arrive(self, target, slot):
-        pltpu.make_async_remote_copy(
-            src_ref=target,
-            dst_ref=target,
-            send_sem=self.send.at[0],
-            recv_sem=self.recv.at[slot],
-            device_id=spot_of(self.depths, 0, 1),
-            device_id_type=MESH,
-        ).wait_recv()
+    push = Moves.start
+    arrive = Moves.landed
 
     def begin(self):
         for flip in (6, 2, 4, 0):
@@ -233,9 +213,10 @@
         for turn in range(1, self.depths):
             self.arrive(self.far.at[2, turn], last + turn)
             out = out + self.far[2, turn].astype(F32)
-        for copy in self.sent:
-            copy.wait_send()
         return out
+
+    def close(self):
+        self.drain(self.near.at[0])
 
 
 def scatter_scratch(block, depths):
@@ -245,43 +226,6 @@
         pltpu.VMEM((depths,) + block, BF16),
         pltpu.VMEM((3, depths) + block, BF16),
     ]
-
-
-def scatter_kernel(depths, count, *refs):
-    parts, outs = refs[:count], refs[count : 2 * count]
-    send, recv = refs[-2:]
-    greet(depths)
-    moves = []
-    for a in range(count):
-        mate, total, near, far = refs[2 * count + 4 * a : 2 * count + 4 * a + 4]
-        moves.append(Scatter(depths, parts[a], mate, total, near, far, send.at[a], recv.at[a]))
-    for move in moves:
-        move.begin()
-    for move in moves:
-        move.cross()
-    for move in moves:
-        move.spread()
-    for move in moves:
-        move.climb()
-    for a, move in enumerate(moves):
-        outs[a][...] = move.finish()
-
-
-def scatter_blocks(parts, depths):
-    count = len(parts)
-    scratch = []
-    for part in parts:
-        scratch += scatter_scratch(part.shape[2:], depths)
-    return pl.pallas_call(
-        functools.partial(scatter_kernel, depths, count),
-        in_specs=[pl.BlockSpec(memory_space=pltpu.VMEM)] * count,
-        out_specs=[pl.BlockSpec(memory_space=pltpu.VMEM)] * count,
-        out_shape=[jax.ShapeDtypeStruct(p.shape[2:], F32) for p in parts],
-        scratch_shapes=scratch
-        + [pltpu.SemaphoreType.DMA((count, 8 * depths)), pltpu.SemaphoreType.DMA((count, 8 * depths))],
-        compiler_params=pltpu.CompilerParams(collective_id=1, has_side_effects=True, vmem_limit_bytes=VMEM_MOST),
-        name="scatter",
-    )(*parts)
 
 
 def dot(a, b):
@@ -408,78 +352,89 @@
     )(x, x_prev, w_qkv, gain)
 
 
-def attend_kernel(
-    span, prefix_ref, block_ref, q_ref, k_ref, v_ref, kp_ref, vp_ref, sums_ref, mixed_ref, prob_ref, psum_ref
-):
-    width = q_ref.shape[1]
+def attend_one(span, block, prefix, queries, keys, values, sums, keep_prob):
+    width = queries.shape[1]
     pair = 2 * width // HEADS
     half = pair // 2
-    count = sums_ref.shape[1]
-    tile = pl.program_id(0)
-    block = block_ref[0]
+    count = sums.shape[0]
     select = head_select(count, width)
     unit_pos = lax.broadcasted_iota(jnp.int32, (span, span), 0)
     query_pos = lax.broadcasted_iota(jnp.int32, (span, span), 1)
     sum_id = lax.broadcasted_iota(jnp.int32, (count, span), 0)
     sum_query = lax.broadcasted_iota(jnp.int32, (count, span), 1)
     bias_prev = jnp.where(block >= 1, 0.0, MASKED).astype(F32)
+    start = block * span
+    own_ok = (unit_pos <= query_pos) | (start + unit_pos < prefix)
+    bias_own = jnp.where(own_ok, 0.0, MASKED)
+    sum_ok = (sum_id <= block - 1) | (
+        (start + sum_query < prefix) & (sum_id >= block + 1) & ((sum_id + 1) * span <= prefix)
+    )
+    bias_sum = jnp.where(sum_ok, math.log(span), MASKED)
+    values_t = values.T
+    sum_keys = per_head(sums[:, :width], select)
+    sum_values_t = per_head(sums[:, width : 2 * width], select).T
+    sum_scores = dot_t(sum_keys, queries)
+    mixed_parts = []
+    sum_probs = []
+    for p in range(HEADS // 2):
+        lanes = slice(p * pair, (p + 1) * pair)
+        scores = dot_t(keys[:, lanes], pair_halves(queries[:, lanes]))
+        probs = []
+        for e in range(2):
+            h = 2 * p + e
+            cols = slice(e * span, (e + 1) * span)
+            s_prev = scores[:span, cols]
+            s_own = scores[span:, cols] + bias_own
+            s_sum = sum_scores[h * count : (h + 1) * count] + bias_sum
+            most = jnp.maximum(
+                jnp.maximum(
+                    jnp.max(s_prev, axis=0, keepdims=True) + bias_prev,
+                    jnp.max(s_own, axis=0, keepdims=True),
+                ),
+                jnp.max(s_sum, axis=0, keepdims=True),
+            )
+            e_prev = jnp.exp(s_prev + (bias_prev - most))
+            e_own = jnp.exp(s_own - most)
+            e_sum = jnp.exp(s_sum - most)
+            total = (
+                jnp.sum(e_prev, axis=0, keepdims=True)
+                + jnp.sum(e_own, axis=0, keepdims=True)
+                + jnp.sum(e_sum, axis=0, keepdims=True)
+            )
+            inverse = 1.0 / total
+            probs.append(jnp.concatenate([e_prev * inverse, e_own * inverse], axis=0).astype(BF16))
+            sum_probs.append(e_sum * inverse)
+        both = jnp.concatenate(probs, axis=1)
+        keep_prob(p, both)
+        crossed = dot(values_t[lanes, :], both)
+        mixed_parts.append(crossed[:half, :span])
+        mixed_parts.append(crossed[half:, span:])
+    all_sums = jnp.concatenate(sum_probs, axis=0).astype(BF16)
+    mixed_t = jnp.concatenate(mixed_parts, axis=0) + dot(sum_values_t, all_sums)
+    return mixed_t.T.astype(BF16), all_sums
+
+
+def attend_kernel(
+    span, prefix_ref, block_ref, q_ref, k_ref, v_ref, kp_ref, vp_ref, sums_ref, mixed_ref, prob_ref, psum_ref
+):
     for s in range(TILE_SEQS):
-        prefix = prefix_ref[tile * TILE_SEQS + s]
-        start = block * span
         rows = slice(s * span, (s + 1) * span)
-        own_ok = (unit_pos <= query_pos) | (start + unit_pos < prefix)
-        bias_own = jnp.where(own_ok, 0.0, MASKED)
-        sum_ok = (sum_id <= block - 1) | (
-            (start + sum_query < prefix) & (sum_id >= block + 1) & ((sum_id + 1) * span <= prefix)
+
+        def keep_prob(p, both, s=s):
+            prob_ref[s, p] = both
+
+        mixed, all_sums = attend_one(
+            span,
+            block_ref[0],
+            prefix_ref[pl.program_id(0) * TILE_SEQS + s],
+            q_ref[rows, :],
+            jnp.concatenate([kp_ref[rows, :], k_ref[rows, :]], axis=0),
+            jnp.concatenate([vp_ref[rows, :], v_ref[rows, :]], axis=0),
+            sums_ref[s],
+            keep_prob,
         )
-        bias_sum = jnp.where(sum_ok, math.log(span), MASKED)
-        queries = q_ref[rows, :]
-        keys = jnp.concatenate([kp_ref[rows, :], k_ref[rows, :]], axis=0)
-        values_t = jnp.concatenate([vp_ref[rows, :], v_ref[rows, :]], axis=0).T
-        sum_keys = per_head(sums_ref[s, :, :width], select)
-        sum_values_t = per_head(sums_ref[s, :, width:], select).T
-        sum_scores = dot_t(sum_keys, queries)
-        mixed_parts = []
-        sum_probs = []
-        for p in range(HEADS // 2):
-            lanes = slice(p * pair, (p + 1) * pair)
-            scores = dot_t(keys[:, lanes], pair_halves(queries[:, lanes]))
-            probs = []
-            for e in range(2):
-                h = 2 * p + e
-                cols = slice(e * span, (e + 1) * span)
-                s_prev = scores[:span, cols]
-                s_own = scores[span:, cols] + bias_own
-                s_sum = sum_scores[h * count : (h + 1) * count] + bias_sum
-                most = jnp.maximum(
-                    jnp.maximum(
-                        jnp.max(s_prev, axis=0, keepdims=True) + bias_prev,
-                        jnp.max(s_own, axis=0, keepdims=True),
-                    ),
-                    jnp.max(s_sum, axis=0, keepdims=True),
-                )
-                e_prev = jnp.exp(s_prev + (bias_prev - most))
-                e_own = jnp.exp(s_own - most)
-                e_sum = jnp.exp(s_sum - most)
-                total = (
-                    jnp.sum(e_prev, axis=0, keepdims=True)
-                    + jnp.sum(e_own, axis=0, keepdims=True)
-                    + jnp.sum(e_sum, axis=0, keepdims=True)
-                )
-                inverse = 1.0 / total
-                probs.append(
-                    jnp.concatenate([e_prev * inverse, e_own * inverse], axis=0).astype(BF16)
-                )
-                sum_probs.append(e_sum * inverse)
-            both = jnp.concatenate(probs, axis=1)
-            prob_ref[s, p] = both
-            crossed = dot(values_t[lanes, :], both)
-            mixed_parts.append(crossed[:half, :span])
-            mixed_parts.append(crossed[half:, span:])
-        all_sums = jnp.concatenate(sum_probs, axis=0).astype(BF16)
+        mixed_ref[rows, :] = mixed
         psum_ref[s] = all_sums
-        mixed_t = jnp.concatenate(mixed_parts, axis=0) + dot(sum_values_t, all_sums)
-        mixed_ref[rows, :] = mixed_t.T.astype(BF16)
 
 
 def attend(prefix, block, q, k, v, kp, vp, sums, span):
@@ -596,89 +551,102 @@
     )(x, mixed, grad, w_out, w_up, w_down, gain)
 
 
+def return_one(span, queries, keys, values, sums, grad_mixed, prob_at, sum_low):
+    width = queries.shape[1]
+    pair = 2 * width // HEADS
+    half = pair // 2
+    count = sums.shape[0]
+    scale = half ** -0.5
+    select = head_select(count, width)
+    keys_t = keys.T
+    sum_keys_t = per_head(sums[:, :width], select).T
+    sum_values = per_head(sums[:, width : 2 * width], select)
+    sum_prob = sum_low.astype(F32)
+    sum_moved = sum_prob * dot_t(sum_values, grad_mixed)
+    grad_q_parts = []
+    grad_k_parts = []
+    grad_v_parts = []
+    sum_grads = []
+    for p in range(HEADS // 2):
+        lanes = slice(p * pair, (p + 1) * pair)
+        grads2 = pair_halves(grad_mixed[:, lanes])
+        grad_prob = dot_t(values[:, lanes], grads2)
+        low = prob_at(p)
+        prob = low.astype(F32)
+        moved = prob * grad_prob
+        deltas = jnp.sum(moved, axis=0, keepdims=True)
+        sums_of = []
+        for e in range(2):
+            h = 2 * p + e
+            part = slice(h * count, (h + 1) * count)
+            delta = deltas[:, e * span : (e + 1) * span] + jnp.sum(sum_moved[part], axis=0, keepdims=True)
+            sums_of.append(delta)
+            sum_grads.append(sum_moved[part] - sum_prob[part] * delta)
+        grad_scores = (moved - prob * jnp.concatenate(sums_of, axis=1)).astype(BF16)
+        grad_k_parts.append(dot(grad_scores, pair_halves(queries[:, lanes])))
+        grad_v_parts.append(dot(low, grads2))
+        crossed = dot(keys_t[lanes, :], grad_scores)
+        grad_q_parts.append(crossed[:half, :span])
+        grad_q_parts.append(crossed[half:, span:])
+    sum_scores_grad = jnp.concatenate(sum_grads, axis=0).astype(BF16)
+    grad_q = jnp.concatenate(grad_q_parts, axis=0) + dot(sum_keys_t, sum_scores_grad)
+    grad_q = (grad_q.T * scale).astype(BF16)
+    grad_k = jnp.concatenate(grad_k_parts, axis=1).astype(BF16)
+    grad_v = jnp.concatenate(grad_v_parts, axis=1).astype(BF16)
+    wide_k = jnp.where(select, dot(sum_scores_grad, queries), 0.0)
+    wide_v = jnp.where(select, dot(sum_low, grad_mixed), 0.0)
+    folded_k = jnp.sum(wide_k.reshape(HEADS, count, width), axis=0)
+    folded_v = jnp.sum(wide_v.reshape(HEADS, count, width), axis=0)
+    return (
+        jnp.concatenate([grad_q, grad_k[span:], grad_v[span:]], axis=1),
+        jnp.concatenate([grad_k[:span], grad_v[:span]], axis=1),
+        jnp.concatenate([folded_k, folded_v], axis=1) * (1.0 / span),
+    )
+
+
+def return_tile(weight, own, before, shared, normed, normed_prev, normed_sum, acc):
+    width = normed.shape[1]
+    grad_own = jnp.concatenate(own, axis=0)
+    grad_before = jnp.concatenate(before, axis=0)
+    grad_shared = jnp.concatenate(shared, axis=0).astype(BF16)
+    normed_t = normed.T
+    acc[:, :width] += dot(normed_t, grad_own[:, :width])
+    acc[:, width:] += (
+        dot(normed_t, grad_own[:, width:]) + dot(normed_prev.T, grad_before) + dot(normed_sum.T, grad_shared)
+    )
+    return dot(grad_own, weight), dot(grad_before, weight[width:]), dot(grad_shared, weight[width:])
+
+
 def return_kernel(
     span, q_ref, k_ref, v_ref, kp_ref, vp_ref, sums_ref, gm_ref, prob_ref, psum_ref, n_ref, np_ref, nsum_ref, w_ref,
     gn_ref, gp_ref, gs_ref, gqkv_ref, acc,
 ):
-    width = q_ref.shape[1]
-    pair = 2 * width // HEADS
-    half = pair // 2
-    count = sums_ref.shape[1]
-    scale = half ** -0.5
     step = pl.program_id(0)
-    select = head_select(count, width)
 
     @pl.when(step == 0)
     def _():
         acc[...] = jnp.zeros_like(acc)
 
-    own = []
-    before = []
-    shared = []
+    parts = []
     for s in range(TILE_SEQS):
         rows = slice(s * span, (s + 1) * span)
-        queries = q_ref[rows, :]
-        grad_mixed = gm_ref[rows, :]
-        keys_t = jnp.concatenate([kp_ref[rows, :], k_ref[rows, :]], axis=0).T
-        values = jnp.concatenate([vp_ref[rows, :], v_ref[rows, :]], axis=0)
-        sum_keys_t = per_head(sums_ref[s, :, :width], select).T
-        sum_values = per_head(sums_ref[s, :, width:], select)
-        sum_low = psum_ref[s]
-        sum_prob = sum_low.astype(F32)
-        sum_moved = sum_prob * dot_t(sum_values, grad_mixed)
-        grad_q_parts = []
-        grad_k_parts = []
-        grad_v_parts = []
-        sum_grads = []
-        for p in range(HEADS // 2):
-            lanes = slice(p * pair, (p + 1) * pair)
-            grads2 = pair_halves(grad_mixed[:, lanes])
-            grad_prob = dot_t(values[:, lanes], grads2)
-            low = prob_ref[s, p]
-            prob = low.astype(F32)
-            moved = prob * grad_prob
-            deltas = jnp.sum(moved, axis=0, keepdims=True)
-            sums = []
-            for e in range(2):
-                h = 2 * p + e
-                part = slice(h * count, (h + 1) * count)
-                delta = deltas[:, e * span : (e + 1) * span] + jnp.sum(
-                    sum_moved[part], axis=0, keepdims=True
-                )
-                sums.append(delta)
-                sum_grads.append(sum_moved[part] - sum_prob[part] * delta)
-            grad_scores = (moved - prob * jnp.concatenate(sums, axis=1)).astype(BF16)
-            grad_k_parts.append(dot(grad_scores, pair_halves(queries[:, lanes])))
-            grad_v_parts.append(dot(low, grads2))
-            crossed = dot(keys_t[lanes, :], grad_scores)
-            grad_q_parts.append(crossed[:half, :span])
-            grad_q_parts.append(crossed[half:, span:])
-        sum_scores_grad = jnp.concatenate(sum_grads, axis=0).astype(BF16)
-        grad_q = jnp.concatenate(grad_q_parts, axis=0) + dot(sum_keys_t, sum_scores_grad)
-        grad_q = (grad_q.T * scale).astype(BF16)
-        grad_k = jnp.concatenate(grad_k_parts, axis=1).astype(BF16)
-        grad_v = jnp.concatenate(grad_v_parts, axis=1).astype(BF16)
-        own.append(jnp.concatenate([grad_q, grad_k[span:], grad_v[span:]], axis=1))
-        before.append(jnp.concatenate([grad_k[:span], grad_v[:span]], axis=1))
-        wide_k = jnp.where(select, dot(sum_scores_grad, queries), 0.0)
-        wide_v = jnp.where(select, dot(sum_low, grad_mixed), 0.0)
-        folded_k = jnp.sum(wide_k.reshape(HEADS, count, width), axis=0)
-        folded_v = jnp.sum(wide_v.reshape(HEADS, count, width), axis=0)
-        shared.append(jnp.concatenate([folded_k, folded_v], axis=1) * (1.0 / span))
-    grad_own = jnp.concatenate(own, axis=0)
-    grad_before = jnp.concatenate(before, axis=0)
-    grad_shared = jnp.concatenate(shared, axis=0).astype(BF16)
-    weight = rows_of(w_ref)
-    gn_ref[...] = dot(grad_own, weight)
-    gp_ref[...] = dot(grad_before, weight[width:]).astype(BF16)
-    gs_ref[...] = dot(grad_shared, weight[width:]).reshape(gs_ref.shape).astype(BF16)
-    normed_t = n_ref[...].T
-    normed_prev_t = np_ref[...].T
-    normed_sum_t = nsum_ref[...].reshape(-1, width).T
-    acc[:, :width] += dot(normed_t, grad_own[:, :width])
-    acc[:, width:] += (
-        dot(normed_t, grad_own[:, width:]) + dot(normed_prev_t, grad_before) + dot(normed_sum_t, grad_shared)
-    )
+        parts.append(
+            return_one(
+                span,
+                q_ref[rows, :],
+                jnp.concatenate([kp_ref[rows, :], k_ref[rows, :]], axis=0),
+                jnp.concatenate([vp_ref[rows, :], v_ref[rows, :]], axis=0),
+                sums_ref[s],
+                gm_ref[rows, :],
+                lambda p, s=s: prob_ref[s, p],
+                psum_ref[s],
+            )
+        )
+    normed_sum = nsum_ref[...].reshape(-1, nsum_ref.shape[2])
+    gn, gp, gs = return_tile(rows_of(w_ref), *zip(*parts), n_ref[...], np_ref[...], normed_sum, acc)
+    gn_ref[...] = gn
+    gp_ref[...] = gp.astype(BF16)
+    gs_ref[...] = gs.reshape(gs_ref.shape).astype(BF16)
 
     @pl.when(step == pl.num_programs(0) - 1)
     def _():
@@ -761,6 +729,507 @@
     )(x, gn, gb, gs, gr, gain)
 
 
+def in_order(count, seqs):
+    row = lax.broadcasted_iota(jnp.int32, (count * seqs, count * seqs), 0)
+    col = lax.broadcasted_iota(jnp.int32, (count * seqs, count * seqs), 1)
+    return ((col % seqs == row // count) & (col // seqs == row % count)).astype(BF16)
+
+
+def neighbour(by):
+    depth, spot = lax.axis_index("dp"), lax.axis_index("ctx")
+    return depth, lax.rem(spot + by + FLIPS, FLIPS)
+
+
+ENTER_RELAYS = {
+    0: ((1, "spread"),),
+    1: ((2, "spread"), (3, "spread")),
+    2: ((1, "cross"),),
+    3: ((2, "cross"),),
+    4: ((1, "hand_over"), (3, "cross")),
+    5: ((2, "hand_over"),),
+    6: ((3, "hand_over"),),
+}
+
+
+def enter_kernel(
+    depths, span,
+    x_ref, prefix_ref, bq_ref, bo_ref, bu_ref, bd_ref, gain_ref,
+    wq_out, wo_out, wu_out, wd_out, gain_out, q_out, k_out, v_out, kp_out, vp_out, n_out, np_out, mixed_out, prob_out,
+    sums_out, psum_out,
+    xp, wq, gains, q, k, v, kp, vp, n, n_prev, mixed, prob, slots,
+    send, recv, keep, gain_send, gain_recv, sum_send, sum_recv, tok_send, tok_recv, out_sem, prob_sem, wq_sem,
+):
+    rows, width = x_ref.shape
+    tile = TILE_SEQS * span
+    tiles = rows // tile
+    seqs = rows // span
+    spot = lax.axis_index("ctx")
+    scale = (width // HEADS) ** -0.5
+    gathers = [
+        Gather(depths, own, full, send.at[a], recv.at[a], keep.at[a])
+        for a, (own, full) in enumerate(((bq_ref, wq), (bo_ref, wo_out), (bu_ref, wu_out), (bd_ref, wd_out)))
+    ]
+    gain_share = Share(depths, gains, gain_send, gain_recv)
+    sum_share = Share(depths, slots, sum_send, sum_recv)
+    gains[spot] = gain_ref[...]
+
+    @pl.when(spot == 0)
+    def _():
+        xp[...] = jnp.zeros_like(xp)
+
+    greet(depths)
+    gathers[0].begin()
+    gain_share.begin()
+    gathers[0].spread()
+    gain_share.forward()
+    gain_share.complete()
+    gain = gains[0]
+    for c in range(1, FLIPS):
+        gain = gain + gains[c]
+    gain_out[...] = gain
+
+    def at(i):
+        return pl.ds(pl.multiple_of(i * tile, tile), tile)
+
+    def token_copy(i):
+        return pltpu.make_async_remote_copy(
+            src_ref=x_ref.at[at(i)],
+            dst_ref=xp.at[at(i)],
+            send_sem=tok_send.at[i],
+            recv_sem=tok_recv.at[i],
+            device_id=neighbour(1),
+            device_id_type=MESH,
+        )
+
+    def out_copy(a, i):
+        pairs = ((q, q_out), (k, k_out), (v, v_out), (n, n_out), (kp, kp_out), (vp, vp_out), (n_prev, np_out), (mixed, mixed_out))
+        return pltpu.make_async_copy(pairs[a][0].at[at(i)], pairs[a][1].at[at(i)], out_sem.at[a, i])
+
+    def prob_copy(i):
+        part = pl.ds(i * TILE_SEQS, TILE_SEQS)
+        return pltpu.make_async_copy(prob.at[part], prob_out.at[part], prob_sem.at[i])
+
+    @pl.loop(0, tiles)
+    def _(i):
+        n[at(i), :] = (standardize(x_ref[at(i), :].astype(F32))[0] * gain[0:1]).astype(BF16)
+
+    gathers[0].cross()
+    gathers[0].hand_over()
+
+    @pl.when(spot < FLIPS - 1)
+    def _():
+        for i in range(tiles):
+            token_copy(i).start()
+
+    for gather in gathers[1:]:
+        gather.begin()
+    gathers[0].complete()
+    wq_copy = pltpu.make_async_copy(wq, wq_out, wq_sem.at[0])
+    wq_copy.start()
+
+    @pl.loop(0, tiles)
+    def _(i):
+        weight = rows_of(wq)
+        normed = n[at(i), :]
+        q[at(i), :] = (dot_t(normed, weight[:width]).astype(BF16).astype(F32) * scale).astype(BF16)
+        k[at(i), :] = dot_t(normed, weight[width : 2 * width]).astype(BF16)
+        v[at(i), :] = dot_t(normed, weight[2 * width :]).astype(BF16)
+        for a in range(4):
+            out_copy(a, i).start()
+
+    for part, (ref, weigh) in enumerate(((k, 1.0 / span), (v, 1.0 / span), (n, 1.0))):
+        means = [
+            jnp.sum(ref[s * span : (s + 1) * span, :].astype(F32), axis=0, keepdims=True) * weigh for s in range(seqs)
+        ]
+        slots[spot, :, part * width : (part + 1) * width] = jnp.concatenate(means, axis=0).astype(BF16)
+    sum_share.begin()
+
+    def project_prev(i):
+        @pl.when(spot > 0)
+        def _():
+            token_copy(i).wait_recv()
+
+        weight = rows_of(wq)
+        normed = (standardize(xp[at(i), :].astype(F32))[0] * gain[0:1]).astype(BF16)
+        n_prev[at(i), :] = normed
+        kp[at(i), :] = dot_t(normed, weight[width : 2 * width]).astype(BF16)
+        vp[at(i), :] = dot_t(normed, weight[2 * width :]).astype(BF16)
+        for a in range(4, 7):
+            out_copy(a, i).start()
+
+    project_prev(0)
+    sum_share.forward()
+    sum_share.complete()
+    ordered = dot(in_order(FLIPS, seqs), slots[...].reshape(FLIPS * seqs, 3 * width)).astype(BF16)
+    sums_out[...] = ordered.reshape(sums_out.shape)
+
+    @pl.loop(0, tiles)
+    def _(i):
+        @pl.when(i + 1 < tiles)
+        def _():
+            project_prev(i + 1)
+
+        for s in range(TILE_SEQS):
+            here = pl.ds(pl.multiple_of(i * tile + s * span, span), span)
+            seq = i * TILE_SEQS + s
+
+            def keep_prob(p, both, seq=seq):
+                prob[seq, p] = both
+
+            rows_mixed, all_sums = attend_one(
+                span,
+                spot,
+                prefix_ref[seq],
+                q[here, :],
+                jnp.concatenate([kp[here, :], k[here, :]], axis=0),
+                jnp.concatenate([vp[here, :], v[here, :]], axis=0),
+                sums_out[seq],
+                keep_prob,
+            )
+            mixed[here, :] = rows_mixed
+            psum_out[seq] = all_sums
+        out_copy(7, i).start()
+        prob_copy(i).start()
+        for when, relays in ENTER_RELAYS.items():
+
+            @pl.when(i == when)
+            def _(relays=relays):
+                for a, name in relays:
+                    getattr(gathers[a], name)()
+
+    for gather in gathers[1:]:
+        gather.complete()
+    for move in (*gathers, gain_share, sum_share):
+        move.close()
+
+    @pl.when(spot < FLIPS - 1)
+    def _():
+        for i in range(tiles):
+            token_copy(i).wait_send()
+
+    wq_copy.wait()
+
+    @pl.loop(0, tiles)
+    def _(i):
+        for a in range(8):
+            out_copy(a, i).wait()
+        prob_copy(i).wait()
+
+
+def enter(x, prefix, blocks, gains, span, depths):
+    rows, width = x.shape
+    tile = TILE_SEQS * span
+    tiles, seqs = rows // tile, rows // span
+    low = jax.ShapeDtypeStruct((rows, width), BF16)
+    fulls = [jax.ShapeDtypeStruct((depths, FLIPS) + b.shape, BF16) for b in blocks]
+    prob_shape = (seqs, HEADS // 2, 2 * span, 2 * span)
+    vmem = pl.BlockSpec(memory_space=pltpu.VMEM)
+    far = pl.BlockSpec(memory_space=pl.ANY)
+    sems = pltpu.SemaphoreType.DMA
+    held = pltpu.VMEM((rows, width), BF16)
+    return pl.pallas_call(
+        functools.partial(enter_kernel, depths, span),
+        in_specs=[vmem, pl.BlockSpec(memory_space=pltpu.SMEM)] + [vmem] * 5,
+        out_specs=[far] * 4 + [vmem] + [far] * 9 + [vmem] * 2,
+        out_shape=fulls
+        + [jax.ShapeDtypeStruct(gains.shape, F32)]
+        + [low] * 8
+        + [
+            jax.ShapeDtypeStruct(prob_shape, BF16),
+            jax.ShapeDtypeStruct((seqs, FLIPS, 3 * width), BF16),
+            jax.ShapeDtypeStruct((seqs, HEADS * FLIPS, span), BF16),
+        ],
+        scratch_shapes=[
+            held,
+            pltpu.VMEM(fulls[0].shape, BF16),
+            pltpu.VMEM((FLIPS,) + gains.shape, F32),
+        ]
+        + [held] * 8
+        + [pltpu.VMEM(prob_shape, BF16), pltpu.VMEM((FLIPS, seqs, 3 * width), BF16)]
+        + [
+            sems((4, depths * FLIPS)), sems((4, depths * FLIPS)), sems((4,)),
+            sems((FLIPS,)), sems((FLIPS,)), sems((FLIPS,)), sems((FLIPS,)),
+            sems((tiles,)), sems((tiles,)), sems((8, tiles)), sems((tiles,)), sems((1,)),
+        ],
+        compiler_params=pltpu.CompilerParams(collective_id=0, has_side_effects=True, vmem_limit_bytes=VMEM_MOST),
+        name="enter",
+    )(x, prefix, *blocks, gains)
+
+
+LEAVE_RELAYS = {
+    1: ((0, "cross"),),
+    2: ((1, "cross"), (0, "spread")),
+    3: ((2, "cross"), (0, "climb")),
+    4: ((1, "spread"),),
+    5: ((2, "spread"), (1, "climb")),
+    6: ((2, "climb"),),
+}
+
+
+def leave_kernel(
+    depths, span,
+    q_in, k_in, v_in, kp_in, vp_in, gm_in, n_in, np_in, prob_in, gr_in, x_in,
+    psum_ref, sums_ref, wq_ref, gout_ref, gup_ref, gdown_ref, gain_ref, ggain_ref,
+    ig_out, dqkv_out, dout_out, dup_out, ddown_out, dgain_out,
+    held, prob, gn, gp, gb, gr, x, ig, acc, part, gs, gs_send_buf, gs_slots, gain_slots, gain_deep,
+    *rest,
+):
+    moves_refs, sems = rest[:16], rest[16:]
+    send, recv, gs_send, gs_recv, gain_send, gain_recv, deep_send, deep_recv, gb_send, gb_recv, in_sem, late_sem, ig_sem = sems
+    rows, width = gn.shape
+    tile = TILE_SEQS * span
+    tiles = rows // tile
+    seqs = rows // span
+    spot = lax.axis_index("ctx")
+    depth = lax.axis_index("dp")
+    parts = (gout_ref, gup_ref, gdown_ref, part)
+    scatters = [
+        Scatter(depths, parts[a], *moves_refs[4 * a : 4 * a + 4], send.at[a], recv.at[a]) for a in range(4)
+    ]
+    gain_share = Share(depths, gain_slots, gain_send, gain_recv)
+    gs_moves = Moves(depths, gs_send, gs_recv)
+    deep_moves = Moves(depths, deep_send, deep_recv)
+
+    def at(i):
+        return pl.ds(pl.multiple_of(i * tile, tile), tile)
+
+    def loads(i, slot):
+        arrays = (q_in, k_in, v_in, kp_in, vp_in, gm_in, n_in, np_in)
+        copies = [pltpu.make_async_copy(ref.at[at(i)], held.at[slot, a], in_sem.at[slot, a]) for a, ref in enumerate(arrays)]
+        of_tile = pl.ds(i * TILE_SEQS, TILE_SEQS)
+        return copies + [pltpu.make_async_copy(prob_in.at[of_tile], prob.at[slot], in_sem.at[slot, len(arrays)])]
+
+    def gb_copy(i):
+        return pltpu.make_async_remote_copy(
+            src_ref=gp.at[at(i)],
+            dst_ref=gb.at[at(i)],
+            send_sem=gb_send.at[i],
+            recv_sem=gb_recv.at[i],
+            device_id=neighbour(-1),
+            device_id_type=MESH,
+        )
+
+    for copy in loads(0, 0):
+        copy.start()
+    late = [pltpu.make_async_copy(gr_in, gr, late_sem.at[0]), pltpu.make_async_copy(x_in, x, late_sem.at[1])]
+
+    @pl.when(spot == FLIPS - 1)
+    def _():
+        gb[...] = jnp.zeros_like(gb)
+
+    greet(depths)
+    for scatter in scatters[:3]:
+        scatter.begin()
+    acc[...] = jnp.zeros_like(acc)
+
+    def tile_step(i, gain_sum):
+        slot = lax.rem(i, 2)
+        for copy in loads(i, slot):
+            copy.wait()
+
+        @pl.when(i + 1 < tiles)
+        def _():
+            for copy in loads(i + 1, 1 - slot):
+                copy.start()
+
+        pieces = []
+        for s in range(TILE_SEQS):
+            here = slice(s * span, (s + 1) * span)
+            seq = i * TILE_SEQS + s
+            pieces.append(
+                return_one(
+                    span,
+                    held[slot, 0, here],
+                    jnp.concatenate([held[slot, 3, here], held[slot, 1, here]], axis=0),
+                    jnp.concatenate([held[slot, 4, here], held[slot, 2, here]], axis=0),
+                    sums_ref[seq],
+                    held[slot, 5, here],
+                    lambda p, s=s: prob[slot, s, p],
+                    psum_ref[seq],
+                )
+            )
+        of_tile = pl.ds(i * TILE_SEQS, TILE_SEQS)
+        normed, normed_prev = held[slot, 6], held[slot, 7]
+        normed_sum = sums_ref[of_tile, :, 2 * width :].reshape(-1, width)
+        to_own, to_prev, to_sums = return_tile(rows_of(wq_ref), *zip(*pieces), normed, normed_prev, normed_sum, acc)
+        gn[at(i), :] = to_own
+        gp[at(i), :] = to_prev.astype(BF16)
+        gs[i] = to_sums.astype(BF16)
+
+        @pl.when(spot > 0)
+        def _():
+            gb_copy(i).start()
+
+        for when, relays in LEAVE_RELAYS.items():
+
+            @pl.when(i == when)
+            def _(relays=relays):
+                for a, name in relays:
+                    getattr(scatters[a], name)()
+
+        @pl.when(i == tiles - 3)
+        def _():
+            for copy in late:
+                copy.start()
+
+        return (
+            gain_sum
+            + fold_rows(to_own * normed.astype(F32))
+            + fold_rows(to_prev * normed_prev.astype(F32))
+            + fold_rows(to_sums * normed_sum.astype(F32))
+        )
+
+    gain_sum = lax.fori_loop(0, tiles, tile_step, jnp.zeros((8, width), F32))
+
+    by_spot = lax.dot_general(
+        in_order(FLIPS, seqs), gs[...].reshape(seqs * FLIPS, width), (((0,), (0,)), ((), ())), preferred_element_type=F32
+    )
+    gs_send_buf[...] = by_spot.astype(BF16).reshape(gs_send_buf.shape)
+    for flip in (6, 7, 2, 4, 3, 5, 1):
+        gs_moves.start(gs_send_buf.at[spot_of(depths, 0, flip)[1]], gs_slots.at[flip], flip, 0, flip)
+    total_one = jnp.sum(gain_sum, axis=0, keepdims=True) / gain_ref[0:1]
+    total_two = jnp.sum(ggain_ref[...], axis=0, keepdims=True)
+    gain_slots[spot] = jnp.concatenate([total_one, total_two], axis=0)
+    gain_share.begin()
+    put_blocks(part, acc[...].astype(BF16).T, 1)
+    scatters[3].begin()
+    dout_out[...] = scatters[0].finish()
+    gain_share.forward()
+    scatters[3].cross()
+    dup_out[...] = scatters[1].finish()
+    ddown_out[...] = scatters[2].finish()
+    for copy in late:
+        copy.wait()
+    for flip in range(1, FLIPS):
+        gs_moves.landed(gs_slots.at[flip], flip)
+    shared = gs_send_buf[spot].astype(F32)
+    for flip in range(1, FLIPS):
+        shared = shared + gs_slots[flip].astype(F32)
+    gain = gain_ref[0:1]
+
+    def close_tile(i):
+        @pl.when(spot < FLIPS - 1)
+        def _():
+            gb_copy(i).wait_recv()
+
+        unit, inv = standardize(x[at(i), :].astype(F32))
+        grad_norm = gn[at(i), :] + gb[at(i), :].astype(F32)
+        lifted = [
+            grad_norm[s * span : (s + 1) * span] + shared[i * TILE_SEQS + s : i * TILE_SEQS + s + 1]
+            for s in range(TILE_SEQS)
+        ]
+        grad_norm = jnp.concatenate(lifted, axis=0)
+        ig[at(i), :] = (gr[at(i), :] + norm_back(grad_norm, unit, inv, gain)).astype(BF16)
+        pltpu.make_async_copy(ig.at[at(i)], ig_out.at[at(i)], ig_sem.at[i]).start()
+
+    cut = tiles // 3
+    for i in range(cut):
+        close_tile(i)
+    scatters[3].spread()
+    gain_share.complete()
+    over_ctx = gain_slots[0]
+    for c in range(1, FLIPS):
+        over_ctx = over_ctx + gain_slots[c]
+    gain_deep[0] = over_ctx
+    for turn in range(1, depths):
+        deep_moves.start(gain_deep.at[0], gain_deep.at[depths - turn], depths - turn, turn, 0)
+    for i in range(cut, 2 * cut):
+        close_tile(i)
+    scatters[3].climb()
+    for i in range(2 * cut, tiles):
+        close_tile(i)
+    for turn in range(1, depths):
+        deep_moves.landed(gain_deep.at[turn], turn)
+    over_all = gain_deep[0]
+    for turn in range(1, depths):
+        over_all = over_all + gain_deep[turn]
+    lanes = width // FLIPS
+    mine = jnp.zeros((2, lanes), F32)
+    for c in range(FLIPS):
+        mine = jnp.where(spot == c, over_all[:, c * lanes : (c + 1) * lanes], mine)
+    dgain_out[...] = mine
+    dqkv_out[...] = scatters[3].finish()
+    for scatter in scatters:
+        scatter.close()
+    gain_share.close()
+    gs_moves.drain(gs_slots.at[0])
+    deep_moves.drain(gain_deep.at[0])
+
+    @pl.when(spot > 0)
+    def _():
+        for i in range(tiles):
+            gb_copy(i).wait_send()
+
+    for i in range(tiles):
+        pltpu.make_async_copy(ig.at[at(i)], ig_out.at[at(i)], ig_sem.at[i]).wait()
+
+
+def leave(arrays, psum, sums, wq, partials, gains, ggain, span, depths):
+    rows, width = arrays[0].shape
+    tile = TILE_SEQS * span
+    tiles, seqs = rows // tile, rows // span
+    vmem = pl.BlockSpec(memory_space=pltpu.VMEM)
+    far = pl.BlockSpec(memory_space=pl.ANY)
+    sems = pltpu.SemaphoreType.DMA
+    low = pltpu.VMEM((rows, width), BF16)
+    high = pltpu.VMEM((rows, width), F32)
+    shapes = [p.shape[2:] for p in (*partials, wq)]
+    scratch = [
+        pltpu.VMEM((2, 8, tile, width), BF16),
+        pltpu.VMEM((2, TILE_SEQS, HEADS // 2, 2 * span, 2 * span), BF16),
+        high, low, low, high, low, low,
+        pltpu.VMEM((width, 3 * width), F32),
+        pltpu.VMEM(wq.shape, BF16),
+        pltpu.VMEM((tiles, TILE_SEQS * FLIPS, width), BF16),
+        pltpu.VMEM((FLIPS, seqs, width), BF16),
+        pltpu.VMEM((FLIPS, seqs, width), BF16),
+        pltpu.VMEM((FLIPS, 2, width), F32),
+        pltpu.VMEM((depths, 2, width), F32),
+    ]
+    for shape in shapes:
+        scratch += scatter_scratch(shape, depths)
+    scratch += [
+        sems((4, 8 * depths)), sems((4, 8 * depths)), sems((FLIPS,)), sems((FLIPS,)), sems((FLIPS,)), sems((FLIPS,)),
+        sems((depths,)), sems((depths,)), sems((tiles,)), sems((tiles,)), sems((2, 9)), sems((2,)), sems((tiles,)),
+    ]
+    outs = [jax.ShapeDtypeStruct(shape, F32) for shape in (shapes[3], *shapes[:3])]
+    return pl.pallas_call(
+        functools.partial(leave_kernel, depths, span),
+        in_specs=[far] * 11 + [vmem] * 8,
+        out_specs=[far] + [vmem] * 5,
+        out_shape=[jax.ShapeDtypeStruct((rows, width), BF16), *outs, jax.ShapeDtypeStruct((2, width // FLIPS), F32)],
+        scratch_shapes=scratch,
+        compiler_params=pltpu.CompilerParams(collective_id=1, has_side_effects=True, vmem_limit_bytes=VMEM_MOST),
+        name="leave",
+    )(*arrays, psum, sums, wq, *partials, gains, ggain)
+
+
+def direct_shards(tokens, prefix, blocks, gain_one, gain_two, cotangent):
+    span, width = tokens.shape[2], tokens.shape[3]
+    depths = lax.axis_size("dp")
+    x = tokens.reshape(-1, width)
+    grad = cotangent.reshape(-1, width)
+    shard = jnp.stack([gain_one, gain_two]).astype(F32)
+    lane_owner = lax.broadcasted_iota(jnp.int32, (2, width), 1) // shard.shape[1]
+    gains = jnp.where(lane_owner == lax.axis_index("ctx"), jnp.tile(shard, (1, FLIPS)), 0.0)
+    (wq, wo, wu, wd, gains, q, k, v, kp, vp, n, n_prev, mixed, prob, sums, psum) = enter(
+        x, prefix.reshape(-1), blocks, gains, span, depths
+    )
+    out, gm, gr, gout, gup, gdown, ggain = feed(x, mixed, grad, wo, wu, wd, gains[1:2], TILE_SEQS * span)
+    arrays = (q, k, v, kp, vp, gm, n, n_prev, prob, gr, x)
+    ig, dqkv, dout, dup, ddown, dgain = leave(arrays, psum, sums, wq, (gout, gup, gdown), gains, ggain, span, depths)
+    return (
+        out.reshape(tokens.shape),
+        ig.reshape(tokens.shape),
+        dqkv.T,
+        dout.T,
+        dup,
+        ddown.T,
+        dgain[0],
+        dgain[1],
+    )
+
+
 def fetch(block, rows_along):
     spot, depth = (0, 1) if rows_along == 1 else (1, 0)
     whole = lax.all_gather(lax.all_gather(block, "ctx", axis=spot, tiled=True), "dp", axis=depth, tiled=True)
@@ -776,6 +1245,10 @@
 def shards(tokens, prefix, w_qkv, w_out, w_up, w_down, gain_one, gain_two, cotangent):
     span, width = tokens.shape[2], tokens.shape[3]
     count = lax.axis_size("ctx")
+    blocks = (w_qkv.T, w_out.T, w_up, w_down.T)
+    if count == FLIPS and all(b.shape[0] % 16 == 0 and b.shape[1] % 128 == 0 for b in blocks):
+        return direct_shards(tokens, prefix, blocks, gain_one, gain_two, cotangent)
+    along = (1, 1, 0, 1)
     x = tokens.reshape(-1, width)
     grad = cotangent.reshape(-1, width)
     tile = TILE_SEQS * span
@@ -783,14 +1256,7 @@
     x_prev = lax.ppermute(x, "ctx", [(i, i + 1) for i in range(count - 1)])
     gain1 = lax.all_gather(gain_one, "ctx", axis=0, tiled=True).astype(F32).reshape(1, width)
     gain2 = lax.all_gather(gain_two, "ctx", axis=0, tiled=True).astype(F32).reshape(1, width)
-    depths = lax.axis_size("dp")
-    blocks = (w_qkv.T, w_out.T, w_up, w_down.T)
-    along = (1, 1, 0, 1)
-    direct = count == FLIPS and all(b.shape[0] % 16 == 0 and b.shape[1] % 128 == 0 for b in blocks)
-    if direct:
-        wq, wo, wu, wd = gather_blocks(blocks, depths)
-    else:
-        wq, wo, wu, wd = (fetch(b, r) for b, r in zip(blocks, along))
+    wq, wo, wu, wd = (fetch(b, r) for b, r in zip(blocks, along))
     q, k, v, kp, vp, n, n_prev, own_sums = project(x, x_prev, wq, gain1, span)
     own_sums = own_sums.reshape(-1, 2 * width)
     n_sum = jnp.sum(n.reshape(-1, span, width).astype(F32), axis=1).astype(BF16)
@@ -806,11 +1272,7 @@
     gains = jnp.concatenate([jnp.sum(ggain1, axis=0), jnp.sum(ggain2, axis=0)]).reshape(2, width)
     gains = lax.psum(gains, "dp")
     gains = lax.psum_scatter(gains, "ctx", scatter_dimension=1, tiled=True)
-    partials = (gqkv, gout, gup, gdown)
-    if direct:
-        sums_w = scatter_blocks(partials, depths)
-    else:
-        sums_w = [reduce_weight(p, r) for p, r in zip(partials, along)]
+    sums_w = [reduce_weight(p, r) for p, r in zip((gqkv, gout, gup, gdown), along)]
     return (
         out.reshape(tokens.shape),
         input_grad.reshape(tokens.shape),

time: 345 us -> 221 us (0.64)
  blocking collectives: 46 us -> 0 us
  waiting for transfers between devices: 37.1 us -> 0 us
  between operations: 14.8 us -> 0.69 us
  local copies, waits for them, and re-layouts: 20.5 us -> 9.54 us
  Pallas kernels: 218 us -> 209 us
  starting transfers between devices: 3.9 us -> 0 us
    reduce_scatter x1 -> x0, waiting for transfers between devices: 37.1 us -> none  [shards(): gs_own = lax.psum_scatter(gs, 'ctx', scatter_dimension=1, tiled=True)]
    unnamed x1 -> x0, blocking collectives: 27.1 us -> none
    psum x1 -> x0, blocking collectives: 10.4 us -> none  [shards(): gains = lax.psum(gains, 'dp')]
    all_gather x1 -> x0, blocking collectives: 8.5 us -> none  [shards(): lax.all_gather(jnp.concatenate([own_sums, n_sum], axis=1), 'ctx', axis=0,...]
    pallas_call x6 -> x2, Pallas kernels: 174 us -> 166 us  [the longest x1 86.5 us: enter(): pl.pallas_call(functools.partial(enter_kernel, depths, span), in_specs=[v...]
    unnamed x17 -> x13, local copies, waits for them, and re-layouts: 13.3 us -> 5.72 us
    ppermute x2 -> x0, starting transfers between devices: 3.82 us -> none  [the longest x1 2.53 us: shards(): x_prev = lax.ppermute(x, 'ctx', [(i, i + 1) for i in range(count - 1)])]
  transfers between devices with their start and end apart: 4 -> 0, of which waited for: 1 -> 0; matrix products, arithmetic and copies ran while one was open for 2% -> 0% of each run, Pallas kernels for 25% -> 0%
where the time goes in v3:
time: 221 us
  Pallas kernels  209 us (95%)
  local copies, waits for them, and re-layouts  9.54 us (4%)
    pallas_call x1, Pallas kernels, enter(): pl.pallas_call(functools.partial(enter_kernel, depths, span), in_specs=[v...  86.5 us
    pallas_call x1, Pallas kernels, leave(): pl.pallas_call(functools.partial(leave_kernel, depths, span), in_specs=[f...  79.4 us
    pallas_call x1, Pallas kernels, feed(): pl.pallas_call(feed_kernel, grid=(rows // tile,), in_specs=[row_spec(tile...  43.4 us
    unnamed x13, local copies, waits for them, and re-layouts  5.72 us

profile of v3, /device:TPU:0, one launch (start us, length us, event | category | flops | bytes accessed | tf_op | source)
XLA Modules:
  0.0 220.8 jit_solution(2489893792096965913)
XLA Ops:
  0.6 1.3 reshape.52.prefix_ref
  1.9 0.7 maximum_convert_fusion
  2.6 0.1 tile.10
  2.7 0.6 compare_select_fusion.gain_ref
  3.3 86.5 %enter.1 = (bf16[4,8,192,128]{3,2,1,0:T(8,128)(2,1)}, bf16[4,8,64,128]{3,2,1,0:T(8,128)(2,1)}, bf16[4,8,128,256]{3,2,1,0:T(8,128)(2,1)}, bf16[4,8,64,512]{3,2,1,...) custom-call(bf16[2048,512]{1,0:T(8,128)(2,1)} %bitcast.16, ...), custom_call_target="tpu_custom_call" | custom-call | tf_op jit(solution)/shard_map/enter/pallas_call | solution.py:930
  89.8 1.3 slice.9.gain_ref
  91.0 43.4 %feed.1 = (bf16[2048,512]{1,0:T(8,128)(2,1)}, bf16[2048,512]{1,0:T(8,128)(2,1)}, f32[2048,512]{1,0:T(8,128)}, bf16[4,8,64,128]{3,2,1,0:T(8,128)(2,1)}, bf16[4,8,...) custom-call(bf16[2048,512]{1,0:T(8,128)(2,1)} %bitcast.17, ...), custom_call_target="tpu_custom_call" | custom-call | tf_op jit(solution)/shard_map/feed/pallas_call | solution.py:527
  134.4 79.4 %leave.1 = (bf16[2048,512]{1,0:T(8,128)(2,1)}, f32[192,128]{1,0:T(8,128)}, f32[64,128]{1,0:T(8,128)}, f32[128,256]{1,0:T(8,128)}, f32[64,512]{1,0:T(8,128)}, /*index=5*/f32[2,64]{1,0:T(2,128)}) custom-call(bf16[2048,512]{1,0:T(8,128)(2,1)} %get-tuple-element.43.q_in, bf16[2048,512]{1,0:T(8,128)(2,1)} %get-tuple-element.44.k_in, ...), custom_call_target="tpu_custom_call" | custom-call | tf_op jit(solution)/shard_map/leave/pallas_call | solution.py:1196
  213.8 1.2 slice_bitcast_fusion
  215.1 0.0 copy-start.2
  215.1 0.0 copy-start.3
  215.1 0.0 copy-start.1
  215.1 0.0 copy-start
  215.1 3.1 %copy.22 = bf16[2,8,128,512]{3,2,1,0:T(8,128)(2,1)} copy(bf16[2,8,128,512]{3,2,1,0:T(8,128)(2,1)} %bitcast.19) | data formatting | bytes 4194304
  218.2 0.0 copy-done.2
  218.2 0.6 copy.23
  218.9 0.0 copy-done.3
  218.9 0.6 copy.24
  219.5 0.0 copy-done.1
  219.5 0.7 copy.25
  220.1 0.0 copy-done
  220.1 0.7 copy.26
  (3 shorter events, 0.0 us)
Async XLA Ops:
  215.1 3.2 %copy-start.2 = (f32[192,128]{1,0:T(8,128)S(1)}, f32[192,128]{1,0:T(8,128)}, u32[]{:S(2)}) copy-start(f32[192,128]{1,0:T(8,128)} %get-tuple-element.61) | copy-start | bytes 294916
  215.1 3.8 %copy-start.3 = (f32[64,128]{1,0:T(8,128)S(1)}, f32[64,128]{1,0:T(8,128)}, u32[]{:S(2)}) copy-start(f32[64,128]{1,0:T(8,128)} %get-tuple-element.62) | copy-start | bytes 98308
  215.1 4.4 %copy-start.1 = (f32[128,256]{1,0:T(8,128)S(1)}, f32[128,256]{1,0:T(8,128)}, u32[]{:S(2)}) copy-start(f32[128,256]{1,0:T(8,128)} %get-tuple-element.82) | copy-start | bytes 393220
  215.1 5.1 %copy-start = (f32[64,512]{1,0:T(8,128)S(1)}, f32[64,512]{1,0:T(8,128)}, u32[]{:S(2)}) copy-start(f32[64,512]{1,0:T(8,128)} %get-tuple-element.64) | copy-start | bytes 393220

commit v4 on v3

--- a/solution.py
+++ b/solution.py
@@ -14,6 +14,7 @@
 F32 = jnp.float32
 BF16 = jnp.bfloat16
 TILE_SEQS = 2
+CHUNK_TILES = 2
 FF_CHUNK = 512
 VMEM_MOST = 60 * 1024 * 1024
 
@@ -477,7 +478,7 @@
         acc_down[...] = jnp.zeros_like(acc_down)
         acc_gain[...] = jnp.zeros_like(acc_gain)
 
-    gain = gain_ref[...]
+    gain = gain_ref[gain_ref.shape[0] - 1 :, :]
     mixed = mixed_ref[...]
     w_out = rows_of(wo_ref)
     resid = x_ref[...].astype(F32) + dot_t(mixed, w_out)
@@ -741,19 +742,18 @@
 
 
 ENTER_RELAYS = {
-    0: ((1, "spread"),),
-    1: ((2, "spread"), (3, "spread")),
-    2: ((1, "cross"),),
-    3: ((2, "cross"),),
-    4: ((1, "hand_over"), (3, "cross")),
-    5: ((2, "hand_over"),),
-    6: ((3, "hand_over"),),
+    0: ((1, "spread"), (2, "spread"), (3, "spread")),
+    3: ((1, "cross"),),
+    4: ((2, "cross"),),
+    5: ((3, "cross"),),
+    6: ((1, "hand_over"), (2, "hand_over")),
+    7: ((3, "hand_over"),),
 }
 
 
 def enter_kernel(
     depths, span,
-    x_ref, prefix_ref, bq_ref, bo_ref, bu_ref, bd_ref, gain_ref,
+    x_ref, prefix_ref, bq_ref, bo_ref, bu_ref, bd_ref, one_ref, two_ref,
     wq_out, wo_out, wu_out, wd_out, gain_out, q_out, k_out, v_out, kp_out, vp_out, n_out, np_out, mixed_out, prob_out,
     sums_out, psum_out,
     xp, wq, gains, q, k, v, kp, vp, n, n_prev, mixed, prob, slots,
@@ -762,6 +762,7 @@
     rows, width = x_ref.shape
     tile = TILE_SEQS * span
     tiles = rows // tile
+    chunks = tiles // CHUNK_TILES
     seqs = rows // span
     spot = lax.axis_index("ctx")
     scale = (width // HEADS) ** -0.5
@@ -771,25 +772,19 @@
     ]
     gain_share = Share(depths, gains, gain_send, gain_recv)
     sum_share = Share(depths, slots, sum_send, sum_recv)
-    gains[spot] = gain_ref[...]
+    shard = jnp.concatenate([one_ref[...].reshape(1, -1), two_ref[...].reshape(1, -1)], axis=0).astype(F32)
+    owner = lax.broadcasted_iota(jnp.int32, (2, width), 1) // shard.shape[1]
+    gains[spot] = jnp.where(owner == spot, jnp.concatenate([shard] * FLIPS, axis=1), 0.0)
 
     @pl.when(spot == 0)
     def _():
         xp[...] = jnp.zeros_like(xp)
 
-    greet(depths)
-    gathers[0].begin()
-    gain_share.begin()
-    gathers[0].spread()
-    gain_share.forward()
-    gain_share.complete()
-    gain = gains[0]
-    for c in range(1, FLIPS):
-        gain = gain + gains[c]
-    gain_out[...] = gain
-
     def at(i):
         return pl.ds(pl.multiple_of(i * tile, tile), tile)
+
+    def chunk_at(c):
+        return pl.ds(pl.multiple_of(c * CHUNK_TILES * tile, CHUNK_TILES * tile), CHUNK_TILES * tile)
 
     def token_copy(i):
         return pltpu.make_async_remote_copy(
@@ -809,65 +804,96 @@
         part = pl.ds(i * TILE_SEQS, TILE_SEQS)
         return pltpu.make_async_copy(prob.at[part], prob_out.at[part], prob_sem.at[i])
 
-    @pl.loop(0, tiles)
-    def _(i):
-        n[at(i), :] = (standardize(x_ref[at(i), :].astype(F32))[0] * gain[0:1]).astype(BF16)
-
-    gathers[0].cross()
-    gathers[0].hand_over()
-
-    @pl.when(spot < FLIPS - 1)
-    def _():
-        for i in range(tiles):
-            token_copy(i).start()
-
-    for gather in gathers[1:]:
-        gather.begin()
-    gathers[0].complete()
-    wq_copy = pltpu.make_async_copy(wq, wq_out, wq_sem.at[0])
-    wq_copy.start()
-
-    @pl.loop(0, tiles)
-    def _(i):
-        weight = rows_of(wq)
-        normed = n[at(i), :]
-        q[at(i), :] = (dot_t(normed, weight[:width]).astype(BF16).astype(F32) * scale).astype(BF16)
-        k[at(i), :] = dot_t(normed, weight[width : 2 * width]).astype(BF16)
-        v[at(i), :] = dot_t(normed, weight[2 * width :]).astype(BF16)
-        for a in range(4):
-            out_copy(a, i).start()
-
-    for part, (ref, weigh) in enumerate(((k, 1.0 / span), (v, 1.0 / span), (n, 1.0))):
+    def send_tokens(first, last):
+        @pl.when(spot < FLIPS - 1)
+        def _():
+            for i in range(first, last):
+                token_copy(i).start()
+
+    greet(depths)
+    gathers[0].begin()
+    gain_share.begin()
+    send_tokens(0, 2)
+    gain_share.forward()
+    gain_share.complete()
+    gain = gains[0]
+    for c in range(1, FLIPS):
+        gain = gain + gains[c]
+    gain_out[...] = gain
+
+    def normalize(c):
+        n[chunk_at(c), :] = (standardize(x_ref[chunk_at(c), :].astype(F32))[0] * gain[0:1]).astype(BF16)
+
+    def keep_mean(part, ref, weigh):
         means = [
             jnp.sum(ref[s * span : (s + 1) * span, :].astype(F32), axis=0, keepdims=True) * weigh for s in range(seqs)
         ]
         slots[spot, :, part * width : (part + 1) * width] = jnp.concatenate(means, axis=0).astype(BF16)
+
+    pl.loop(0, chunks // 2)(normalize)
+    gathers[0].spread()
+    pl.loop(chunks // 2, chunks)(normalize)
+    gathers[0].cross()
+    keep_mean(2, n, 1.0)
+    gathers[0].hand_over()
+    for gather in gathers[1:]:
+        gather.begin()
+    send_tokens(2, 5)
+    gathers[0].complete()
+    wq_copy = pltpu.make_async_copy(wq, wq_out, wq_sem.at[0])
+    wq_copy.start()
+
+    def send_out(a, c):
+        for t in range(CHUNK_TILES):
+            out_copy(a, c * CHUNK_TILES + t).start()
+
+    @pl.loop(0, chunks)
+    def _(c):
+        weight = rows_of(wq)
+        normed = n[chunk_at(c), :]
+        k[chunk_at(c), :] = dot_t(normed, weight[width : 2 * width]).astype(BF16)
+        v[chunk_at(c), :] = dot_t(normed, weight[2 * width :]).astype(BF16)
+        for a in (1, 2, 3):
+            send_out(a, c)
+
+    keep_mean(0, k, 1.0 / span)
+    keep_mean(1, v, 1.0 / span)
     sum_share.begin()
-
-    def project_prev(i):
+    send_tokens(5, tiles)
+
+    @pl.loop(0, chunks)
+    def _(c):
+        weight = rows_of(wq)
+        rows_q = dot_t(n[chunk_at(c), :], weight[:width]).astype(BF16)
+        q[chunk_at(c), :] = (rows_q.astype(F32) * scale).astype(BF16)
+        send_out(0, c)
+
+    sum_share.forward()
+
+    def project_prev(c):
         @pl.when(spot > 0)
         def _():
-            token_copy(i).wait_recv()
+            for t in range(CHUNK_TILES):
+                token_copy(c * CHUNK_TILES + t).wait_recv()
 
         weight = rows_of(wq)
-        normed = (standardize(xp[at(i), :].astype(F32))[0] * gain[0:1]).astype(BF16)
-        n_prev[at(i), :] = normed
-        kp[at(i), :] = dot_t(normed, weight[width : 2 * width]).astype(BF16)
-        vp[at(i), :] = dot_t(normed, weight[2 * width :]).astype(BF16)
-        for a in range(4, 7):
-            out_copy(a, i).start()
-
-    project_prev(0)
-    sum_share.forward()
+        normed = (standardize(xp[chunk_at(c), :].astype(F32))[0] * gain[0:1]).astype(BF16)
+        n_prev[chunk_at(c), :] = normed
+        kp[chunk_at(c), :] = dot_t(normed, weight[width : 2 * width]).astype(BF16)
+        vp[chunk_at(c), :] = dot_t(normed, weight[2 * width :]).astype(BF16)
+        for a in (4, 5, 6):
+            send_out(a, c)
+
+    pl.loop(0, 2)(project_prev)
     sum_share.complete()
     ordered = dot(in_order(FLIPS, seqs), slots[...].reshape(FLIPS * seqs, 3 * width)).astype(BF16)
     sums_out[...] = ordered.reshape(sums_out.shape)
 
     @pl.loop(0, tiles)
     def _(i):
-        @pl.when(i + 1 < tiles)
+        @pl.when((lax.rem(i, CHUNK_TILES) == 0) & (i >= 2 * CHUNK_TILES))
         def _():
-            project_prev(i + 1)
+            project_prev(i // CHUNK_TILES)
 
         for s in range(TILE_SEQS):
             here = pl.ds(pl.multiple_of(i * tile + s * span, span), span)
@@ -879,7 +905,7 @@
             rows_mixed, all_sums = attend_one(
                 span,
                 spot,
-                prefix_ref[seq],
+                prefix_ref[seq // prefix_ref.shape[1], lax.rem(seq, prefix_ref.shape[1])],
                 q[here, :],
                 jnp.concatenate([kp[here, :], k[here, :]], axis=0),
                 jnp.concatenate([vp[here, :], v[here, :]], axis=0),
@@ -916,7 +942,7 @@
         prob_copy(i).wait()
 
 
-def enter(x, prefix, blocks, gains, span, depths):
+def enter(x, prefix, blocks, gain_one, gain_two, span, depths):
     rows, width = x.shape
     tile = TILE_SEQS * span
     tiles, seqs = rows // tile, rows // span
@@ -929,10 +955,10 @@
     held = pltpu.VMEM((rows, width), BF16)
     return pl.pallas_call(
         functools.partial(enter_kernel, depths, span),
-        in_specs=[vmem, pl.BlockSpec(memory_space=pltpu.SMEM)] + [vmem] * 5,
+        in_specs=[vmem, pl.BlockSpec(memory_space=pltpu.SMEM)] + [vmem] * 6,
         out_specs=[far] * 4 + [vmem] + [far] * 9 + [vmem] * 2,
         out_shape=fulls
-        + [jax.ShapeDtypeStruct(gains.shape, F32)]
+        + [jax.ShapeDtypeStruct((2, width), F32)]
         + [low] * 8
         + [
             jax.ShapeDtypeStruct(prob_shape, BF16),
@@ -942,7 +968,7 @@
         scratch_shapes=[
             held,
             pltpu.VMEM(fulls[0].shape, BF16),
-            pltpu.VMEM((FLIPS,) + gains.shape, F32),
+            pltpu.VMEM((FLIPS, 2, width), F32),
         ]
         + [held] * 8
         + [pltpu.VMEM(prob_shape, BF16), pltpu.VMEM((FLIPS, seqs, 3 * width), BF16)]
@@ -953,7 +979,7 @@
         ],
         compiler_params=pltpu.CompilerParams(collective_id=0, has_side_effects=True, vmem_limit_bytes=VMEM_MOST),
         name="enter",
-    )(x, prefix, *blocks, gains)
+    )(x, prefix, *blocks, gain_one, gain_two)
 
 
 LEAVE_RELAYS = {
@@ -1209,13 +1235,10 @@
     depths = lax.axis_size("dp")
     x = tokens.reshape(-1, width)
     grad = cotangent.reshape(-1, width)
-    shard = jnp.stack([gain_one, gain_two]).astype(F32)
-    lane_owner = lax.broadcasted_iota(jnp.int32, (2, width), 1) // shard.shape[1]
-    gains = jnp.where(lane_owner == lax.axis_index("ctx"), jnp.tile(shard, (1, FLIPS)), 0.0)
     (wq, wo, wu, wd, gains, q, k, v, kp, vp, n, n_prev, mixed, prob, sums, psum) = enter(
-        x, prefix.reshape(-1), blocks, gains, span, depths
+        x, prefix, blocks, gain_one, gain_two, span, depths
     )
-    out, gm, gr, gout, gup, gdown, ggain = feed(x, mixed, grad, wo, wu, wd, gains[1:2], TILE_SEQS * span)
+    out, gm, gr, gout, gup, gdown, ggain = feed(x, mixed, grad, wo, wu, wd, gains, TILE_SEQS * span)
     arrays = (q, k, v, kp, vp, gm, n, n_prev, prob, gr, x)
     ig, dqkv, dout, dup, ddown, dgain = leave(arrays, psum, sums, wq, (gout, gup, gdown), gains, ggain, span, depths)
     return (

time: 221 us -> 207 us (0.937)
  Pallas kernels: 209 us -> 199 us
  local copies, waits for them, and re-layouts: 9.54 us -> 6.94 us
    pallas_call x1, Pallas kernels: 86.5 us -> 72.9 us  [enter(): pl.pallas_call(functools.partial(enter_kernel, depths, span), in_specs=[v...]
    pallas_call x1, Pallas kernels: 79.4 us -> 83.2 us  [leave(): pl.pallas_call(functools.partial(leave_kernel, depths, span), in_specs=[f...]
where the time goes in v4:
time: 207 us
  Pallas kernels  199 us (96%)
  local copies, waits for them, and re-layouts  6.94 us (3%)
    pallas_call x1, Pallas kernels, leave(): pl.pallas_call(functools.partial(leave_kernel, depths, span), in_specs=[f...  83.2 us
    pallas_call x1, Pallas kernels, enter(): pl.pallas_call(functools.partial(enter_kernel, depths, span), in_specs=[v...  72.9 us
    pallas_call x1, Pallas kernels, feed(): pl.pallas_call(feed_kernel, grid=(rows // tile,), in_specs=[row_spec(tile...  43.4 us
    unnamed x13, local copies, waits for them, and re-layouts  5.72 us

profile of v4, /device:TPU:0, one launch (start us, length us, event | category | flops | bytes accessed | tf_op | source)
XLA Modules:
  0.0 207.0 jit_solution(15907437474627673523)
XLA Ops:
  0.6 72.9 %enter.1 = (bf16[4,8,192,128]{3,2,1,0:T(8,128)(2,1)}, bf16[4,8,64,128]{3,2,1,0:T(8,128)(2,1)}, bf16[4,8,128,256]{3,2,1,0:T(8,128)(2,1)}, bf16[4,8,64,512]{3,2,1,...) custom-call(bf16[2048,512]{1,0:T(8,128)(2,1)} %bitcast.14, ...), custom_call_target="tpu_custom_call" | custom-call | tf_op jit(solution)/shard_map/enter/pallas_call | solution.py:956
  73.5 43.4 %feed.1 = (bf16[2048,512]{1,0:T(8,128)(2,1)}, bf16[2048,512]{1,0:T(8,128)(2,1)}, f32[2048,512]{1,0:T(8,128)}, bf16[4,8,64,128]{3,2,1,0:T(8,128)(2,1)}, bf16[4,8,...) custom-call(bf16[2048,512]{1,0:T(8,128)(2,1)} %bitcast.15, ...), custom_call_target="tpu_custom_call" | custom-call | tf_op jit(solution)/shard_map/feed/pallas_call | solution.py:528
  116.9 83.2 %leave.1 = (bf16[2048,512]{1,0:T(8,128)(2,1)}, f32[192,128]{1,0:T(8,128)}, f32[64,128]{1,0:T(8,128)}, f32[128,256]{1,0:T(8,128)}, f32[64,512]{1,0:T(8,128)}, /*index=5*/f32[2,64]{1,0:T(2,128)}) custom-call(bf16[2048,512]{1,0:T(8,128)(2,1)} %get-tuple-element.43.q_in, bf16[2048,512]{1,0:T(8,128)(2,1)} %get-tuple-element.44.k_in, ...), custom_call_target="tpu_custom_call" | custom-call | tf_op jit(solution)/shard_map/leave/pallas_call | solution.py:1222
  200.1 1.2 slice_bitcast_fusion
  201.3 0.0 copy-start.2
  201.3 0.0 copy-start.3
  201.3 0.0 copy-start.1
  201.3 0.0 copy-start
  201.3 3.1 %copy.22 = bf16[2,8,128,512]{3,2,1,0:T(8,128)(2,1)} copy(bf16[2,8,128,512]{3,2,1,0:T(8,128)(2,1)} %bitcast.18) | data formatting | bytes 4194304
  204.5 0.0 copy-done.2
  204.5 0.6 copy.23
  205.1 0.0 copy-done.3
  205.1 0.6 copy.24
  205.7 0.0 copy-done.1
  205.7 0.7 copy.25
  206.4 0.0 copy-done
  206.4 0.7 copy.26
Async XLA Ops:
  201.3 3.2 %copy-start.2 = (f32[192,128]{1,0:T(8,128)S(1)}, f32[192,128]{1,0:T(8,128)}, u32[]{:S(2)}) copy-start(f32[192,128]{1,0:T(8,128)} %get-tuple-element.61) | copy-start | bytes 294916
  201.3 3.8 %copy-start.3 = (f32[64,128]{1,0:T(8,128)S(1)}, f32[64,128]{1,0:T(8,128)}, u32[]{:S(2)}) copy-start(f32[64,128]{1,0:T(8,128)} %get-tuple-element.62) | copy-start | bytes 98308
  201.3 4.4 %copy-start.1 = (f32[128,256]{1,0:T(8,128)S(1)}, f32[128,256]{1,0:T(8,128)}, u32[]{:S(2)}) copy-start(f32[128,256]{1,0:T(8,128)} %get-tuple-element.80) | copy-start | bytes 393220
  201.3 5.1 %copy-start = (f32[64,512]{1,0:T(8,128)S(1)}, f32[64,512]{1,0:T(8,128)}, u32[]{:S(2)}) copy-start(f32[64,512]{1,0:T(8,128)} %get-tuple-element.64) | copy-start | bytes 393220

commit v5 on v4

--- a/solution.py
+++ b/solution.py
@@ -15,7 +15,7 @@
 BF16 = jnp.bfloat16
 TILE_SEQS = 2
 CHUNK_TILES = 2
-FF_CHUNK = 512
+FF_CHUNK = 1024
 VMEM_MOST = 60 * 1024 * 1024
 
 MESH = pl.DeviceIdType.MESH
@@ -164,9 +164,9 @@
     push = Moves.start
     arrive = Moves.landed
 
-    def begin(self):
+    def begin(self, turns):
         for flip in (6, 2, 4, 0):
-            for turn in range(self.depths):
+            for turn in turns:
                 at = (flip // 2, turn)
                 self.push(self.block(turn, flip ^ 1), self.mate.at[at], flip // 2 * self.depths + turn, 0, 1)
 
@@ -175,17 +175,17 @@
         mine = self.block(turn, flip)[...].astype(F32)
         self.total[flip // 2, turn] = (mine + self.mate[flip // 2, turn].astype(F32)).astype(BF16)
 
-    def cross(self):
+    def cross(self, turns):
         base = 4 * self.depths
-        for turn in range(self.depths):
+        for turn in turns:
             self.fold(turn, 6)
             by = 2 if turn < self.depths // 2 else 4
             self.push(self.total.at[3, turn], self.near.at[turn], base + turn, 0, by)
 
-    def spread(self):
+    def spread(self, turns):
         base = 4 * self.depths
         late = 5 * self.depths
-        for turn in range(self.depths):
+        for turn in turns:
             self.fold(turn, 2)
             self.fold(turn, 4)
             via = 2 if turn < self.depths // 2 else 1
@@ -194,10 +194,10 @@
             self.push(self.total.at[1, turn], self.far.at[0, turn], late + turn, 0, 2)
             self.push(self.total.at[2, turn], self.far.at[1, turn], late + self.depths + turn, 0, 4)
 
-    def climb(self):
+    def climb(self, turns):
         late = 5 * self.depths
         last = 7 * self.depths
-        for turn in [*range(1, self.depths), 0]:
+        for turn in turns:
             self.fold(turn, 0)
             self.arrive(self.far.at[0, turn], late + turn)
             self.arrive(self.far.at[1, turn], late + self.depths + turn)
@@ -615,7 +615,7 @@
     acc[:, width:] += (
         dot(normed_t, grad_own[:, width:]) + dot(normed_prev.T, grad_before) + dot(normed_sum.T, grad_shared)
     )
-    return dot(grad_own, weight), dot(grad_before, weight[width:]), dot(grad_shared, weight[width:])
+    return grad_own, dot(grad_before, weight[width:]), dot(grad_shared, weight[width:])
 
 
 def return_kernel(
@@ -644,8 +644,9 @@
             )
         )
     normed_sum = nsum_ref[...].reshape(-1, nsum_ref.shape[2])
-    gn, gp, gs = return_tile(rows_of(w_ref), *zip(*parts), n_ref[...], np_ref[...], normed_sum, acc)
-    gn_ref[...] = gn
+    weight = rows_of(w_ref)
+    grad_own, gp, gs = return_tile(weight, *zip(*parts), n_ref[...], np_ref[...], normed_sum, acc)
+    gn_ref[...] = dot(grad_own, weight)
     gp_ref[...] = gp.astype(BF16)
     gs_ref[...] = gs.reshape(gs_ref.shape).astype(BF16)
 
@@ -742,12 +743,10 @@
 
 
 ENTER_RELAYS = {
-    0: ((1, "spread"), (2, "spread"), (3, "spread")),
-    3: ((1, "cross"),),
-    4: ((2, "cross"),),
+    1: ((1, "spread"), (2, "spread"), (3, "spread")),
+    4: ((1, "cross"), (2, "cross")),
     5: ((3, "cross"),),
-    6: ((1, "hand_over"), (2, "hand_over")),
-    7: ((3, "hand_over"),),
+    7: ((1, "hand_over"), (2, "hand_over"), (3, "hand_over")),
 }
 
 
@@ -836,8 +835,6 @@
     gathers[0].cross()
     keep_mean(2, n, 1.0)
     gathers[0].hand_over()
-    for gather in gathers[1:]:
-        gather.begin()
     send_tokens(2, 5)
     gathers[0].complete()
     wq_copy = pltpu.make_async_copy(wq, wq_out, wq_sem.at[0])
@@ -860,6 +857,8 @@
     keep_mean(1, v, 1.0 / span)
     sum_share.begin()
     send_tokens(5, tiles)
+    for gather in gathers[1:]:
+        gather.begin()
 
     @pl.loop(0, chunks)
     def _(c):
@@ -983,12 +982,12 @@
 
 
 LEAVE_RELAYS = {
-    1: ((0, "cross"),),
-    2: ((1, "cross"), (0, "spread")),
-    3: ((2, "cross"), (0, "climb")),
-    4: ((1, "spread"),),
-    5: ((2, "spread"), (1, "climb")),
-    6: ((2, "climb"),),
+    1: ((0, "cross"), (1, "cross")),
+    2: ((2, "cross"),),
+    3: ((0, "spread"), (1, "spread")),
+    4: ((2, "spread"),),
+    6: ((0, "climb"), (1, "climb")),
+    7: ((2, "climb"),),
 }
 
 
@@ -997,17 +996,16 @@
     q_in, k_in, v_in, kp_in, vp_in, gm_in, n_in, np_in, prob_in, gr_in, x_in,
     psum_ref, sums_ref, wq_ref, gout_ref, gup_ref, gdown_ref, gain_ref, ggain_ref,
     ig_out, dqkv_out, dout_out, dup_out, ddown_out, dgain_out,
-    held, prob, gn, gp, gb, gr, x, ig, acc, part, gs, gs_send_buf, gs_slots, gain_slots, gain_deep,
+    held, prob, kept, before, shared_rows, turned, turned_prev, turned_sum, one_sum, gp, gb, gr, x, ig, part, gs_send_buf, gs_slots, gain_slots, gain_deep,
     *rest,
 ):
     moves_refs, sems = rest[:16], rest[16:]
     send, recv, gs_send, gs_recv, gain_send, gain_recv, deep_send, deep_recv, gb_send, gb_recv, in_sem, late_sem, ig_sem = sems
-    rows, width = gn.shape
+    rows, width = gp.shape
     tile = TILE_SEQS * span
     tiles = rows // tile
     seqs = rows // span
     spot = lax.axis_index("ctx")
-    depth = lax.axis_index("dp")
     parts = (gout_ref, gup_ref, gdown_ref, part)
     scatters = [
         Scatter(depths, parts[a], *moves_refs[4 * a : 4 * a + 4], send.at[a], recv.at[a]) for a in range(4)
@@ -1018,6 +1016,9 @@
 
     def at(i):
         return pl.ds(pl.multiple_of(i * tile, tile), tile)
+
+    def at_sums(i):
+        return pl.ds(pl.multiple_of(i * TILE_SEQS * FLIPS, TILE_SEQS * FLIPS), TILE_SEQS * FLIPS)
 
     def loads(i, slot):
         arrays = (q_in, k_in, v_in, kp_in, vp_in, gm_in, n_in, np_in)
@@ -1044,11 +1045,12 @@
         gb[...] = jnp.zeros_like(gb)
 
     greet(depths)
+    turns = (*range(1, depths), 0)
     for scatter in scatters[:3]:
-        scatter.begin()
-    acc[...] = jnp.zeros_like(acc)
-
-    def tile_step(i, gain_sum):
+        scatter.begin(turns)
+
+    @pl.loop(0, tiles)
+    def _(i):
         slot = lax.rem(i, 2)
         for copy in loads(i, slot):
             copy.wait()
@@ -1074,13 +1076,14 @@
                     psum_ref[seq],
                 )
             )
-        of_tile = pl.ds(i * TILE_SEQS, TILE_SEQS)
-        normed, normed_prev = held[slot, 6], held[slot, 7]
-        normed_sum = sums_ref[of_tile, :, 2 * width :].reshape(-1, width)
-        to_own, to_prev, to_sums = return_tile(rows_of(wq_ref), *zip(*pieces), normed, normed_prev, normed_sum, acc)
-        gn[at(i), :] = to_own
-        gp[at(i), :] = to_prev.astype(BF16)
-        gs[i] = to_sums.astype(BF16)
+        own, back, shared = (jnp.concatenate(rows, axis=0) for rows in zip(*pieces))
+        weight_kv = rows_of(wq_ref)[width:]
+        kept[at(i), :] = own
+        before[at(i), :] = back
+        gp[at(i), :] = dot(back, weight_kv).astype(BF16)
+        shared_rows[at_sums(i), :] = shared.astype(BF16)
+        turned[:, at(i)] = held[slot, 6].T
+        turned_prev[:, at(i)] = held[slot, 7].T
 
         @pl.when(spot > 0)
         def _():
@@ -1091,39 +1094,48 @@
             @pl.when(i == when)
             def _(relays=relays):
                 for a, name in relays:
-                    getattr(scatters[a], name)()
+                    getattr(scatters[a], name)(turns)
 
         @pl.when(i == tiles - 3)
         def _():
             for copy in late:
                 copy.start()
 
-        return (
-            gain_sum
-            + fold_rows(to_own * normed.astype(F32))
-            + fold_rows(to_prev * normed_prev.astype(F32))
-            + fold_rows(to_sums * normed_sum.astype(F32))
-        )
-
-    gain_sum = lax.fori_loop(0, tiles, tile_step, jnp.zeros((8, width), F32))
-
+    to_sums = dot(shared_rows[...], rows_of(wq_ref)[width:]).astype(BF16)
     by_spot = lax.dot_general(
-        in_order(FLIPS, seqs), gs[...].reshape(seqs * FLIPS, width), (((0,), (0,)), ((), ())), preferred_element_type=F32
+        in_order(FLIPS, seqs), to_sums, (((0,), (0,)), ((), ())), preferred_element_type=F32
     )
     gs_send_buf[...] = by_spot.astype(BF16).reshape(gs_send_buf.shape)
     for flip in (6, 7, 2, 4, 3, 5, 1):
         gs_moves.start(gs_send_buf.at[spot_of(depths, 0, flip)[1]], gs_slots.at[flip], flip, 0, flip)
-    total_one = jnp.sum(gain_sum, axis=0, keepdims=True) / gain_ref[0:1]
+    turned_sum[...] = sums_ref[:, :, 2 * width :].reshape(seqs * FLIPS, width).T
+    lanes_in = width // depths
+
+    def weigh(turns):
+        owners = [spot_of(depths, turn, 0)[0] for turn in turns]
+        tops = [pl.ds(pl.multiple_of(owner * lanes_in, lanes_in), lanes_in) for owner in owners]
+        rows_own, rows_prev, rows_sum = (
+            jnp.concatenate([ref[top, :] for top in tops], axis=0) for ref in (turned, turned_prev, turned_sum)
+        )
+        grad_q = dot(rows_own, kept[:, :width])
+        grad_kv = dot(rows_own, kept[:, width:]) + dot(rows_prev, before[...]) + dot(rows_sum, shared_rows[...])
+        low = jnp.concatenate([grad_q.astype(BF16), grad_kv.astype(BF16)], axis=1)
+        for t, (owner, top) in enumerate(zip(owners, tops)):
+            flat = low[t * lanes_in : (t + 1) * lanes_in].T
+            part[owner] = flat.reshape(part.shape[1:])
+            weighed = flat.astype(F32) * wq_ref[owner].reshape(flat.shape).astype(F32)
+            one_sum[:, top] = jnp.sum(weighed, axis=0, keepdims=True)
+        scatters[3].begin(turns)
+
+    first, second = turns[: depths // 2], turns[depths // 2 :]
+    weigh(first)
+    weigh(second)
+    scatters[3].cross(first)
+    total_one = one_sum[...] / gain_ref[0:1]
     total_two = jnp.sum(ggain_ref[...], axis=0, keepdims=True)
     gain_slots[spot] = jnp.concatenate([total_one, total_two], axis=0)
     gain_share.begin()
-    put_blocks(part, acc[...].astype(BF16).T, 1)
-    scatters[3].begin()
-    dout_out[...] = scatters[0].finish()
     gain_share.forward()
-    scatters[3].cross()
-    dup_out[...] = scatters[1].finish()
-    ddown_out[...] = scatters[2].finish()
     for copy in late:
         copy.wait()
     for flip in range(1, FLIPS):
@@ -1139,7 +1151,7 @@
             gb_copy(i).wait_recv()
 
         unit, inv = standardize(x[at(i), :].astype(F32))
-        grad_norm = gn[at(i), :] + gb[at(i), :].astype(F32)
+        grad_norm = dot(kept[at(i), :], rows_of(wq_ref)) + gb[at(i), :].astype(F32)
         lifted = [
             grad_norm[s * span : (s + 1) * span] + shared[i * TILE_SEQS + s : i * TILE_SEQS + s + 1]
             for s in range(TILE_SEQS)
@@ -1148,21 +1160,24 @@
         ig[at(i), :] = (gr[at(i), :] + norm_back(grad_norm, unit, inv, gain)).astype(BF16)
         pltpu.make_async_copy(ig.at[at(i)], ig_out.at[at(i)], ig_sem.at[i]).start()
 
-    cut = tiles // 3
-    for i in range(cut):
-        close_tile(i)
-    scatters[3].spread()
-    gain_share.complete()
-    over_ctx = gain_slots[0]
-    for c in range(1, FLIPS):
-        over_ctx = over_ctx + gain_slots[c]
-    gain_deep[0] = over_ctx
-    for turn in range(1, depths):
-        deep_moves.start(gain_deep.at[0], gain_deep.at[depths - turn], depths - turn, turn, 0)
-    for i in range(cut, 2 * cut):
-        close_tile(i)
-    scatters[3].climb()
-    for i in range(2 * cut, tiles):
+    def share_deep():
+        gain_share.complete()
+        over_ctx = gain_slots[0]
+        for c in range(1, FLIPS):
+            over_ctx = over_ctx + gain_slots[c]
+        gain_deep[0] = over_ctx
+        for turn in range(1, depths):
+            deep_moves.start(gain_deep.at[0], gain_deep.at[depths - turn], depths - turn, turn, 0)
+
+    after = {
+        1: (functools.partial(scatters[3].cross, second), functools.partial(scatters[3].spread, first)),
+        2: (share_deep, functools.partial(scatters[3].spread, second)),
+        4: (functools.partial(scatters[3].climb, first),),
+        6: (functools.partial(scatters[3].climb, second),),
+    }
+    for i in range(tiles):
+        for relay in after.get(i, ()):
+            relay()
         close_tile(i)
     for turn in range(1, depths):
         deep_moves.landed(gain_deep.at[turn], turn)
@@ -1174,7 +1189,8 @@
     for c in range(FLIPS):
         mine = jnp.where(spot == c, over_all[:, c * lanes : (c + 1) * lanes], mine)
     dgain_out[...] = mine
-    dqkv_out[...] = scatters[3].finish()
+    for out, scatter in zip((dout_out, dup_out, ddown_out, dqkv_out), scatters):
+        out[...] = scatter.finish()
     for scatter in scatters:
         scatter.close()
     gain_share.close()
@@ -1203,10 +1219,15 @@
     scratch = [
         pltpu.VMEM((2, 8, tile, width), BF16),
         pltpu.VMEM((2, TILE_SEQS, HEADS // 2, 2 * span, 2 * span), BF16),
-        high, low, low, high, low, low,
-        pltpu.VMEM((width, 3 * width), F32),
+        pltpu.VMEM((rows, 3 * width), BF16),
+        pltpu.VMEM((rows, 2 * width), BF16),
+        pltpu.VMEM((seqs * FLIPS, 2 * width), BF16),
+        pltpu.VMEM((width, rows), BF16),
+        pltpu.VMEM((width, rows), BF16),
+        pltpu.VMEM((width, seqs * FLIPS), BF16),
+        pltpu.VMEM((1, width), F32),
+        low, low, high, low, low,
         pltpu.VMEM(wq.shape, BF16),
-        pltpu.VMEM((tiles, TILE_SEQS * FLIPS, width), BF16),
         pltpu.VMEM((FLIPS, seqs, width), BF16),
         pltpu.VMEM((FLIPS, seqs, width), BF16),
         pltpu.VMEM((FLIPS, 2, width), F32),
@@ -1238,7 +1259,7 @@
     (wq, wo, wu, wd, gains, q, k, v, kp, vp, n, n_prev, mixed, prob, sums, psum) = enter(
         x, prefix, blocks, gain_one, gain_two, span, depths
     )
-    out, gm, gr, gout, gup, gdown, ggain = feed(x, mixed, grad, wo, wu, wd, gains, TILE_SEQS * span)
+    out, gm, gr, gout, gup, gdown, ggain = feed(x, mixed, grad, wo, wu, wd, gains, 2 * TILE_SEQS * span)
     arrays = (q, k, v, kp, vp, gm, n, n_prev, prob, gr, x)
     ig, dqkv, dout, dup, ddown, dgain = leave(arrays, psum, sums, wq, (gout, gup, gdown), gains, ggain, span, depths)
     return (

time: 207 us -> 194 us (0.937)
  Pallas kernels: 199 us -> 186 us
    pallas_call x1, Pallas kernels: 83.2 us -> 73.4 us  [leave(): pl.pallas_call(functools.partial(leave_kernel, depths, span), in_specs=[f...]
    pallas_call x1, Pallas kernels: 43.4 us -> 41.1 us  [feed(): pl.pallas_call(feed_kernel, grid=(rows // tile,), in_specs=[row_spec(tile...]
where the time goes in v5:
time: 194 us
  Pallas kernels  186 us (96%)
  local copies, waits for them, and re-layouts  6.94 us (4%)
    pallas_call x1, Pallas kernels, leave(): pl.pallas_call(functools.partial(leave_kernel, depths, span), in_specs=[f...  73.4 us
    pallas_call x1, Pallas kernels, enter(): pl.pallas_call(functools.partial(enter_kernel, depths, span), in_specs=[v...  71.8 us
    pallas_call x1, Pallas kernels, feed(): pl.pallas_call(feed_kernel, grid=(rows // tile,), in_specs=[row_spec(tile...  41.1 us
    unnamed x13, local copies, waits for them, and re-layouts  5.72 us

profile of v5, /device:TPU:0, one launch (start us, length us, event | category | flops | bytes accessed | tf_op | source)
XLA Modules:
  0.0 193.9 jit_solution(9604100058604032023)
XLA Ops:
  0.6 71.8 %enter.1 = (bf16[4,8,192,128]{3,2,1,0:T(8,128)(2,1)}, bf16[4,8,64,128]{3,2,1,0:T(8,128)(2,1)}, bf16[4,8,128,256]{3,2,1,0:T(8,128)(2,1)}, bf16[4,8,64,512]{3,2,1,...) custom-call(bf16[2048,512]{1,0:T(8,128)(2,1)} %bitcast.14, ...), custom_call_target="tpu_custom_call" | custom-call | tf_op jit(solution)/shard_map/enter/pallas_call | solution.py:955
  72.4 41.1 %feed.1 = (bf16[2048,512]{1,0:T(8,128)(2,1)}, bf16[2048,512]{1,0:T(8,128)(2,1)}, f32[2048,512]{1,0:T(8,128)}, bf16[4,8,64,128]{3,2,1,0:T(8,128)(2,1)}, bf16[4,8,...) custom-call(bf16[2048,512]{1,0:T(8,128)(2,1)} %bitcast.15, ...), custom_call_target="tpu_custom_call" | custom-call | tf_op jit(solution)/shard_map/feed/pallas_call | solution.py:528
  113.5 73.4 %leave.1 = (bf16[2048,512]{1,0:T(8,128)(2,1)}, f32[192,128]{1,0:T(8,128)}, f32[64,128]{1,0:T(8,128)}, f32[128,256]{1,0:T(8,128)}, f32[64,512]{1,0:T(8,128)}, /*index=5*/f32[2,64]{1,0:T(2,128)}) custom-call(bf16[2048,512]{1,0:T(8,128)(2,1)} %get-tuple-element.43.q_in, bf16[2048,512]{1,0:T(8,128)(2,1)} %get-tuple-element.44.k_in, ...), custom_call_target="tpu_custom_call" | custom-call | tf_op jit(solution)/shard_map/leave/pallas_call | solution.py:1243
  186.9 1.2 slice_bitcast_fusion
  188.2 0.0 copy-start.2
  188.2 0.0 copy-start.3
  188.2 0.0 copy-start.1
  188.2 0.0 copy-start
  188.2 3.1 %copy.22 = bf16[2,8,128,512]{3,2,1,0:T(8,128)(2,1)} copy(bf16[2,8,128,512]{3,2,1,0:T(8,128)(2,1)} %bitcast.18) | data formatting | bytes 4194304
  191.3 0.0 copy-done.2
  191.3 0.6 copy.23
  192.0 0.0 copy-done.3
  192.0 0.6 copy.24
  192.6 0.0 copy-done.1
  192.6 0.7 copy.25
  193.3 0.0 copy-done
  193.3 0.7 copy.26
Async XLA Ops:
  188.2 3.2 %copy-start.2 = (f32[192,128]{1,0:T(8,128)S(1)}, f32[192,128]{1,0:T(8,128)}, u32[]{:S(2)}) copy-start(f32[192,128]{1,0:T(8,128)} %get-tuple-element.61) | copy-start | bytes 294916
  188.2 3.8 %copy-start.3 = (f32[64,128]{1,0:T(8,128)S(1)}, f32[64,128]{1,0:T(8,128)}, u32[]{:S(2)}) copy-start(f32[64,128]{1,0:T(8,128)} %get-tuple-element.62) | copy-start | bytes 98308
  188.2 4.4 %copy-start.1 = (f32[128,256]{1,0:T(8,128)S(1)}, f32[128,256]{1,0:T(8,128)}, u32[]{:S(2)}) copy-start(f32[128,256]{1,0:T(8,128)} %get-tuple-element.80) | copy-start | bytes 393220
  188.2 5.1 %copy-start = (f32[64,512]{1,0:T(8,128)S(1)}, f32[64,512]{1,0:T(8,128)}, u32[]{:S(2)}) copy-start(f32[64,512]{1,0:T(8,128)} %get-tuple-element.64) | copy-start | bytes 393220

commit v6 on v5

--- a/solution.py
+++ b/solution.py
@@ -102,8 +102,8 @@
             for flip in (2, 4, 1):
                 self.push(turn, 0, 0, flip)
 
-    def cross(self):
-        for turn in range(self.depths):
+    def cross(self, first_turn=0, last_turn=None):
+        for turn in range(first_turn, self.depths if last_turn is None else last_turn):
             self.arrive(turn, 2)
             if turn < self.depths // 2:
                 self.push(turn, 2, 0, 4)
@@ -752,12 +752,14 @@
 
 def enter_kernel(
     depths, span,
-    x_ref, prefix_ref, bq_ref, bo_ref, bu_ref, bd_ref, one_ref, two_ref,
+    x_in, prefix_ref, bq_ref, bo_ref, bu_ref, bd_ref, one_ref, two_ref,
     wq_out, wo_out, wu_out, wd_out, gain_out, q_out, k_out, v_out, kp_out, vp_out, n_out, np_out, mixed_out, prob_out,
     sums_out, psum_out,
-    xp, wq, gains, q, k, v, kp, vp, n, n_prev, mixed, prob, slots,
-    send, recv, keep, gain_send, gain_recv, sum_send, sum_recv, tok_send, tok_recv, out_sem, prob_sem, wq_sem,
+    x_ref, xp, wq, gains, q, k, v, kp, vp, n, n_prev, mixed, prob, slots,
+    send, recv, keep, gain_send, gain_recv, sum_send, sum_recv, tok_send, tok_recv, out_sem, prob_sem, wq_sem, x_sem,
 ):
+    x_copy = pltpu.make_async_copy(x_in, x_ref, x_sem.at[0])
+    x_copy.start()
     rows, width = x_ref.shape
     tile = TILE_SEQS * span
     tiles = rows // tile
@@ -812,6 +814,7 @@
     greet(depths)
     gathers[0].begin()
     gain_share.begin()
+    x_copy.wait()
     send_tokens(0, 2)
     gain_share.forward()
     gain_share.complete()
@@ -830,9 +833,10 @@
         slots[spot, :, part * width : (part + 1) * width] = jnp.concatenate(means, axis=0).astype(BF16)
 
     pl.loop(0, chunks // 2)(normalize)
+    gathers[0].cross(0, 1)
     gathers[0].spread()
     pl.loop(chunks // 2, chunks)(normalize)
-    gathers[0].cross()
+    gathers[0].cross(1)
     keep_mean(2, n, 1.0)
     gathers[0].hand_over()
     send_tokens(2, 5)
@@ -867,8 +871,6 @@
         q[chunk_at(c), :] = (rows_q.astype(F32) * scale).astype(BF16)
         send_out(0, c)
 
-    sum_share.forward()
-
     def project_prev(c):
         @pl.when(spot > 0)
         def _():
@@ -883,11 +885,12 @@
         for a in (4, 5, 6):
             send_out(a, c)
 
-    pl.loop(0, 2)(project_prev)
+    project_prev(0)
+    sum_share.forward()
+    project_prev(1)
     sum_share.complete()
     ordered = dot(in_order(FLIPS, seqs), slots[...].reshape(FLIPS * seqs, 3 * width)).astype(BF16)
     sums_out[...] = ordered.reshape(sums_out.shape)
-
     @pl.loop(0, tiles)
     def _(i):
         @pl.when((lax.rem(i, CHUNK_TILES) == 0) & (i >= 2 * CHUNK_TILES))
@@ -954,7 +957,7 @@
     held = pltpu.VMEM((rows, width), BF16)
     return pl.pallas_call(
         functools.partial(enter_kernel, depths, span),
-        in_specs=[vmem, pl.BlockSpec(memory_space=pltpu.SMEM)] + [vmem] * 6,
+        in_specs=[far, pl.BlockSpec(memory_space=pltpu.SMEM)] + [vmem] * 6,
         out_specs=[far] * 4 + [vmem] + [far] * 9 + [vmem] * 2,
         out_shape=fulls
         + [jax.ShapeDtypeStruct((2, width), F32)]
@@ -966,6 +969,7 @@
         ],
         scratch_shapes=[
             held,
+            held,
             pltpu.VMEM(fulls[0].shape, BF16),
             pltpu.VMEM((FLIPS, 2, width), F32),
         ]
@@ -974,7 +978,7 @@
         + [
             sems((4, depths * FLIPS)), sems((4, depths * FLIPS)), sems((4,)),
             sems((FLIPS,)), sems((FLIPS,)), sems((FLIPS,)), sems((FLIPS,)),
-            sems((tiles,)), sems((tiles,)), sems((8, tiles)), sems((tiles,)), sems((1,)),
+            sems((tiles,)), sems((tiles,)), sems((8, tiles)), sems((tiles,)), sems((1,)), sems((1,)),
         ],
         compiler_params=pltpu.CompilerParams(collective_id=0, has_side_effects=True, vmem_limit_bytes=VMEM_MOST),
         name="enter",
@@ -982,25 +986,29 @@
 
 
 LEAVE_RELAYS = {
-    1: ((0, "cross"), (1, "cross")),
-    2: ((2, "cross"),),
+    0: ((0, "cross"),),
+    1: ((1, "cross"), (2, "cross")),
     3: ((0, "spread"), (1, "spread")),
-    4: ((2, "spread"),),
+    5: ((2, "spread"),),
     6: ((0, "climb"), (1, "climb")),
-    7: ((2, "climb"),),
 }
 
 
 def leave_kernel(
     depths, span,
     q_in, k_in, v_in, kp_in, vp_in, gm_in, n_in, np_in, prob_in, gr_in, x_in,
-    psum_ref, sums_ref, wq_ref, gout_ref, gup_ref, gdown_ref, gain_ref, ggain_ref,
+    psum_in, sums_in, wq_in, gout_in, gup_in, gdown_in, gain_ref, ggain_ref,
     ig_out, dqkv_out, dout_out, dup_out, ddown_out, dgain_out,
-    held, prob, kept, before, shared_rows, turned, turned_prev, turned_sum, one_sum, gp, gb, gr, x, ig, part, gs_send_buf, gs_slots, gain_slots, gain_deep,
+    psum_ref, sums_ref, wq_ref, gout_ref, gup_ref, gdown_ref, held, prob, kept, before, shared_rows, turned, turned_prev, turned_sum, one_sum, gp, gb, gr, x, ig, part, gs_send_buf, gs_slots, gain_slots, gain_deep,
     *rest,
 ):
     moves_refs, sems = rest[:16], rest[16:]
-    send, recv, gs_send, gs_recv, gain_send, gain_recv, deep_send, deep_recv, gb_send, gb_recv, in_sem, late_sem, ig_sem = sems
+    send, recv, gs_send, gs_recv, gain_send, gain_recv, deep_send, deep_recv, gb_send, gb_recv, in_sem, late_sem, ig_sem, whole_sem = sems
+    inputs = (gout_in, gup_in, gdown_in, psum_in, sums_in, wq_in)
+    landing = (gout_ref, gup_ref, gdown_ref, psum_ref, sums_ref, wq_ref)
+    wholes = [pltpu.make_async_copy(a, b, whole_sem.at[n]) for n, (a, b) in enumerate(zip(inputs, landing))]
+    for copy in wholes:
+        copy.start()
     rows, width = gp.shape
     tile = TILE_SEQS * span
     tiles = rows // tile
@@ -1046,8 +1054,11 @@
 
     greet(depths)
     turns = (*range(1, depths), 0)
-    for scatter in scatters[:3]:
+    for copy, scatter in zip(wholes, scatters[:3]):
+        copy.wait()
         scatter.begin(turns)
+    for copy in wholes[3:]:
+        copy.wait()
 
     @pl.loop(0, tiles)
     def _(i):
@@ -1172,6 +1183,7 @@
     after = {
         1: (functools.partial(scatters[3].cross, second), functools.partial(scatters[3].spread, first)),
         2: (share_deep, functools.partial(scatters[3].spread, second)),
+        0: (functools.partial(scatters[2].climb, turns),),
         4: (functools.partial(scatters[3].climb, first),),
         6: (functools.partial(scatters[3].climb, second),),
     }
@@ -1216,7 +1228,8 @@
     low = pltpu.VMEM((rows, width), BF16)
     high = pltpu.VMEM((rows, width), F32)
     shapes = [p.shape[2:] for p in (*partials, wq)]
-    scratch = [
+    scratch = [pltpu.VMEM(a.shape, BF16) for a in (psum, sums, wq, *partials)]
+    scratch += [
         pltpu.VMEM((2, 8, tile, width), BF16),
         pltpu.VMEM((2, TILE_SEQS, HEADS // 2, 2 * span, 2 * span), BF16),
         pltpu.VMEM((rows, 3 * width), BF16),
@@ -1237,12 +1250,12 @@
         scratch += scatter_scratch(shape, depths)
     scratch += [
         sems((4, 8 * depths)), sems((4, 8 * depths)), sems((FLIPS,)), sems((FLIPS,)), sems((FLIPS,)), sems((FLIPS,)),
-        sems((depths,)), sems((depths,)), sems((tiles,)), sems((tiles,)), sems((2, 9)), sems((2,)), sems((tiles,)),
+        sems((depths,)), sems((depths,)), sems((tiles,)), sems((tiles,)), sems((2, 9)), sems((2,)), sems((tiles,)), sems((6,)),
     ]
     outs = [jax.ShapeDtypeStruct(shape, F32) for shape in (shapes[3], *shapes[:3])]
     return pl.pallas_call(
         functools.partial(leave_kernel, depths, span),
-        in_specs=[far] * 11 + [vmem] * 8,
+        in_specs=[far] * 17 + [vmem] * 2,
         out_specs=[far] + [vmem] * 5,
         out_shape=[jax.ShapeDtypeStruct((rows, width), BF16), *outs, jax.ShapeDtypeStruct((2, width // FLIPS), F32)],
         scratch_shapes=scratch,

time: 194 us -> 192 us (0.990)
  no operation moved by 1% of the time
where the time goes in v6:
time: 192 us
  Pallas kernels  185 us (96%)
  local copies, waits for them, and re-layouts  6.94 us (4%)
    pallas_call x1, Pallas kernels, leave(): pl.pallas_call(functools.partial(leave_kernel, depths, span), in_specs=[f...  73.2 us
    pallas_call x1, Pallas kernels, enter(): pl.pallas_call(functools.partial(enter_kernel, depths, span), in_specs=[f...  70.2 us
    pallas_call x1, Pallas kernels, feed(): pl.pallas_call(feed_kernel, grid=(rows // tile,), in_specs=[row_spec(tile...  41.1 us
    unnamed x13, local copies, waits for them, and re-layouts  5.72 us

profile of v6, /device:TPU:0, one launch (start us, length us, event | category | flops | bytes accessed | tf_op | source)
XLA Modules:
  0.0 192.2 jit_solution(12519217068864028749)
XLA Ops:
  0.6 70.2 %enter.1 = (bf16[4,8,192,128]{3,2,1,0:T(8,128)(2,1)}, bf16[4,8,64,128]{3,2,1,0:T(8,128)(2,1)}, bf16[4,8,128,256]{3,2,1,0:T(8,128)(2,1)}, bf16[4,8,64,512]{3,2,1,...) custom-call(bf16[2048,512]{1,0:T(8,128)(2,1)} %bitcast.14, ...), custom_call_target="tpu_custom_call" | custom-call | tf_op jit(solution)/shard_map/enter/pallas_call | solution.py:958
  70.8 41.1 %feed.1 = (bf16[2048,512]{1,0:T(8,128)(2,1)}, bf16[2048,512]{1,0:T(8,128)(2,1)}, f32[2048,512]{1,0:T(8,128)}, bf16[4,8,64,128]{3,2,1,0:T(8,128)(2,1)}, bf16[4,8,...) custom-call(bf16[2048,512]{1,0:T(8,128)(2,1)} %bitcast.15, ...), custom_call_target="tpu_custom_call" | custom-call | tf_op jit(solution)/shard_map/feed/pallas_call | solution.py:528
  112.0 73.2 %leave.1 = (bf16[2048,512]{1,0:T(8,128)(2,1)}, f32[192,128]{1,0:T(8,128)}, f32[64,128]{1,0:T(8,128)}, f32[128,256]{1,0:T(8,128)}, f32[64,512]{1,0:T(8,128)}, /*index=5*/f32[2,64]{1,0:T(2,128)}) custom-call(bf16[2048,512]{1,0:T(8,128)(2,1)} %get-tuple-element.43.q_in, bf16[2048,512]{1,0:T(8,128)(2,1)} %get-tuple-element.44.k_in, ...), custom_call_target="tpu_custom_call" | custom-call | tf_op jit(solution)/shard_map/leave/pallas_call | solution.py:1256
  185.2 1.2 slice_bitcast_fusion
  186.4 0.0 copy-start.2
  186.4 0.0 copy-start.3
  186.4 0.0 copy-start.1
  186.4 0.0 copy-start
  186.4 3.1 %copy.22 = bf16[2,8,128,512]{3,2,1,0:T(8,128)(2,1)} copy(bf16[2,8,128,512]{3,2,1,0:T(8,128)(2,1)} %bitcast.18) | data formatting | bytes 4194304
  189.6 0.0 copy-done.2
  189.6 0.6 copy.23
  190.2 0.0 copy-done.3
  190.2 0.6 copy.24
  190.8 0.0 copy-done.1
  190.8 0.7 copy.25
  191.5 0.0 copy-done
  191.5 0.7 copy.26
Async XLA Ops:
  186.4 3.2 %copy-start.2 = (f32[192,128]{1,0:T(8,128)S(1)}, f32[192,128]{1,0:T(8,128)}, u32[]{:S(2)}) copy-start(f32[192,128]{1,0:T(8,128)} %get-tuple-element.61) | copy-start | bytes 294916
  186.4 3.8 %copy-start.3 = (f32[64,128]{1,0:T(8,128)S(1)}, f32[64,128]{1,0:T(8,128)}, u32[]{:S(2)}) copy-start(f32[64,128]{1,0:T(8,128)} %get-tuple-element.62) | copy-start | bytes 98308
  186.4 4.4 %copy-start.1 = (f32[128,256]{1,0:T(8,128)S(1)}, f32[128,256]{1,0:T(8,128)}, u32[]{:S(2)}) copy-start(f32[128,256]{1,0:T(8,128)} %get-tuple-element.80) | copy-start | bytes 393220
  186.4 5.1 %copy-start = (f32[64,512]{1,0:T(8,128)S(1)}, f32[64,512]{1,0:T(8,128)}, u32[]{:S(2)}) copy-start(f32[64,512]{1,0:T(8,128)} %get-tuple-element.64) | copy-start | bytes 393220

commit v7 on v6

--- a/solution.py
+++ b/solution.py
@@ -1264,6 +1264,45 @@
     )(*arrays, psum, sums, wq, *partials, gains, ggain)
 
 
+FINISH_PIECES = 8
+
+
+def finish_kernel(ig_in, *refs):
+    turned, (gains, ig_out), flat = refs[:4], refs[4:6], refs[6:10]
+    one_out, two_out, held, load_sem, store_sem = refs[10:]
+    rows = ig_in.shape[0] // FINISH_PIECES
+    pieces = [pl.ds(i * rows, rows) for i in range(FINISH_PIECES)]
+    loads = [pltpu.make_async_copy(ig_in.at[p], held.at[p], load_sem.at[i]) for i, p in enumerate(pieces)]
+    stores = [pltpu.make_async_copy(held.at[p], ig_out.at[p], store_sem.at[i]) for i, p in enumerate(pieces)]
+    for copy in loads:
+        copy.start()
+    for given, out in zip(turned, flat):
+        out[...] = given[...] if given.shape == out.shape else given[...].T
+    one_out[...] = gains[0:1, :].reshape(one_out.shape)
+    two_out[...] = gains[1:2, :].reshape(two_out.shape)
+    for load, store in zip(loads, stores):
+        load.wait()
+        store.start()
+    for copy in stores:
+        copy.wait()
+
+
+def finish(ig, grads, dgain, shapes):
+    vmem = pl.BlockSpec(memory_space=pltpu.VMEM)
+    far = pl.BlockSpec(memory_space=pl.ANY)
+    outs = [jax.ShapeDtypeStruct(shape, F32) for shape in (*shapes, dgain.shape[1:], dgain.shape[1:])]
+    sems = pltpu.SemaphoreType.DMA((FINISH_PIECES,))
+    return pl.pallas_call(
+        finish_kernel,
+        in_specs=[far] + [vmem] * 5,
+        out_specs=[far] + [vmem] * 6,
+        out_shape=[jax.ShapeDtypeStruct(ig.shape, ig.dtype), *outs],
+        scratch_shapes=[pltpu.VMEM(ig.shape, ig.dtype), sems, sems],
+        compiler_params=params(),
+        name="finish",
+    )(ig, *grads, dgain)
+
+
 def direct_shards(tokens, prefix, blocks, gain_one, gain_two, cotangent):
     span, width = tokens.shape[2], tokens.shape[3]
     depths = lax.axis_size("dp")
@@ -1275,16 +1314,9 @@
     out, gm, gr, gout, gup, gdown, ggain = feed(x, mixed, grad, wo, wu, wd, gains, 2 * TILE_SEQS * span)
     arrays = (q, k, v, kp, vp, gm, n, n_prev, prob, gr, x)
     ig, dqkv, dout, dup, ddown, dgain = leave(arrays, psum, sums, wq, (gout, gup, gdown), gains, ggain, span, depths)
-    return (
-        out.reshape(tokens.shape),
-        ig.reshape(tokens.shape),
-        dqkv.T,
-        dout.T,
-        dup,
-        ddown.T,
-        dgain[0],
-        dgain[1],
-    )
+    shapes = [blocks[0].shape[::-1], blocks[1].shape[::-1], blocks[2].shape, blocks[3].shape[::-1]]
+    ig, *rest = finish(ig, (dqkv, dout, dup, ddown), dgain, shapes)
+    return out.reshape(tokens.shape), ig.reshape(tokens.shape), *rest
 
 
 def fetch(block, rows_along):

time: 192 us -> 195 us (1.016)
  Pallas kernels: 185 us -> 189 us
  local copies, waits for them, and re-layouts: 6.94 us -> 4.9 us
    pallas_call x0 -> x1, Pallas kernels: none -> 4.24 us  [finish(): pl.pallas_call(finish_kernel, in_specs=[far] + [vmem] * 5, out_specs=[far...]
    unnamed x13 -> x3, local copies, waits for them, and re-layouts: 5.72 us -> 4.9 us
where the time goes in v7:
time: 195 us; the launch traced here: 194 us
  Pallas kernels  189 us (97%)
  local copies, waits for them, and re-layouts  4.9 us (3%)
    pallas_call x1, Pallas kernels, leave(): pl.pallas_call(functools.partial(leave_kernel, depths, span), in_specs=[f...  73.2 us
    pallas_call x1, Pallas kernels, enter(): pl.pallas_call(functools.partial(enter_kernel, depths, span), in_specs=[f...  70.2 us
    pallas_call x1, Pallas kernels, feed(): pl.pallas_call(feed_kernel, grid=(rows // tile,), in_specs=[row_spec(tile...  41.1 us
    unnamed x3, local copies, waits for them, and re-layouts  4.9 us
    pallas_call x1, Pallas kernels, finish(): pl.pallas_call(finish_kernel, in_specs=[far] + [vmem] * 5, out_specs=[far...  4.24 us

profile of v7, /device:TPU:0, one launch (start us, length us, event | category | flops | bytes accessed | tf_op | source)
XLA Modules:
  0.0 194.4 jit_solution(8286842863108897292)
XLA Ops:
  0.6 70.2 %enter.1 = (bf16[4,8,192,128]{3,2,1,0:T(8,128)(2,1)}, bf16[4,8,64,128]{3,2,1,0:T(8,128)(2,1)}, bf16[4,8,128,256]{3,2,1,0:T(8,128)(2,1)}, bf16[4,8,64,512]{3,2,1,...) custom-call(bf16[2048,512]{1,0:T(8,128)(2,1)} %bitcast.7, ...), custom_call_target="tpu_custom_call" | custom-call | tf_op jit(solution)/shard_map/enter/pallas_call | solution.py:958
  70.8 41.1 %feed.1 = (bf16[2048,512]{1,0:T(8,128)(2,1)}, bf16[2048,512]{1,0:T(8,128)(2,1)}, f32[2048,512]{1,0:T(8,128)}, bf16[4,8,64,128]{3,2,1,0:T(8,128)(2,1)}, bf16[4,8,...) custom-call(bf16[2048,512]{1,0:T(8,128)(2,1)} %bitcast.8, ...), custom_call_target="tpu_custom_call" | custom-call | tf_op jit(solution)/shard_map/feed/pallas_call | solution.py:528
  112.0 73.2 %leave.1 = (bf16[2048,512]{1,0:T(8,128)(2,1)}, f32[192,128]{1,0:T(8,128)}, f32[64,128]{1,0:T(8,128)}, f32[128,256]{1,0:T(8,128)}, f32[64,512]{1,0:T(8,128)}, /*index=5*/f32[2,64]{1,0:T(2,128)}) custom-call(bf16[2048,512]{1,0:T(8,128)(2,1)} %get-tuple-element.50.q_in, bf16[2048,512]{1,0:T(8,128)(2,1)} %get-tuple-element.51.k_in, ...), custom_call_target="tpu_custom_call" | custom-call | tf_op jit(solution)/shard_map/leave/pallas_call | solution.py:1256
  185.2 4.2 %finish.1 = (bf16[2048,512]{1,0:T(8,128)(2,1)}, f32[128,192]{1,0:T(8,128)}, f32[128,64]{1,0:T(8,128)}, f32[128,256]{1,0:T(8,128)}, f32[512,64]{1,0:T(8,128)}, /*index=5*/f32[64]{0:T(128)}, f32[64]{0:T(128)}) custom-call(bf16[2048,512]{1,0:T(8,128)(2,1)} %get-tuple-element.67.ig_in, f32[192,128]{1,0:T(8,128)} %get-tuple-element.68.refs_0_, ...), custom_call_target="tpu_custom_call" | custom-call | tf_op jit(solution)/shard_map/finish/pallas_call | solution.py:1295
  189.5 1.5 copy.18
  191.0 1.6 copy.17
  192.6 1.7 copy.19

commit v8 on v7

--- a/solution.py
+++ b/solution.py
@@ -1277,7 +1277,7 @@
     for copy in loads:
         copy.start()
     for given, out in zip(turned, flat):
-        out[...] = given[...] if given.shape == out.shape else given[...].T
+        out[...] = given[...]
     one_out[...] = gains[0:1, :].reshape(one_out.shape)
     two_out[...] = gains[1:2, :].reshape(two_out.shape)
     for load, store in zip(loads, stores):
@@ -1314,9 +1314,8 @@
     out, gm, gr, gout, gup, gdown, ggain = feed(x, mixed, grad, wo, wu, wd, gains, 2 * TILE_SEQS * span)
     arrays = (q, k, v, kp, vp, gm, n, n_prev, prob, gr, x)
     ig, dqkv, dout, dup, ddown, dgain = leave(arrays, psum, sums, wq, (gout, gup, gdown), gains, ggain, span, depths)
-    shapes = [blocks[0].shape[::-1], blocks[1].shape[::-1], blocks[2].shape, blocks[3].shape[::-1]]
-    ig, *rest = finish(ig, (dqkv, dout, dup, ddown), dgain, shapes)
-    return out.reshape(tokens.shape), ig.reshape(tokens.shape), *rest
+    ig, dqkv, dout, dup, ddown, one, two = finish(ig, (dqkv, dout, dup, ddown), dgain, [b.shape for b in blocks])
+    return out.reshape(tokens.shape), ig.reshape(tokens.shape), dqkv.T, dout.T, dup, ddown.T, one, two
 
 
 def fetch(block, rows_along):

time: 195 us -> 190 us (0.974)
  local copies, waits for them, and re-layouts: 4.9 us -> 0 us
    unnamed x3 -> x0, local copies, waits for them, and re-layouts: 4.9 us -> none
where the time goes in v8:
time: 190 us
  Pallas kernels  189 us (99%)
    pallas_call x1, Pallas kernels, leave(): pl.pallas_call(functools.partial(leave_kernel, depths, span), in_specs=[f...  73.2 us
    pallas_call x1, Pallas kernels, enter(): pl.pallas_call(functools.partial(enter_kernel, depths, span), in_specs=[f...  70.2 us
    pallas_call x1, Pallas kernels, feed(): pl.pallas_call(feed_kernel, grid=(rows // tile,), in_specs=[row_spec(tile...  41.1 us
    pallas_call x1, Pallas kernels, finish(): pl.pallas_call(finish_kernel, in_specs=[far] + [vmem] * 5, out_specs=[far...  4.18 us

profile of v8, /device:TPU:0, one launch (start us, length us, event | category | flops | bytes accessed | tf_op | source)
XLA Modules:
  0.0 189.6 jit_solution(17313827840695070672)
XLA Ops:
  0.6 70.2 %enter.1 = (bf16[4,8,192,128]{3,2,1,0:T(8,128)(2,1)}, bf16[4,8,64,128]{3,2,1,0:T(8,128)(2,1)}, bf16[4,8,128,256]{3,2,1,0:T(8,128)(2,1)}, bf16[4,8,64,512]{3,2,1,...) custom-call(bf16[2048,512]{1,0:T(8,128)(2,1)} %bitcast.10, ...), custom_call_target="tpu_custom_call" | custom-call | tf_op jit(solution)/shard_map/enter/pallas_call | solution.py:958
  70.8 41.1 %feed.1 = (bf16[2048,512]{1,0:T(8,128)(2,1)}, bf16[2048,512]{1,0:T(8,128)(2,1)}, f32[2048,512]{1,0:T(8,128)}, bf16[4,8,64,128]{3,2,1,0:T(8,128)(2,1)}, bf16[4,8,...) custom-call(bf16[2048,512]{1,0:T(8,128)(2,1)} %bitcast.11, ...), custom_call_target="tpu_custom_call" | custom-call | tf_op jit(solution)/shard_map/feed/pallas_call | solution.py:528
  112.0 73.2 %leave.1 = (bf16[2048,512]{1,0:T(8,128)(2,1)}, f32[192,128]{1,0:T(8,128)}, f32[64,128]{1,0:T(8,128)}, f32[128,256]{1,0:T(8,128)}, f32[64,512]{1,0:T(8,128)}, /*index=5*/f32[2,64]{1,0:T(2,128)}) custom-call(bf16[2048,512]{1,0:T(8,128)(2,1)} %get-tuple-element.50.q_in, bf16[2048,512]{1,0:T(8,128)(2,1)} %get-tuple-element.51.k_in, ...), custom_call_target="tpu_custom_call" | custom-call | tf_op jit(solution)/shard_map/leave/pallas_call | solution.py:1256
  185.2 4.2 %finish.1 = (bf16[2048,512]{1,0:T(8,128)(2,1)}, f32[192,128]{1,0:T(8,128)}, f32[64,128]{1,0:T(8,128)}, f32[128,256]{1,0:T(8,128)}, f32[64,512]{1,0:T(8,128)}, /*index=5*/f32[64]{0:T(128)}, f32[64]{0:T(128)}) custom-call(bf16[2048,512]{1,0:T(8,128)(2,1)} %get-tuple-element.67.ig_in, f32[192,128]{1,0:T(8,128)} %get-tuple-element.68.refs_0_, ...), custom_call_target="tpu_custom_call" | custom-call | tf_op jit(solution)/shard_map/finish/pallas_call | solution.py:1295
